TPU v7x, 256 devices: a whole 4x4x8 slice. The times are simulated.
256 devices in a mesh: chan: 16 (over y_lo, x, core), space: 16 (over y_hi, z).
Axes of the slice: x: 4, y: 4 (y_hi: 2, y_lo: 2; y = y_hi * 2 + y_lo), z: 8, core: 2. Of those that a mesh axis runs over, the one named last changes fastest.
Arguments:
- features: bfloat16 [256, 2, 128, 64], P('chan', None, 'space'), may hold values from -6 to 6
- weights: bfloat16 [4, 4, 4, 256, 128], P(None, None, None, None, 'chan'), may hold values from -0.1875 to 0.1875
- cotangent: bfloat16 [128, 4, 256, 128], P('chan', None, 'space'), may hold values from -6 to 6
Outputs:
- decoded: bfloat16 [128, 4, 256, 128], P('chan', None, 'space')
- input_grad: bfloat16 [256, 2, 128, 64], P('chan', None, 'space')
All inputs are finite; a program needn't handle non-finite values.
Results may differ from a plain program's by a relative error of at most 0.0012.
Values may be sent and summed in bfloat16 or wider, within the bound.
No kernel may reach another device: no remote copies, remote signals or barrier semaphores. Data moves between devices by JAX's collectives and lax.ppermute only.
A program may use at most 64 MiB of HBM per device.

v0:
```python
import jax
import jax.numpy as jnp
from jax import lax
from jax.sharding import PartitionSpec as P


def with_halo(x, sides, width):
    for axis, dim in sides:
        devices, length = (lax.axis_size(axis), x.shape[dim])
        up = [(i, (i + 1) % devices) for i in range(devices - 1)]
        down = [(j, i) for i, j in up]
        last = lax.slice_in_dim(x, length - width, length, axis=dim)
        initial = lax.slice_in_dim(x, 0, width, axis=dim)
        before = lax.ppermute(last, axis, up)
        after = lax.ppermute(initial, axis, down)
        x = jnp.concatenate([before, x, after], axis=dim)
    return x


def sent_to_all(x, axis):
    devices = lax.axis_size(axis)
    return lax.all_to_all(jnp.broadcast_to(x[None], (devices, *x.shape)), axis, 0, 0, tiled=True)


def laid_out(pieces, dim):
    shape = list(pieces.shape[1:])
    shape[dim] *= pieces.shape[0]
    return jnp.moveaxis(pieces, 0, dim).reshape(shape)


def collect(x, axis, dim):
    pieces = sent_to_all(x, axis)
    return laid_out(pieces, dim)


def split_up(x, dim, devices):
    before, after = (x.shape[:dim], x.shape[dim + 1 :])
    return jnp.moveaxis(x.reshape(*before, devices, -1, *after), dim, 0)


def sum_at_owner(x, axis, dim):
    devices = lax.axis_size(axis)
    pieces = lax.all_to_all(split_up(x, dim, devices), axis, 0, 0, tiled=True)
    return jnp.sum(pieces, axis=0)


def transposed_part(feature_block, kernel_block, depth_pad):
    return lax.conv_general_dilated(
        feature_block[None],
        kernel_block,
        (1, 1, 1),
        ((2, 2), (0, 0), (depth_pad, depth_pad)),
        lhs_dilation=(2, 2, 2),
        dimension_numbers=("NCDHW", "DHWIO", "NCDHW"),
        preferred_element_type=jnp.float32,
    )


def strided_part(grad_block, kernel_block, depth_pad):
    return lax.conv_general_dilated(
        grad_block[None],
        kernel_block,
        (2, 2, 2),
        ((1, 1), (0, 0), (depth_pad, depth_pad)),
        dimension_numbers=("NCDHW", "DHWOI", "NCDHW"),
        preferred_element_type=jnp.float32,
    )[0]


def local(features, weights, cotangent):
    kernel_flip = jnp.flip(weights, (0, 1, 2))
    padded_in = with_halo(features, (("space", 2),), 1)
    initial = jnp.zeros(
        (1, weights.shape[4], 2 * features.shape[1], 2 * features.shape[2], 2 * features.shape[3]),
        jnp.float32,
    )
    kernel_block = kernel_flip
    summed = initial + transposed_part(collect(padded_in, "chan", 0), kernel_block, 2)
    decoded = summed[0].astype(jnp.bfloat16)
    padded_grad = with_halo(cotangent, (("space", 2),), 1)
    kernel_block = weights
    grad_sum = sum_at_owner(strided_part(padded_grad, kernel_block, 1), "chan", 0)
    return (decoded, grad_sum.astype(jnp.bfloat16))


def solution(mesh):
    return jax.shard_map(
        local,
        mesh=mesh,
        in_specs=(
            P("chan", None, "space", None),
            P(None, None, None, None, "chan"),
            P("chan", None, "space", None),
        ),
        out_specs=(P("chan", None, "space", None), P("chan", None, "space", None)),
        check_vma=False,
    )
```

profile of v0, /device:TPU:25, one launch (start us, length us, event | category | flops | bytes accessed | tf_op | source)
XLA Modules:
  0.0 82.6 jit_solution(2283818198929955852)
XLA Ops:
  0.6 0.9 %fusion.28 = (bf16[16,2,1,64]{3,2,1,0:T(2,128)(2,1)S(1)}, bf16[16,2,1,64]{3,2,1,0:T(2,128)(2,1)S(1)}) fusion(bf16[16,2,8,64]{3,2,1,0:T(8,128)(2,1)} %param.3), kind=kLoop, calls=%fused_computation.31 | loop fusion | bytes 16384 | tf_op jit(solution)/shard_map/slice | solution.py:12
  1.6 3.5 %collective-permute-start = (bf16[16,2,1,64]{3,2,1,0:T(2,128)(2,1)S(1)}, bf16[16,2,1,64]{3,2,1,0:T(2,128)(2,1)S(1)}, u32[]{:S(2)}, u32[]{:S(2)}) collective-permute-start(bf16[16,2,1,64]{3,2,1,0:T(2,128)(2,1)S(1)} %get-tuple-element.14), channel_id=1, source_target_pairs={{0,1},{1,2},{2,3},{3,4},{4,5},{5,6},{6,7},{7,8},{8,9},{9,10},{10,1... | collective-permute-start | bytes 12296 | tf_op jit(solution)/shard_map/ppermute | solution.py:14
  5.1 6.5 %collective-permute-start.1 = (bf16[16,2,1,64]{3,2,1,0:T(2,128)(2,1)S(1)}, bf16[16,2,1,64]{3,2,1,0:T(2,128)(2,1)S(1)}, u32[]{:S(2)}, u32[]{:S(2)}) collective-permute-start(bf16[16,2,1,64]{3,2,1,0:T(2,128)(2,1)S(1)} %get-tuple-element.15), channel_id=1, source_target_pairs={{1,0},{2,1},{3,2},{4,3},{5,4},{6,5},{7,6},{8,7},{9,8},{10,9},{11,1... | collective-permute-start | bytes 12296 | tf_op jit(solution)/shard_map/ppermute | solution.py:15
  11.7 0.9 %fusion.27 = (bf16[8,4,1,128]{3,2,1,0:T(2,128)(2,1)S(1)}, bf16[8,4,1,128]{3,2,1,0:T(2,128)(2,1)S(1)}) fusion(bf16[8,4,16,128]{3,2,1,0:T(8,128)(2,1)} %param.5), kind=kLoop, calls=%fused_computation.30 | loop fusion | bytes 32768 | tf_op jit(solution)/shard_map/slice | solution.py:12
  12.6 1.9 %collective-permute-start.2 = (bf16[8,4,1,128]{3,2,1,0:T(2,128)(2,1)S(1)}, bf16[8,4,1,128]{3,2,1,0:T(2,128)(2,1)S(1)}, u32[]{:S(2)}, u32[]{:S(2)}) collective-permute-start(bf16[8,4,1,128]{3,2,1,0:T(2,128)(2,1)S(1)} %get-tuple-element.12), channel_id=1, source_target_pairs={{0,1},{1,2},{2,3},{3,4},{4,5},{5,6},{6,7},{7,8},{8,9},{9,10},{10,1... | collective-permute-start | bytes 24584 | tf_op jit(solution)/shard_map/ppermute | solution.py:14
  14.5 7.0 %collective-permute-start.3 = (bf16[8,4,1,128]{3,2,1,0:T(2,128)(2,1)S(1)}, bf16[8,4,1,128]{3,2,1,0:T(2,128)(2,1)S(1)}, u32[]{:S(2)}, u32[]{:S(2)}) collective-permute-start(bf16[8,4,1,128]{3,2,1,0:T(2,128)(2,1)S(1)} %get-tuple-element.13), channel_id=1, source_target_pairs={{1,0},{2,1},{3,2},{4,3},{5,4},{6,5},{7,6},{8,7},{9,8},{10,9},{11,1... | collective-permute-start | bytes 24584 | tf_op jit(solution)/shard_map/ppermute | solution.py:15
  21.5 0.9 %pad_maximum_fusion = bf16[16,2,10,64]{3,2,1,0:T(8,128)(2,1)S(1)} fusion(bf16[16,2,1,64]{3,2,1,0:T(2,128)(2,1)S(1)} %collective-permute-done.1, bf16[16,2,8,64]{3,2,1,0:T(8,128)(2,1)} %param.3, bf16[16,2,1,64]{3,2,1,0:T(2,128)(2,1)S(1)} %collective-permute-done), kind=kLoop, calls=%fused_computation.23 | loop fusion | flops 122880 | bytes 81920 | tf_op jit(solution)/shard_map/concatenate | solution.py:16
  22.8 1.7 %reshape.31 = bf16[16,2,10240]{2,1,0:T(2,128)(2,1)} reshape(bf16[16,2,10,16,64]{4,3,2,1,0:T(8,128)(2,1)S(1)} %broadcast_bitcast_fusion) | data formatting | bytes 1310720
  24.5 6.9 %all-to-all-start = ((bf16[16,2,10240]{2,1,0:T(2,128)(2,1)}), bf16[16,2,10240]{2,1,0:T(2,128)(2,1)}, u32[]{:S(2)}, u32[]{:S(2)}) async-start(bf16[16,2,10240]{2,1,0:T(2,128)(2,1)} %reshape.31), calls=%async_computation | async-start | bytes 1310720 | tf_op jit(solution)/shard_map/all_to_all | solution.py:22
  31.7 0.9 %reshape.30 = bf16[8,4,18,1,8,18]{5,4,2,1,0,3:T(8,128)(2,1)S(1)} reshape(bf16[8,4,18,1,144]{4,2,1,0,3:T(8,128)(2,1)S(1)} %pad.2) | data formatting | bytes 331776 | tf_op jit(solution)/shard_map/conv_general_dilated | solution.py:60
  32.6 4.9 %copy.60 = bf16[8,4,18,1,8,18]{0,4,5,2,1,3:T(8,128)(2,1)} copy(bf16[8,4,18,1,8,18]{5,4,2,1,0,3:T(8,128)(2,1)S(1)} %reshape.30) | data formatting | bytes 331776 | tf_op jit(solution)/shard_map/conv_general_dilated | solution.py:60
  37.5 1.1 %slice.22 = bf16[8,4,18,1,7,3]{0,4,5,2,1,3:T(8,128)(2,1)S(1)} slice(bf16[8,4,18,1,8,18]{0,4,5,2,1,3:T(8,128)(2,1)} %copy.60), slice={[0:8], [0:4], [0:18], [0:1], [1:8], [0:3]} | slice | bytes 48384 | tf_op jit(solution)/shard_map/conv_general_dilated | solution.py:60
  38.6 4.3 %fusion.10 = f32[2,8,8,9,256]{4,2,3,1,0:T(8,128)S(1)} fusion(bf16[4,4,4,256,8]{3,4,2,1,0:T(8,128)(2,1)S(1)} %copy-done, bf16[8,4,18,1,7,3]{0,4,5,2,1,3:T(8,128)(2,1)S(1)} %slice.22, bf16[8,4,18,1,8,18]{0,4,5,2,1,3:T(8,128)(2,1)} %copy.60, pred[8,9]{0,1:T(8,128)(4,1)S(1)} %copy-done.3), kind=kOutput, calls=%fused_computation.12 | convolution fusion | flops 227367936 | bytes 1631944 | tf_op jit(solution)/shard_map/conv_general_dilated | solution.py:60
  43.4 1.5 %copy.62 = f32[1,256,2,8,64]{4,3,2,1,0:T(8,128)S(1)} copy(f32[1,256,2,8,64]{1,3,4,2,0:T(8,128)S(1)} %slice_bitcast_fusion) | data formatting | bytes 2097152 | tf_op jit(solution)/shard_map/conv_general_dilated | solution.py:60
  44.9 2.3 %reshape.33 = f32[16,1,16384]{2,1,0:T(1,128)} reshape(f32[16,16,2,8,64]{4,3,2,1,0:T(8,128)S(1)} %bitcast.31) | data formatting | bytes 2097152
  47.2 5.7 %all-to-all-start.1 = ((f32[16,1,16384]{2,1,0:T(1,128)}), f32[16,1,16384]{2,1,0:T(1,128)}, u32[]{:S(2)}, u32[]{:S(2)}) async-start(f32[16,1,16384]{2,1,0:T(1,128)} %reshape.33), calls=%async_computation.1 | async-start | bytes 2097152 | tf_op jit(solution)/shard_map/all_to_all | solution.py:43
  52.9 2.6 %reshape.32 = bf16[16,2,10,16,64]{4,3,2,1,0:T(8,128)(2,1)S(1)} reshape(bf16[16,2,10240]{2,1,0:T(2,128)(2,1)} %all-to-all-done) | data formatting | bytes 1310720
  55.9 1.3 %copy.66 = bf16[256,2,10,1,64]{0,1,4,2,3:T(2,128)(2,1)S(1)} copy(bf16[256,2,10,1,64]{4,0,2,1,3:T(8,128)(2,1)S(1)} %bitcast.33) | data formatting | bytes 1310720
  57.9 11.1 %fusion.15 = bf16[4,16,8,18,8]{4,2,3,1,0:T(8,128)(2,1)} fusion(bf16[4,4,4,256,8]{3,4,2,1,0:T(8,128)(2,1)S(1)} %copy-done, bf16[256,2,10,1,7,2]{0,4,5,2,1,3:T(8,128)(2,1)S(1)} %slice.20, bf16[256,2,10,1,8,9]{0,4,5,2,1,3:T(8,128)(2,1)S(1)} %copy.55), kind=kOutput, calls=%fused_computation.16 | convolution fusion | flops 229195776 | bytes 1290240 | tf_op jit(solution)/shard_map/conv_general_dilated | solution.py:48
  69.0 5.0 %copy.56 = bf16[4,16,8,18,8]{3,4,2,1,0:T(8,128)(2,1)S(1)} copy(bf16[4,16,8,18,8]{4,2,3,1,0:T(8,128)(2,1)} %fusion.15) | data formatting | bytes 294912 | tf_op jit(solution)/shard_map/conv_general_dilated | solution.py:48
  74.6 0.7 reshape.12
  76.6 4.4 %reduce = f32[16,16384]{1,0:T(8,128)S(1)} reduce(f32[16,1,16384]{2,1,0:T(1,128)} %all-to-all-done.1, f32[]{:T(128)} %broadcast.33), dimensions={1}, to_apply=%all_to_all.7.reduce_sub_computation | reduce | bytes 2097156 | tf_op jit(solution)/shard_map/all_to_all | solution.py:43
  81.0 0.8 %reshape.34 = f32[16,16,2,8,64]{4,3,2,1,0:T(8,128)S(1)} reshape(f32[16,16384]{1,0:T(8,128)S(1)} %reduce) | data formatting | bytes 2097152
  81.8 0.8 reduce_sum.9
  (29 shorter events, 3.9 us)
Async XLA Ops:
  0.6 38.0 %copy-start = (bf16[4,4,4,256,8]{3,4,2,1,0:T(8,128)(2,1)S(1)}, bf16[4,4,4,256,8]{3,4,2,1,0:T(8,128)(2,1)}, u32[]{:S(2)}) copy-start(bf16[4,4,4,256,8]{3,4,2,1,0:T(8,128)(2,1)} %param.4) | copy-start | bytes 786436
  1.6 19.9 %collective-permute-start = (bf16[16,2,1,64]{3,2,1,0:T(2,128)(2,1)S(1)}, bf16[16,2,1,64]{3,2,1,0:T(2,128)(2,1)S(1)}, u32[]{:S(2)}, u32[]{:S(2)}) collective-permute-start(bf16[16,2,1,64]{3,2,1,0:T(2,128)(2,1)S(1)} %get-tuple-element.14), channel_id=1, source_target_pairs={{0,1},{1,2},{2,3},{3,4},{4,5},{5,6},{6,7},{7,8},{8,9},{9,10},{10,1... | collective-permute-start | bytes 12296 | tf_op jit(solution)/shard_map/ppermute | solution.py:14
  5.1 16.4 %collective-permute-start.1 = (bf16[16,2,1,64]{3,2,1,0:T(2,128)(2,1)S(1)}, bf16[16,2,1,64]{3,2,1,0:T(2,128)(2,1)S(1)}, u32[]{:S(2)}, u32[]{:S(2)}) collective-permute-start(bf16[16,2,1,64]{3,2,1,0:T(2,128)(2,1)S(1)} %get-tuple-element.15), channel_id=1, source_target_pairs={{1,0},{2,1},{3,2},{4,3},{5,4},{6,5},{7,6},{8,7},{9,8},{10,9},{11,1... | collective-permute-start | bytes 12296 | tf_op jit(solution)/shard_map/ppermute | solution.py:15
  12.6 18.8 %collective-permute-start.2 = (bf16[8,4,1,128]{3,2,1,0:T(2,128)(2,1)S(1)}, bf16[8,4,1,128]{3,2,1,0:T(2,128)(2,1)S(1)}, u32[]{:S(2)}, u32[]{:S(2)}) collective-permute-start(bf16[8,4,1,128]{3,2,1,0:T(2,128)(2,1)S(1)} %get-tuple-element.12), channel_id=1, source_target_pairs={{0,1},{1,2},{2,3},{3,4},{4,5},{5,6},{6,7},{7,8},{8,9},{9,10},{10,1... | collective-permute-start | bytes 24584 | tf_op jit(solution)/shard_map/ppermute | solution.py:14
  14.5 16.8 %collective-permute-start.3 = (bf16[8,4,1,128]{3,2,1,0:T(2,128)(2,1)S(1)}, bf16[8,4,1,128]{3,2,1,0:T(2,128)(2,1)S(1)}, u32[]{:S(2)}, u32[]{:S(2)}) collective-permute-start(bf16[8,4,1,128]{3,2,1,0:T(2,128)(2,1)S(1)} %get-tuple-element.13), channel_id=1, source_target_pairs={{1,0},{2,1},{3,2},{4,3},{5,4},{6,5},{7,6},{8,7},{9,8},{10,9},{11,1... | collective-permute-start | bytes 24584 | tf_op jit(solution)/shard_map/ppermute | solution.py:15
  22.5 8.9 %copy-start.1 = (bf16[8,4,16,128]{3,2,1,0:T(8,128)(2,1)S(1)}, bf16[8,4,16,128]{3,2,1,0:T(8,128)(2,1)}, u32[]{:S(2)}) copy-start(bf16[8,4,16,128]{3,2,1,0:T(8,128)(2,1)} %param.5) | copy-start | bytes 393220
  24.5 22.7 %all-to-all-start = ((bf16[16,2,10240]{2,1,0:T(2,128)(2,1)}), bf16[16,2,10240]{2,1,0:T(2,128)(2,1)}, u32[]{:S(2)}, u32[]{:S(2)}) async-start(bf16[16,2,10240]{2,1,0:T(2,128)(2,1)} %reshape.31), calls=%async_computation | async-start | bytes 1310720 | tf_op jit(solution)/shard_map/all_to_all | solution.py:22
  32.6 6.0 %copy-start.3 = (pred[8,9]{0,1:T(8,128)(4,1)S(1)}, pred[8,9]{0,1:T(8,128)(4,1)}, u32[]{:S(2)}) copy-start(pred[8,9]{0,1:T(8,128)(4,1)} %constant.14) | copy-start | bytes 220
  47.2 28.9 %all-to-all-start.1 = ((f32[16,1,16384]{2,1,0:T(1,128)}), f32[16,1,16384]{2,1,0:T(1,128)}, u32[]{:S(2)}, u32[]{:S(2)}) async-start(f32[16,1,16384]{2,1,0:T(1,128)} %reshape.33), calls=%async_computation.1 | async-start | bytes 2097152 | tf_op jit(solution)/shard_map/all_to_all | solution.py:43
  69.0 5.1 %copy-start.2 = (pred[8,18]{1,0:T(8,128)(4,1)S(1)}, pred[8,18]{1,0:T(8,128)(4,1)}, u32[]{:S(2)}) copy-start(pred[8,18]{1,0:T(8,128)(4,1)} %constant.13) | copy-start | bytes 436
where the time goes:
time: 83.2 us; the launch traced here: 82.6 us
  starting transfers between devices  31.6 us (38%)
  local copies, waits for them, and re-layouts  28.1 us (34%)
  matrix products  15.4 us (19%)
  other arithmetic  6.54 us (8%)
  between operations  0.93 us (1%)
    ppermute x2, starting transfers between devices, with_halo(): after = lax.ppermute(initial, axis, down)  13.5 us
    conv_general_dilated x1, matrix products, transposed_part(): lax.conv_general_dilated(feature_block[None], kernel_block, (1, 1, 1), ((...  11.1 us
    unnamed x15, local copies, waits for them, and re-layouts  9.7 us
    conv_general_dilated x6, local copies, waits for them, and re-layouts, strided_part(): lax.conv_general_dilated(grad_block[None], kernel_block, (2, 2, 2), ((1,...  8.77 us
    all_to_all x1, starting transfers between devices, sent_to_all(): lax.all_to_all(jnp.broadcast_to(x[None], (devices, *x.shape)), axis, 0, 0...  6.9 us
    all_to_all x1, starting transfers between devices, sum_at_owner(): pieces = lax.all_to_all(split_up(x, dim, devices), axis, 0, 0, tiled=True)  5.72 us
    ppermute x2, starting transfers between devices, with_halo(): before = lax.ppermute(last, axis, up)  5.47 us
    conv_general_dilated x3, local copies, waits for them, and re-layouts, transposed_part(): lax.conv_general_dilated(feature_block[None], kernel_block, (1, 1, 1), ((...  5.18 us
  transfers between devices with their start and end apart: 6, of which 0 were waited for; matrix products, arithmetic and copies ran while one was open for 52% of the time, Pallas kernels for 0%

commit v1 on v0

v1 whole, which is shorter than its diff:
```python
import jax
import jax.numpy as jnp
from jax import lax
from jax.experimental import pallas as pl
from jax.experimental.pallas import tpu as pltpu
from jax.sharding import PartitionSpec as P

BF = jnp.bfloat16
F32 = jnp.float32


def call(body, outs, scratch, cost):
    return pl.pallas_call(
        body,
        out_shape=outs,
        scratch_shapes=scratch,
        cost_estimate=pl.CostEstimate(flops=cost[0], bytes_accessed=cost[1], transcendentals=0),
    )


def dot(a, b, dims=((1,), (0,))):
    return lax.dot_general(a, b, (dims, ((), ())), preferred_element_type=F32)


def core_index():
    return lax.rem(lax.axis_index("chan"), 2)


def pack_body(feat, cot, flat, turned, edge_a, edge_b, fs, cs):
    for ch in range(16):
        for u in range(2):
            fs[pl.ds(ch * 16 + u * 8, 8), :] = feat[ch, u].astype(F32)
    for o in range(8):
        for a in range(4):
            cs[pl.ds((o * 4 + a) * 16, 16), :] = cot[o, a].astype(F32)
    tiles = []
    for v in range(8):
        tile = jnp.concatenate([fs[pl.ds(v, 16, stride=16), :], fs[pl.ds(8 + v, 16, stride=16), :]], axis=1)
        tiles.append(tile)
        flat[:, v * 128 : (v + 1) * 128] = tile.astype(BF)
    firsts, lasts = [], []
    for a in range(4):
        for b in range(0, 16, 2):
            lo = cs[pl.ds(a * 16 + b, 8, stride=64), :]
            hi = cs[pl.ds(a * 16 + b + 1, 8, stride=64), :]
            turned[pl.ds((a * 16 + b) * 8, 16), :] = jnp.concatenate([lo, hi], axis=0).astype(BF)
            if b == 0:
                firsts.append(lo)
            if b == 14:
                lasts.append(hi)
    first = jnp.concatenate([tiles[0]] + firsts, axis=0)
    last = jnp.concatenate([tiles[7]] + lasts, axis=0)
    core = jnp.full(first.shape, core_index(), jnp.int32)
    edge_a[...] = jnp.where(core == 0, last, first).astype(BF)
    edge_b[...] = jnp.where(core == 0, first, last).astype(BF)


def pack(feat, cot):
    s = jax.ShapeDtypeStruct
    return call(
        pack_body,
        (s((16, 1024), BF), s((512, 128), BF), s((48, 128), BF), s((48, 128), BF)),
        [pltpu.VMEM((256, 64), F32), pltpu.VMEM((512, 128), F32)],
        (0, 400000),
    )(feat, cot)


def grad_body(w_own, w_other, c_own, c_other, h_own, h_other, out, rows, cols, wk):
    core = core_index()
    i = lax.broadcasted_iota(jnp.int32, (256, 512), 0)
    j = lax.broadcasted_iota(jnp.int32, (256, 512), 1)
    c = lax.rem(i, 128)
    want = 2 * lax.rem(j, 64) + lax.div(j, 128) - 1
    same = lax.div(i, 128) == lax.rem(lax.div(j, 64), 2)
    select = jnp.where((c == want) & same, 1.0, 0.0).astype(BF)
    zero = jnp.zeros((80, 128), BF)
    for k, (w_ref, c_ref, h_ref) in enumerate(((w_own, c_own, h_own), (w_other, c_other, h_other))):
        for a in range(4):
            @pl.when(core == 0)
            def _():
                rows[k, a, 0:8, :] = h_ref[16 + 8 * a : 24 + 8 * a, :].astype(F32)
                rows[k, a, 8:80, :] = c_ref[a * 128 : a * 128 + 72, :].astype(F32)

            @pl.when(core == 1)
            def _():
                rows[k, a, 0:72, :] = c_ref[a * 128 + 56 : a * 128 + 128, :].astype(F32)
                rows[k, a, 72:80, :] = h_ref[16 + 8 * a : 24 + 8 * a, :].astype(F32)
        plane = [rows[k, a].astype(BF) for a in range(4)]
        for p in range(4):
            low = plane[p - 1] if p > 0 else zero
            high = plane[p + 1] if p < 3 else zero
            cols[k, p] = dot(jnp.concatenate([low, high], axis=1), select).astype(BF)
            for r in range(4):
                taps = [w_ref[p, q, r].astype(F32) for q in range(4)]
                wk[pl.ds(((k * 4 + p) * 4 + r) * 32, 32), :] = jnp.concatenate(taps, axis=0).astype(BF)
    wt = wk[...].T
    for pair in range(2):
        halves = []
        for v in (2 * pair, 2 * pair + 1):
            parts = [
                cols[k, p, 16 * v : 16 * v + 32, r * 128 : (r + 1) * 128]
                for k in range(2)
                for p in range(4)
                for r in range(4)
            ]
            halves.append(jnp.concatenate(parts, axis=0))
        out[:, pair * 256 : (pair + 1) * 256] = dot(wt, jnp.concatenate(halves, axis=1))


def grad(w_own, w_other, c_own, c_other, h_own, h_other):
    return call(
        grad_body,
        jax.ShapeDtypeStruct((256, 512), F32),
        [pltpu.VMEM((2, 4, 80, 128), F32), pltpu.VMEM((2, 4, 80, 512), BF), pltpu.VMEM((1024, 256), BF)],
        (500000000, 1400000),
    )(w_own, w_other, c_own, c_other, h_own, h_other)


def total_body(parts, out, rows):
    for half in range(2):
        acc = parts[half]
        for chip in range(1, 8):
            acc = acc + parts[2 * chip + half]
        for k in range(4):
            v = 4 * half + k
            for u in range(2):
                rows[pl.ds(u * 8 + v, 16, stride=16), :] = acc[:, k * 128 + u * 64 : k * 128 + (u + 1) * 64]
    for ch in range(16):
        for u in range(2):
            out[ch, u] = rows[pl.ds(ch * 16 + u * 8, 8), :].astype(BF)


def total(parts):
    return call(
        total_body,
        jax.ShapeDtypeStruct((16, 2, 8, 64), BF),
        [pltpu.VMEM((256, 64), F32)],
        (200000, 600000),
    )(parts)


def up_body(weights, own, other, out, f, y, fine):
    core = core_index()
    mine = pl.multiple_of(core * 16, 16)
    theirs = pl.multiple_of(16 - core * 16, 16)
    side, far = core * 9, 9 - core * 9
    for chip in range(8):
        a = pl.ds(pl.multiple_of(chip * 32 + mine, 16), 16)
        b = pl.ds(pl.multiple_of(chip * 32 + theirs, 16), 16)
        for v in range(8):
            f[v + 1, a, :] = own[chip, :, v * 128 : (v + 1) * 128]
            f[v + 1, b, :] = other[chip, :, v * 128 : (v + 1) * 128]
        f[side, a, :] = own[chip, :, 1024:1152]
        f[side, b, :] = own[chip, :, 1152:1280]
        f[far, b, :] = other[chip, :, 1024:1152]
        f[far, a, :] = other[chip, :, 1152:1280]
    w = weights[...]
    for t in range(5):
        y[t] = dot(w, jnp.concatenate([f[2 * t], f[2 * t + 1]], axis=1))

    def tap(p, q, r, v):
        t = v + 1
        return y[t // 2, pl.ds(((p * 4 + q) * 4 + r) * 8, 8), (t % 2) * 128 : (t % 2 + 1) * 128]

    lane = lax.broadcasted_iota(jnp.int32, (8, 128), 1)
    first_half = lane < 64
    cell = lax.rem(lane, 64)
    ii = lax.broadcasted_iota(jnp.int32, (256, 256), 0)
    jj = lax.broadcasted_iota(jnp.int32, (256, 256), 1)
    spread = jnp.where(
        (lax.div(jj, 128) == lax.rem(lax.div(ii, 64), 2))
        & (lax.rem(jj, 128) == 2 * lax.rem(ii, 64) + lax.div(ii, 128)),
        1.0,
        0.0,
    ).astype(BF)
    for pb in range(2):
        blocks = {0: [], 1: []}
        for n in range(8):
            pairs = ((1, n), (3, n - 1)) if pb == 0 else ((2, n), (0, n + 1))
            got = {0: [], 1: []}
            for r in range(4):
                s = [sum(tap(p, q, r, v) for q, v in pairs) for p in range(4)]
                moved = pltpu.roll(jnp.where(first_half, s[3], s[0]), 64, 1)
                got[0].append(s[1] + jnp.where(first_half, 0.0, moved))
                got[1].append(s[2] + jnp.where(first_half, moved, 0.0))
            for pa in range(2):
                t0, t1, t2, t3 = got[pa]
                even = t1 + jnp.where(cell == 0, 0.0, pltpu.roll(t3, 1, 1))
                odd = t2 + jnp.where(cell == 63, 0.0, pltpu.roll(t0, 127, 1))
                blocks[pa].append(jnp.concatenate([even, odd], axis=1))
        for pa in range(2):
            rows = dot(jnp.concatenate(blocks[pa], axis=0).astype(BF), spread)
            for n in range(8):
                for m in range(2):
                    fine[pl.ds((2 * m + pa) * 16 + 2 * n + pb, 8, stride=64), :] = rows[
                        n * 8 : (n + 1) * 8, m * 128 : (m + 1) * 128
                    ]
    for o in range(8):
        for a in range(4):
            out[o, a] = fine[pl.ds((o * 4 + a) * 16, 16), :].astype(BF)


def upsample(weights, own, other):
    return call(
        up_body,
        jax.ShapeDtypeStruct((8, 4, 16, 128), BF),
        [pltpu.VMEM((10, 256, 128), BF), pltpu.VMEM((5, 512, 256), F32), pltpu.VMEM((512, 128), F32)],
        (400000000, 1100000),
    )(weights, own, other)


def local(features, weights, cotangent):
    tiles = lax.axis_size("space")
    chans = lax.axis_size("chan")
    at = lambda ch, sp: ch * tiles + sp
    swap = [(ch, ch ^ 1) for ch in range(chans)]
    cross_a, cross_b = [], []
    for ch in range(chans):
        for sp in range(tiles):
            if ch % 2 == 0:
                if sp + 1 < tiles:
                    cross_a.append((at(ch, sp), at(ch, sp + 1)))
                    cross_b.append((at(ch + 1, sp), at(ch, sp + 1)))
            elif sp > 0:
                cross_a.append((at(ch, sp), at(ch, sp - 1)))
                cross_b.append((at(ch - 1, sp), at(ch, sp - 1)))
    both = ("chan", "space")
    by_core = [[2 * chip + core for chip in range(chans // 2)] for core in range(2)]

    w_own = jnp.transpose(weights, (0, 1, 2, 4, 3))
    w_other = lax.ppermute(w_own, "chan", swap)
    flat, turned, edge_a, edge_b = pack(features, cotangent)
    turned_other = lax.ppermute(turned, "chan", swap)
    halo_a = lax.ppermute(edge_a, both, cross_a)
    halo_b = lax.ppermute(edge_b, both, cross_b)

    block = jnp.concatenate([flat, halo_a[:16], halo_b[:16]], axis=1)
    copies = jnp.broadcast_to(block[None], (8, 16, 1280))
    own = lax.all_to_all(copies, "chan", 0, 0, tiled=True, axis_index_groups=by_core)

    partial = grad(w_own, w_other, turned, turned_other, halo_a, halo_b)
    pieces = lax.all_to_all(partial.reshape(16, 16, 512), "chan", 0, 0, tiled=True)

    other = lax.ppermute(own, "chan", swap)
    decoded = upsample(w_own.reshape(512, 256), own, other)
    return decoded, total(pieces)


def solution(mesh):
    return jax.shard_map(
        local,
        mesh=mesh,
        in_specs=(
            P("chan", None, "space", None),
            P(None, None, None, None, "chan"),
            P("chan", None, "space", None),
        ),
        out_specs=(P("chan", None, "space", None), P("chan", None, "space", None)),
        check_vma=False,
    )
```

time: 83.2 us -> 47.9 us (0.58)
  the two profiles are of different devices: /device:TPU:25 before, /device:TPU:16 now
where the time goes in v1:
time: 47.9 us; the launch traced here: 47.4 us
  starting transfers between devices  19.1 us (40%)
  waiting for transfers between devices  13.6 us (28%)
  Pallas kernels  9.56 us (20%)
  local copies, waits for them, and re-layouts  3.62 us (8%)
  other arithmetic  0.77 us (2%)
  between operations  0.71 us (1%)
    ppermute x1, starting transfers between devices, local(): halo_b = lax.ppermute(edge_b, both, cross_b)  5.79 us
    all_to_all x1, waiting for transfers between devices, local(): lax.all_to_all(partial.reshape(16, 16, 512), 'chan', 0, 0, tiled=True)  5.4 us
    all_to_all x1, starting transfers between devices, local(): lax.all_to_all(copies, 'chan', 0, 0, tiled=True, axis_index_groups=by_core)  5.15 us
    ppermute x1, starting transfers between devices, local(): halo_a = lax.ppermute(edge_a, both, cross_a)  3.81 us
    all_to_all x1, starting transfers between devices, local(): lax.all_to_all(partial.reshape(16, 16, 512), 'chan', 0, 0, tiled=True)  3.57 us
    pallas_call x1, Pallas kernels, grad(): call(grad_body, jax.ShapeDtypeStruct((256, 512), F32), [pltpu.VMEM((2, 4,...  3.04 us
    pallas_call x1, Pallas kernels, upsample(): call(up_body, jax.ShapeDtypeStruct((8, 4, 16, 128), BF), [pltpu.VMEM((10,...  2.94 us
    ppermute x1, waiting for transfers between devices, local(): halo_b = lax.ppermute(edge_b, both, cross_b)  2.91 us
  transfers between devices with their start and end apart: 7, of which 5 were waited for; matrix products, arithmetic and copies ran while one was open for 3% of the time, Pallas kernels for 13%

profile of v1, /device:TPU:16, one launch (start us, length us, event | category | flops | bytes accessed | tf_op | source)
XLA Modules:
  0.0 47.4 jit_solution(17764381028021391986)
XLA Ops:
  0.6 1.8 %shard_map.50 = (bf16[16,1024]{1,0:T(8,128)(2,1)}, bf16[512,128]{1,0:T(8,128)(2,1)}, bf16[48,128]{1,0:T(8,128)(2,1)}, bf16[48,128]{1,0:T(8,128)(2,1)}) custom-call(bf16[16,2,8,64]{3,2,1,0:T(8,128)(2,1)} %feat.1, bf16[8,4,16,128]{3,2,1,0:T(8,128)(2,1)} %cot.1), custom_call_target="tpu_custom_call" | custom-call | bytes 400000 | tf_op jit(solution)/shard_map/pallas_call | solution.py:60
  2.4 3.8 %collective-permute-start = (bf16[48,128]{1,0:T(8,128)(2,1)}, bf16[48,128]{1,0:T(8,128)(2,1)S(1)}, u32[]{:S(2)}, u32[]{:S(2)}) collective-permute-start(bf16[48,128]{1,0:T(8,128)(2,1)} %get-tuple-element.7), channel_id=1, source_target_pairs={{0,1},{1,2},{2,3},{3,4},{4,5},{5,6},{6,7},{7,8},{8,9},{9,10},{10,1... | collective-permute-start | bytes 36872 | tf_op jit(solution)/shard_map/ppermute | solution.py:234
  6.2 5.8 %collective-permute-start.1 = (bf16[48,128]{1,0:T(8,128)(2,1)}, bf16[48,128]{1,0:T(8,128)(2,1)S(1)}, u32[]{:S(2)}, u32[]{:S(2)}) collective-permute-start(bf16[48,128]{1,0:T(8,128)(2,1)} %get-tuple-element.8), channel_id=1, source_target_pairs={{16,1},{17,2},{18,3},{19,4},{20,5},{21,6},{22,7},{23,8},{24,9},{25... | collective-permute-start | bytes 36872 | tf_op jit(solution)/shard_map/ppermute | solution.py:235
  12.0 0.1 collective-permute-start.3
  12.1 0.0 collective-permute-done.h_own
  12.2 2.9 %collective-permute-done.1.h_other = bf16[48,128]{1,0:T(8,128)(2,1)S(1)} collective-permute-done((bf16[48,128]{1,0:T(8,128)(2,1)}, bf16[48,128]{1,0:T(8,128)(2,1)S(1)}, u32[]{:S(2)}, u32[]{:S(2)}) %collective-permute-start.1) | collective-permute-done | bytes 12320 | tf_op jit(solution)/shard_map/ppermute | solution.py:235
  15.1 0.8 %pad_maximum_fusion = bf16[16,1280]{1,0:T(8,128)(2,1)S(1)} fusion(bf16[16,128]{1,0:T(8,128)(2,1)S(1)} %slice.9, bf16[16,128]{1,0:T(8,128)(2,1)S(1)} %slice.8, bf16[16,1024]{1,0:T(8,128)(2,1)} %get-tuple-element.6), kind=kLoop, calls=%fused_computation | loop fusion | flops 122880 | bytes 81920 | tf_op jit(solution)/shard_map/concatenate | solution.py:237
  15.9 0.7 %broadcast_in_dim.2 = bf16[8,16,1280]{2,1,0:T(8,128)(2,1)} broadcast(bf16[16,1280]{1,0:T(8,128)(2,1)S(1)} %pad_maximum_fusion), dimensions={1,2} | broadcast | bytes 368640 | tf_op jit(solution)/shard_map/broadcast_in_dim | solution.py:238
  16.6 5.2 %all-to-all-start = ((bf16[8,16,1280]{2,1,0:T(8,128)(2,1)}), bf16[8,16,1280]{2,1,0:T(8,128)(2,1)S(1)}, u32[]{:S(2)}, u32[]{:S(2)}) async-start(bf16[8,16,1280]{2,1,0:T(8,128)(2,1)} %broadcast_in_dim.2), calls=%async_computation | async-start | bytes 655360 | tf_op jit(solution)/shard_map/all_to_all | solution.py:239
  21.8 0.4 collective-permute-start.4
  22.1 1.1 %collective-permute-done.4.c_other = bf16[512,128]{1,0:T(8,128)(2,1)S(1)} collective-permute-done((bf16[512,128]{1,0:T(8,128)(2,1)S(1)}, bf16[512,128]{1,0:T(8,128)(2,1)S(1)}, u32[]{:S(2)}, u32[]{:S(2)}) %collective-permute-start.4) | collective-permute-done | bytes 131104 | tf_op jit(solution)/shard_map/ppermute | solution.py:233
  23.2 0.0 collective-permute-done.3.w_other
  23.2 0.6 %copy-done.7 = bf16[512,128]{1,0:T(8,128)(2,1)} copy-done((bf16[512,128]{1,0:T(8,128)(2,1)}, bf16[512,128]{1,0:T(8,128)(2,1)S(1)}, u32[]{:S(2)}) %copy-start.7) | copy-done | bytes 131096
  23.9 0.7 %copy-done.5 = bf16[4,4,4,8,256]{4,3,2,1,0:T(8,128)(2,1)} copy-done((bf16[4,4,4,8,256]{4,3,2,1,0:T(8,128)(2,1)}, bf16[4,4,4,8,256]{4,3,2,1,0:T(8,128)(2,1)S(1)}, u32[]{:S(2)}) %copy-start.5) | copy-done | bytes 262168
  24.5 3.0 %shard_map.52 = f32[256,512]{1,0:T(8,128)} custom-call(bf16[4,4,4,8,256]{4,3,2,1,0:T(8,128)(2,1)} %bitcast.6, bf16[4,4,4,8,256]{4,3,2,1,0:T(8,128)(2,1)} %copy-done.5, bf16[512,128]{1,0:T(8,128)(2,1)} %get-tuple-element.9.c_own, bf16[512,128]{1,0:T(8,128)(2,1)} %copy-done.7, bf16[48,128]{1,0:T(8,128)(2,1)} %copy-done.2, bf16[48,128]{1,0:T(8,128)(2,1)} %copy-done.3), custom_call_target="tpu_custom_call" | custom-call | flops 500000000 | bytes 1400000 | tf_op jit(solution)/shard_map/pallas_call | solution.py:111
  27.6 2.9 %all-to-all-done.own = bf16[8,16,1280]{2,1,0:T(8,128)(2,1)S(1)} async-done(((bf16[8,16,1280]{2,1,0:T(8,128)(2,1)}), bf16[8,16,1280]{2,1,0:T(8,128)(2,1)S(1)}, u32[]{:S(2)}, u32[]{:S(2)}) %all-to-all-start) | async-done | bytes 327712 | tf_op jit(solution)/shard_map/all_to_all | solution.py:239
  30.5 3.6 %all-to-all-start.1 = ((f32[16,16,512]{2,1,0:T(8,128)}), f32[16,16,512]{2,1,0:T(8,128)S(1)}, u32[]{:S(2)}, u32[]{:S(2)}) async-start(f32[16,16,512]{2,1,0:T(8,128)} %bitcast.4), calls=%async_computation.1 | async-start | bytes 1048576 | tf_op jit(solution)/shard_map/all_to_all | solution.py:242
  34.0 0.4 collective-permute-start.2
  34.4 1.3 %collective-permute-done.2.other = bf16[8,16,1280]{2,1,0:T(8,128)(2,1)S(1)} collective-permute-done((bf16[8,16,1280]{2,1,0:T(8,128)(2,1)S(1)}, bf16[8,16,1280]{2,1,0:T(8,128)(2,1)S(1)}, u32[]{:S(2)}, u32[]{:S(2)}) %collective-permute-start.2) | collective-permute-done | bytes 327712 | tf_op jit(solution)/shard_map/ppermute | solution.py:244
  35.8 0.7 %copy-done.4 = bf16[8,16,1280]{2,1,0:T(8,128)(2,1)} copy-done((bf16[8,16,1280]{2,1,0:T(8,128)(2,1)}, bf16[8,16,1280]{2,1,0:T(8,128)(2,1)S(1)}, u32[]{:S(2)}) %copy-start.4) | copy-done | bytes 327704
  36.5 2.9 %shard_map.51 = bf16[8,4,16,128]{3,2,1,0:T(8,128)(2,1)} custom-call(bf16[512,256]{1,0:T(8,128)(2,1)} %bitcast.7, bf16[8,16,1280]{2,1,0:T(8,128)(2,1)} %copy-done.1, bf16[8,16,1280]{2,1,0:T(8,128)(2,1)} %copy-done.4), custom_call_target="tpu_custom_call" | custom-call | flops 400000000 | bytes 1100000 | tf_op jit(solution)/shard_map/pallas_call | solution.py:204
  39.4 5.4 %all-to-all-done.1.parts = f32[16,16,512]{2,1,0:T(8,128)S(1)} async-done(((f32[16,16,512]{2,1,0:T(8,128)}), f32[16,16,512]{2,1,0:T(8,128)S(1)}, u32[]{:S(2)}, u32[]{:S(2)}) %all-to-all-start.1) | async-done | bytes 524320 | tf_op jit(solution)/shard_map/all_to_all | solution.py:242
  44.8 0.8 %copy-done = f32[16,16,512]{2,1,0:T(8,128)} copy-done((f32[16,16,512]{2,1,0:T(8,128)}, f32[16,16,512]{2,1,0:T(8,128)S(1)}, u32[]{:S(2)}) %copy-start) | copy-done | bytes 524312
  45.6 1.8 %shard_map.53 = bf16[16,2,8,64]{3,2,1,0:T(8,128)(2,1)} custom-call(f32[16,16,512]{2,1,0:T(8,128)} %copy-done), custom_call_target="tpu_custom_call" | custom-call | flops 200000 | bytes 600000 | tf_op jit(solution)/shard_map/pallas_call | solution.py:134
  (14 shorter events, 0.0 us)
Async XLA Ops:
  2.4 9.7 %collective-permute-start = (bf16[48,128]{1,0:T(8,128)(2,1)}, bf16[48,128]{1,0:T(8,128)(2,1)S(1)}, u32[]{:S(2)}, u32[]{:S(2)}) collective-permute-start(bf16[48,128]{1,0:T(8,128)(2,1)} %get-tuple-element.7), channel_id=1, source_target_pairs={{0,1},{1,2},{2,3},{3,4},{4,5},{5,6},{6,7},{7,8},{8,9},{9,10},{10,1... | collective-permute-start | bytes 36872 | tf_op jit(solution)/shard_map/ppermute | solution.py:234
  6.2 8.8 %collective-permute-start.1 = (bf16[48,128]{1,0:T(8,128)(2,1)}, bf16[48,128]{1,0:T(8,128)(2,1)S(1)}, u32[]{:S(2)}, u32[]{:S(2)}) collective-permute-start(bf16[48,128]{1,0:T(8,128)(2,1)} %get-tuple-element.8), channel_id=1, source_target_pairs={{16,1},{17,2},{18,3},{19,4},{20,5},{21,6},{22,7},{23,8},{24,9},{25... | collective-permute-start | bytes 36872 | tf_op jit(solution)/shard_map/ppermute | solution.py:235
  12.0 11.2 %collective-permute-start.3 = (bf16[4,4,4,8,256]{4,3,2,1,0:T(8,128)(2,1)}, bf16[4,4,4,8,256]{4,3,2,1,0:T(8,128)(2,1)S(1)}, u32[]{:S(2)}, u32[]{:S(2)}) collective-permute-start(bf16[4,4,4,8,256]{4,3,2,1,0:T(8,128)(2,1)} %bitcast.5), channel_id=1, source_target_pairs={{0,16},{16,0},{32,48},{48,32},{64,80},{80,64},{96,112},{112,96},{1... | collective-permute-start | bytes 786440 | tf_op jit(solution)/shard_map/ppermute | solution.py:231
  12.2 3.7 %copy-start.2 = (bf16[48,128]{1,0:T(8,128)(2,1)}, bf16[48,128]{1,0:T(8,128)(2,1)S(1)}, u32[]{:S(2)}) copy-start(bf16[48,128]{1,0:T(8,128)(2,1)S(1)} %collective-permute-done.h_own) | copy-start | bytes 36868
  15.1 0.8 %copy-start.3 = (bf16[48,128]{1,0:T(8,128)(2,1)}, bf16[48,128]{1,0:T(8,128)(2,1)S(1)}, u32[]{:S(2)}) copy-start(bf16[48,128]{1,0:T(8,128)(2,1)S(1)} %collective-permute-done.1.h_other) | copy-start | bytes 36868
  16.6 5.2 %copy-start.6 = (bf16[512,128]{1,0:T(8,128)(2,1)S(1)}, bf16[512,128]{1,0:T(8,128)(2,1)}, u32[]{:S(2)}) copy-start(bf16[512,128]{1,0:T(8,128)(2,1)} %get-tuple-element.9.c_own) | copy-start | bytes 393220
  16.6 13.8 %all-to-all-start = ((bf16[8,16,1280]{2,1,0:T(8,128)(2,1)}), bf16[8,16,1280]{2,1,0:T(8,128)(2,1)S(1)}, u32[]{:S(2)}, u32[]{:S(2)}) async-start(bf16[8,16,1280]{2,1,0:T(8,128)(2,1)} %broadcast_in_dim.2), calls=%async_computation | async-start | bytes 655360 | tf_op jit(solution)/shard_map/all_to_all | solution.py:239
  21.8 1.4 %collective-permute-start.4 = (bf16[512,128]{1,0:T(8,128)(2,1)S(1)}, bf16[512,128]{1,0:T(8,128)(2,1)S(1)}, u32[]{:S(2)}, u32[]{:S(2)}) collective-permute-start(bf16[512,128]{1,0:T(8,128)(2,1)S(1)} %copy-done.6), channel_id=1, source_target_pairs={{0,16},{16,0},{32,48},{48,32},{64,80},{80,64},{96,112},{112,96},{1... | collective-permute-start | bytes 393224 | tf_op jit(solution)/shard_map/ppermute | solution.py:233
  23.2 0.7 %copy-start.7 = (bf16[512,128]{1,0:T(8,128)(2,1)}, bf16[512,128]{1,0:T(8,128)(2,1)S(1)}, u32[]{:S(2)}) copy-start(bf16[512,128]{1,0:T(8,128)(2,1)S(1)} %collective-permute-done.4.c_other) | copy-start | bytes 393220
  23.9 0.7 %copy-start.5 = (bf16[4,4,4,8,256]{4,3,2,1,0:T(8,128)(2,1)}, bf16[4,4,4,8,256]{4,3,2,1,0:T(8,128)(2,1)S(1)}, u32[]{:S(2)}) copy-start(bf16[4,4,4,8,256]{4,3,2,1,0:T(8,128)(2,1)S(1)} %collective-permute-done.3.w_other) | copy-start | bytes 786436
  30.5 3.6 %copy-start.1 = (bf16[8,16,1280]{2,1,0:T(8,128)(2,1)}, bf16[8,16,1280]{2,1,0:T(8,128)(2,1)S(1)}, u32[]{:S(2)}) copy-start(bf16[8,16,1280]{2,1,0:T(8,128)(2,1)S(1)} %all-to-all-done.own) | copy-start | bytes 983044
  30.5 14.4 %all-to-all-start.1 = ((f32[16,16,512]{2,1,0:T(8,128)}), f32[16,16,512]{2,1,0:T(8,128)S(1)}, u32[]{:S(2)}, u32[]{:S(2)}) async-start(f32[16,16,512]{2,1,0:T(8,128)} %bitcast.4), calls=%async_computation.1 | async-start | bytes 1048576 | tf_op jit(solution)/shard_map/all_to_all | solution.py:242
  34.0 1.7 %collective-permute-start.2 = (bf16[8,16,1280]{2,1,0:T(8,128)(2,1)S(1)}, bf16[8,16,1280]{2,1,0:T(8,128)(2,1)S(1)}, u32[]{:S(2)}, u32[]{:S(2)}) collective-permute-start(bf16[8,16,1280]{2,1,0:T(8,128)(2,1)S(1)} %all-to-all-done.own), channel_id=1, source_target_pairs={{0,16},{16,0},{32,48},{48,32},{64,80},{80,64},{96,112},{112,96},{1... | collective-permute-start | bytes 983048 | tf_op jit(solution)/shard_map/ppermute | solution.py:244
  35.8 0.7 %copy-start.4 = (bf16[8,16,1280]{2,1,0:T(8,128)(2,1)}, bf16[8,16,1280]{2,1,0:T(8,128)(2,1)S(1)}, u32[]{:S(2)}) copy-start(bf16[8,16,1280]{2,1,0:T(8,128)(2,1)S(1)} %collective-permute-done.2.other) | copy-start | bytes 983044
  44.8 0.8 %copy-start = (f32[16,16,512]{2,1,0:T(8,128)}, f32[16,16,512]{2,1,0:T(8,128)S(1)}, u32[]{:S(2)}) copy-start(f32[16,16,512]{2,1,0:T(8,128)S(1)} %all-to-all-done.1.parts) | copy-start | bytes 1572868

commit v2 on v1

v2 whole, which is shorter than its diff:
```python
import jax
import jax.numpy as jnp
from jax import lax
from jax.experimental import pallas as pl
from jax.experimental.pallas import tpu as pltpu
from jax.sharding import PartitionSpec as P

BF = jnp.bfloat16
F32 = jnp.float32


def s(shape, kind=BF):
    return jax.ShapeDtypeStruct(shape, kind)


def call(body, outs, scratch, cost, **kw):
    return pl.pallas_call(
        body,
        out_shape=outs,
        scratch_shapes=scratch,
        cost_estimate=pl.CostEstimate(flops=cost[0], bytes_accessed=cost[1], transcendentals=0),
        compiler_params=pltpu.CompilerParams(vmem_limit_bytes=12 * 1024 * 1024),
        **kw,
    )


def dot(a, b, dims=((1,), (0,))):
    return lax.dot_general(a, b, (dims, ((), ())), preferred_element_type=F32)


def core_index():
    return lax.rem(lax.axis_index("chan"), 2)


def pick(core, zero, one):
    return jnp.where(jnp.full(zero.shape, core, jnp.int32) == 0, zero, one)


def cell_rows(feat, fs, rows):
    for ch in range(16):
        for u in range(2):
            fs[pl.ds(ch * 16 + u * 8, 8), :] = feat[ch, u].astype(F32)
    return {
        v: jnp.concatenate([fs[pl.ds(v, 16, stride=16), :], fs[pl.ds(8 + v, 16, stride=16), :]], axis=1)
        for v in rows
    }


def fine_rows(cot, cs):
    for o in range(8):
        for a in range(4):
            cs[pl.ds((o * 4 + a) * 16, 16), :] = cot[o, a].astype(F32)


def half_rows(cs, core, out):
    for a in range(4):
        for n in range(9):
            near = cs[pl.ds(a * 16 + n, 8, stride=64), :]
            far = cs[pl.ds(a * 16 + n + 7, 8, stride=64), :]
            out[a, n * 8 : (n + 1) * 8, :] = pick(core, near, far)


def edge_rows(tiles, cs, core):
    first = jnp.concatenate([tiles[0]] + [cs[pl.ds(a * 16, 8, stride=64), :] for a in range(4)], axis=0)
    last = jnp.concatenate([tiles[7]] + [cs[pl.ds(a * 16 + 15, 8, stride=64), :] for a in range(4)], axis=0)
    return pick(core, last, first)


def turned_weights(w, wk, out):
    for p in range(4):
        for r in range(4):
            taps = [w[p, q, r].astype(F32) for q in range(4)]
            wk[pl.ds((p * 4 + r) * 32, 32), :] = jnp.concatenate(taps, axis=0).astype(BF)
    out[...] = wk[...].T


def mine_body(feat_hbm, cot_hbm, w_hbm, flat, edge, rows, wt, w_out, feat, cot, fs, cs, wk, sems):
    core = core_index()
    loads = [
        pltpu.make_async_copy(feat_hbm, feat, sems.at[0]),
        pltpu.make_async_copy(cot_hbm, cot, sems.at[1]),
        pltpu.make_async_copy(w_hbm, w_out, sems.at[2]),
    ]
    for load in loads:
        load.start()
    loads[0].wait()
    tiles = cell_rows(feat, fs, range(8))
    for v in range(8):
        flat[v] = tiles[v].astype(BF)
    loads[1].wait()
    fine_rows(cot, cs)
    edge[...] = edge_rows(tiles, cs, core).astype(BF)
    half_rows(cs, core, rows)
    loads[2].wait()
    turned_weights(w_out, wk, wt)


def mine(feat, cot, w):
    return call(
        mine_body,
        (s((8, 16, 128)), s((48, 128)), s((4, 72, 128), F32), s((256, 512)), s((4, 4, 4, 8, 256))),
        [
            pltpu.VMEM((16, 2, 8, 64), BF),
            pltpu.VMEM((8, 4, 16, 128), BF),
            pltpu.VMEM((256, 64), F32),
            pltpu.VMEM((512, 128), F32),
            pltpu.VMEM((512, 256), BF),
            pltpu.SemaphoreType.DMA((3,)),
        ],
        (0, 1500000),
        in_specs=[pl.BlockSpec(memory_space=pltpu.HBM)] * 3,
    )(feat, cot, w)


def pack_body(feat, cot, flat, edge, both, out, fs, cs):
    core = core_index()
    tiles = cell_rows(feat, fs, range(8))
    for v in range(8):
        own = flat[v].astype(F32)
        both[v] = jnp.concatenate([pick(core, own, tiles[v]), pick(core, tiles[v], own)], axis=0).astype(BF)
    fine_rows(cot, cs)
    own, other = edge[...].astype(F32), edge_rows(tiles, cs, core)
    features = [pick(core, own[:16], other[:16]), pick(core, other[:16], own[:16])]
    out[...] = jnp.concatenate(features + [own[16:], other[16:]], axis=0).astype(BF)


def pack(feat, cot, flat, edge):
    return call(
        pack_body,
        (s((8, 32, 128)), s((96, 128))),
        [pltpu.VMEM((256, 64), F32), pltpu.VMEM((512, 128), F32)],
        (0, 600000),
    )(feat, cot, flat, edge)


def turn_body(cot, w, rows, wt, cs, wk):
    fine_rows(cot, cs)
    half_rows(cs, core_index(), rows)
    turned_weights(w, wk, wt)


def turn(cot, w):
    return call(
        turn_body,
        (s((4, 72, 128), F32), s((256, 512))),
        [pltpu.VMEM((512, 128), F32), pltpu.VMEM((512, 256), BF)],
        (0, 1500000),
    )(cot, w)


def merge_body(both, halo, halo_o, out):
    core = core_index()
    own, other = halo[0:32, :].astype(F32), halo_o[0:32, :].astype(F32)
    out[0] = pick(core, own, other).astype(BF)
    out[9] = pick(core, other, own).astype(BF)
    for v in range(8):
        out[v + 1] = both[v]


def merge(both, halo, halo_o):
    return call(merge_body, s((10, 32, 128)), [], (0, 200000))(both, halo, halo_o)


def grad_body(wt, wt_o, rows, rows_o, halo, out, cols):
    core = core_index()
    i = lax.broadcasted_iota(jnp.int32, (256, 512), 0)
    j = lax.broadcasted_iota(jnp.int32, (256, 512), 1)
    want = 2 * (j & 63) + (j >> 7) - 1
    same = (i >> 7) == ((j >> 6) & 1)
    select = jnp.where(((i & 127) == want) & same, 1.0, 0.0).astype(BF)
    zero = jnp.zeros((80, 128), BF)
    for k, body in enumerate((rows, rows_o)):
        plane = []
        for a in range(4):
            at = 32 + (k * 4 + a) * 8
            edge = halo[at : at + 8, :].astype(F32)
            whole = pick(
                core, jnp.concatenate([edge, body[a]], axis=0), jnp.concatenate([body[a], edge], axis=0)
            )
            plane.append(whole.astype(BF))
        for p in range(4):
            low = plane[p - 1] if p > 0 else zero
            high = plane[p + 1] if p < 3 else zero
            cols[k, p] = dot(jnp.concatenate([low, high], axis=1), select).astype(BF)
    for pair in range(2):
        sides = []
        for k in range(2):
            halves = []
            for v in (2 * pair, 2 * pair + 1):
                parts = [
                    cols[k, p, 16 * v : 16 * v + 32, r * 128 : (r + 1) * 128] for p in range(4) for r in range(4)
                ]
                halves.append(jnp.concatenate(parts, axis=0))
            sides.append(jnp.concatenate(halves, axis=1))
        out[:, pair * 256 : (pair + 1) * 256] = dot(wt[...], sides[0]) + dot(wt_o[...], sides[1])


def grad(wt, wt_o, rows, rows_o, halo):
    return call(
        grad_body,
        s((256, 512), F32),
        [pltpu.VMEM((2, 4, 80, 512), BF)],
        (500000000, 1400000),
    )(wt, wt_o, rows, rows_o, halo)


def total_body(parts, out, rows):
    for half in range(2):
        acc = parts[half]
        for chip in range(1, 8):
            acc = acc + parts[2 * chip + half]
        for k in range(4):
            v = 4 * half + k
            for u in range(2):
                rows[pl.ds(u * 8 + v, 16, stride=16), :] = acc[:, k * 128 + u * 64 : k * 128 + (u + 1) * 64]
    for ch in range(16):
        for u in range(2):
            out[ch, u] = rows[pl.ds(ch * 16 + u * 8, 8), :].astype(BF)


def total(parts):
    return call(total_body, s((16, 2, 8, 64)), [pltpu.VMEM((256, 64), F32)], (200000, 600000))(parts)


def up_body(weights, own, side, side_y, far, away, side_o, side_y_o, far_o, out, f, y, fine):
    me = lax.axis_index("chan")
    core = lax.rem(me, 2)
    x, row = lax.rem(lax.div(me, 2), 4), lax.div(me, 8)
    near = lax.rem(x + 3 + 2 * core, 4)
    near_o = lax.rem(x + 5 - 2 * core, 4)
    across = lax.rem(x + 2, 4)
    flip = 1 - row
    far_row = row + core - 2 * row * core
    places = (
        (own, x, row),
        (away, x, flip),
        (side, near, row),
        (side_o, near_o, row),
        (side_y, near, flip),
        (side_y_o, near_o, flip),
        (far, across, far_row),
        (far_o, across, 1 - far_row),
    )
    for ref, px, py in places:
        rows = pl.ds(pl.multiple_of((py * 4 + px) * 32, 32), 32)
        for t in range(10):
            f[t, rows, :] = ref[t]
    w = weights[...]
    for t in range(5):
        y[t] = dot(w, jnp.concatenate([f[2 * t], f[2 * t + 1]], axis=1))

    def tap(p, q, r, v):
        t = v + 1
        return y[t // 2, pl.ds(((p * 4 + q) * 4 + r) * 8, 8), (t % 2) * 128 : (t % 2 + 1) * 128]

    lane = lax.broadcasted_iota(jnp.int32, (8, 128), 1)
    first_half = lane < 64
    cell = lane & 63
    ii = lax.broadcasted_iota(jnp.int32, (256, 256), 0)
    jj = lax.broadcasted_iota(jnp.int32, (256, 256), 1)
    spread = jnp.where(((jj >> 7) == ((ii >> 6) & 1)) & ((jj & 127) == 2 * (ii & 63) + (ii >> 7)), 1.0, 0.0).astype(BF)
    for pb in range(2):
        blocks = {0: [], 1: []}
        for n in range(8):
            pairs = ((1, n), (3, n - 1)) if pb == 0 else ((2, n), (0, n + 1))
            got = {0: [], 1: []}
            for r in range(4):
                t = [sum(tap(p, q, r, v) for q, v in pairs) for p in range(4)]
                moved = pltpu.roll(jnp.where(first_half, t[3], t[0]), 64, 1)
                got[0].append(t[1] + jnp.where(first_half, 0.0, moved))
                got[1].append(t[2] + jnp.where(first_half, moved, 0.0))
            for pa in range(2):
                t0, t1, t2, t3 = got[pa]
                even = t1 + jnp.where(cell == 0, 0.0, pltpu.roll(t3, 1, 1))
                odd = t2 + jnp.where(cell == 63, 0.0, pltpu.roll(t0, 127, 1))
                blocks[pa].append(jnp.concatenate([even, odd], axis=1))
        for pa in range(2):
            rows = dot(jnp.concatenate(blocks[pa], axis=0).astype(BF), spread)
            for n in range(8):
                for m in range(2):
                    fine[pl.ds((2 * m + pa) * 16 + 2 * n + pb, 8, stride=64), :] = rows[
                        n * 8 : (n + 1) * 8, m * 128 : (m + 1) * 128
                    ]
    for o in range(8):
        for a in range(4):
            out[o, a] = fine[pl.ds((o * 4 + a) * 16, 16), :].astype(BF)


def upsample(weights, *blocks):
    return call(
        up_body,
        s((8, 4, 16, 128)),
        [pltpu.VMEM((10, 256, 128), BF), pltpu.VMEM((5, 512, 256), F32), pltpu.VMEM((512, 128), F32)],
        (400000000, 1100000),
    )(weights, *blocks)


def local(features, weights, cotangent):
    tiles = lax.axis_size("space")
    chans = lax.axis_size("chan")
    at = lambda ch, sp: ch * tiles + sp
    index = lambda x, row, core: (row * 4 + x % 4) * 2 + core
    swap = [(ch, ch ^ 1) for ch in range(chans)]
    cross = []
    for ch in range(chans):
        for sp in range(tiles):
            to = sp + 1 - 2 * (ch % 2)
            if 0 <= to < tiles:
                cross.append((at(ch, sp), at(ch, to)))
    chips = [(x, row, core) for row in range(2) for x in range(4) for core in range(2)]
    beside = [(index(x, row, c), index(x + 1 - 2 * c, row, c)) for x, row, c in chips]
    beside_y = [(index(x, row, c), index(x + 1 - 2 * c, 1 - row, c)) for x, row, c in chips]
    over = [(index(x, row, c), index(x + 2, (row + c) % 2, c)) for x, row, c in chips]
    over_y = [(index(x, row, c), index(x, 1 - row, c)) for x, row, c in chips]
    send = lambda a, pairs: lax.ppermute(a, "chan", pairs)

    w_own = jnp.transpose(weights, (0, 1, 2, 4, 3))
    cot_other, feat_other, w_other = send(cotangent, swap), send(features, swap), send(w_own, swap)
    flat, edge, rows, wt, w_near = mine(features, cotangent, w_own)
    cot_other, feat_other, w_other, flat = lax.optimization_barrier((cot_other, feat_other, w_other, flat))
    both, edges = pack(feat_other, cot_other, flat, edge)
    halo = lax.ppermute(edges, ("chan", "space"), cross)
    rows_other, wt_other = turn(cot_other, w_other)
    halo_other = send(halo, swap)

    partial = grad(wt, wt_other, rows, rows_other, halo)
    chip = merge(both, halo, halo_other)
    side, away = send(chip, beside), send(chip, over_y)
    pieces = lax.all_to_all(partial.reshape(16, 16, 512), "chan", 0, 0, tiled=True)
    side_y, far = send(chip, beside_y), send(chip, over)
    side_o, side_y_o, far_o = send(side, swap), send(side_y, swap), send(far, swap)
    decoded = upsample(w_near.reshape(512, 256), chip, side, side_y, far, away, side_o, side_y_o, far_o)
    return decoded, total(pieces)


def solution(mesh):
    return jax.shard_map(
        local,
        mesh=mesh,
        in_specs=(
            P("chan", None, "space", None),
            P(None, None, None, None, "chan"),
            P("chan", None, "space", None),
        ),
        out_specs=(P("chan", None, "space", None), P("chan", None, "space", None)),
        check_vma=False,
    )
```

time: 47.9 us -> 40.1 us (0.84)
  the two profiles are of different devices: /device:TPU:16 before, /device:TPU:25 now
where the time goes in v2:
time: 40.1 us; the launch traced here: 39.6 us
  starting transfers between devices  23.7 us (59%)
  waiting for transfers between devices  7.4 us (18%)
  Pallas kernels  5.19 us (13%)
  local copies, waits for them, and re-layouts  2.69 us (7%)
  between operations  0.7 us (2%)
    ppermute x11, starting transfers between devices, local(): send = lambda a, pairs: lax.ppermute(a, 'chan', pairs)  8.86 us
    ppermute x1, starting transfers between devices, local(): halo = lax.ppermute(edges, ('chan', 'space'), cross)  8.16 us
    ppermute x11, waiting for transfers between devices, local(): send = lambda a, pairs: lax.ppermute(a, 'chan', pairs)  6.69 us
    all_to_all x1, starting transfers between devices, local(): lax.all_to_all(partial.reshape(16, 16, 512), 'chan', 0, 0, tiled=True)  6.63 us
    unnamed x6, local copies, waits for them, and re-layouts  2.69 us
    pallas_call x1, Pallas kernels, upsample(): call(up_body, s((8, 4, 16, 128)), [pltpu.VMEM((10, 256, 128), BF), pltpu....  1.74 us
    pallas_call x1, Pallas kernels, grad(): call(grad_body, s((256, 512), F32), [pltpu.VMEM((2, 4, 80, 512), BF)], (5...  1.72 us
  transfers between devices with their start and end apart: 13, of which 5 were waited for; matrix products, arithmetic and copies ran while one was open for 0% of the time, Pallas kernels for 7%

profile of v2, /device:TPU:25, one launch (start us, length us, event | category | flops | bytes accessed | tf_op | source)
XLA Modules:
  0.0 39.6 jit_solution(6576880276777058321)
XLA Ops:
  0.6 0.8 %collective-permute-start.2 = (bf16[4,4,4,8,256]{4,3,2,1,0:T(8,128)(2,1)}, bf16[4,4,4,8,256]{4,3,2,1,0:T(8,128)(2,1)S(1)}, u32[]{:S(2)}, u32[]{:S(2)}) collective-permute-start(bf16[4,4,4,8,256]{4,3,2,1,0:T(8,128)(2,1)} %bitcast.3), channel_id=1, source_target_pairs={{0,16},{16,0},{32,48},{48,32},{64,80},{80,64},{96,112},{112,96},{1... | collective-permute-start | bytes 786440 | tf_op jit(solution)/shard_map/ppermute | solution.py:315
  1.5 0.4 %collective-permute-start.1 = (bf16[16,2,8,64]{3,2,1,0:T(8,128)(2,1)}, bf16[16,2,8,64]{3,2,1,0:T(8,128)(2,1)S(1)}, u32[]{:S(2)}, u32[]{:S(2)}) collective-permute-start(bf16[16,2,8,64]{3,2,1,0:T(8,128)(2,1)} %feat_hbm.1), channel_id=1, source_target_pairs={{0,16},{16,0},{32,48},{48,32},{64,80},{80,64},{96,112},{112,96},{1... | collective-permute-start | bytes 98312 | tf_op jit(solution)/shard_map/ppermute | solution.py:315
  1.9 0.9 %copy-done = bf16[4,4,4,256,8]{3,4,2,1,0:T(8,128)(2,1)S(1)} copy-done((bf16[4,4,4,256,8]{3,4,2,1,0:T(8,128)(2,1)S(1)}, bf16[4,4,4,256,8]{3,4,2,1,0:T(8,128)(2,1)}, u32[]{:S(2)}) %copy-start) | copy-done | bytes 262168
  2.9 0.9 %copy-done.1 = bf16[8,4,16,128]{3,2,1,0:T(8,128)(2,1)S(1)} copy-done((bf16[8,4,16,128]{3,2,1,0:T(8,128)(2,1)S(1)}, bf16[8,4,16,128]{3,2,1,0:T(8,128)(2,1)}, u32[]{:S(2)}) %copy-start.1) | copy-done | bytes 131096
  3.8 0.8 %copy-done.2 = bf16[16,2,8,64]{3,2,1,0:T(8,128)(2,1)S(1)} copy-done((bf16[16,2,8,64]{3,2,1,0:T(8,128)(2,1)S(1)}, bf16[16,2,8,64]{3,2,1,0:T(8,128)(2,1)}, u32[]{:S(2)}) %copy-start.2) | copy-done | bytes 32792
  4.6 0.7 %shard_map.50 = (bf16[8,16,128]{2,1,0:T(8,128)(2,1)S(1)}, bf16[48,128]{1,0:T(8,128)(2,1)S(1)}, f32[4,72,128]{2,1,0:T(8,128)S(1)}, bf16[256,512]{1,0:T(8,128)(2,1)S(1)}, bf16[4,4,4,8,256]{4,3,2,1,0:T(8,128)(2,1)S(1)}) custom-call(bf16[16,2,8,64]{3,2,1,0:T(8,128)(2,1)S(1)} %copy-done.2, bf16[8,4,16,128]{3,2,1,0:T(8,128)(2,1)S(1)} %copy-done.1, ...), custom_call_target="tpu_custom_call" | custom-call | bytes 1500000 | tf_op jit(solution)/shard_map/pallas_call | solution.py:99
  5.4 8.2 %collective-permute-start.3 = (bf16[96,128]{1,0:T(8,128)(2,1)S(1)}, bf16[96,128]{1,0:T(8,128)(2,1)S(1)}, u32[]{:S(2)}, u32[]{:S(2)}) collective-permute-start(bf16[96,128]{1,0:T(8,128)(2,1)S(1)} %get-tuple-element.22), channel_id=1, source_target_pairs={{0,1},{1,2},{2,3},{3,4},{4,5},{5,6},{6,7},{7,8},{8,9},{9,10},{10,1... | collective-permute-start | bytes 73736 | tf_op jit(solution)/shard_map/ppermute | solution.py:322
  13.6 0.2 shard_map.54
  13.8 0.7 %collective-permute-done.3.halo = bf16[96,128]{1,0:T(8,128)(2,1)S(1)} collective-permute-done((bf16[96,128]{1,0:T(8,128)(2,1)S(1)}, bf16[96,128]{1,0:T(8,128)(2,1)S(1)}, u32[]{:S(2)}, u32[]{:S(2)}) %collective-permute-start.3) | collective-permute-done | bytes 24608 | tf_op jit(solution)/shard_map/ppermute | solution.py:322
  14.5 1.7 %shard_map.55 = f32[256,512]{1,0:T(8,128)} custom-call(bf16[256,512]{1,0:T(8,128)(2,1)S(1)} %get-tuple-element.23.wt, bf16[256,512]{1,0:T(8,128)(2,1)S(1)} %get-tuple-element.25.wt_o, f32[4,72,128]{2,1,0:T(8,128)S(1)} %get-tuple-element.26.rows, f32[4,72,128]{2,1,0:T(8,128)S(1)} %get-tuple-element.27.rows_o, bf16[96,128]{1,0:T(8,128)(2,1)S(1)} %collective-permute-done.3.halo), custom_call_target="tpu_custom_call" | custom-call | flops 500000000 | bytes 1400000 | tf_op jit(solution)/shard_map/pallas_call | solution.py:199
  16.2 6.6 %all-to-all-start = ((f32[16,16,512]{2,1,0:T(8,128)}), f32[16,16,512]{2,1,0:T(8,128)S(1)}, u32[]{:S(2)}, u32[]{:S(2)}) async-start(f32[16,16,512]{2,1,0:T(8,128)} %bitcast.2), calls=%async_computation | async-start | bytes 1048576 | tf_op jit(solution)/shard_map/all_to_all | solution.py:329
  22.9 0.4 collective-permute-start.4
  23.3 0.9 %collective-permute-done.4.halo_o = bf16[96,128]{1,0:T(8,128)(2,1)S(1)} collective-permute-done((bf16[96,128]{1,0:T(8,128)(2,1)S(1)}, bf16[96,128]{1,0:T(8,128)(2,1)S(1)}, u32[]{:S(2)}, u32[]{:S(2)}) %collective-permute-start.4) | collective-permute-done | bytes 24608 | tf_op jit(solution)/shard_map/ppermute | solution.py:315
  24.2 2.8 %collective-permute-start.7 = (bf16[10,32,128]{2,1,0:T(8,128)(2,1)S(1)}, bf16[10,32,128]{2,1,0:T(8,128)(2,1)S(1)}, u32[]{:S(2)}, u32[]{:S(2)}) collective-permute-start(bf16[10,32,128]{2,1,0:T(8,128)(2,1)S(1)} %shard_map.52.own), channel_id=1, source_target_pairs={{0,64},{16,208},{32,96},{48,240},{64,0},{80,144},{96,32},{112,176}... | collective-permute-start | bytes 245768 | tf_op jit(solution)/shard_map/ppermute | solution.py:315
  27.0 1.8 %collective-permute-start.6 = (bf16[10,32,128]{2,1,0:T(8,128)(2,1)S(1)}, bf16[10,32,128]{2,1,0:T(8,128)(2,1)S(1)}, u32[]{:S(2)}, u32[]{:S(2)}) collective-permute-start(bf16[10,32,128]{2,1,0:T(8,128)(2,1)S(1)} %shard_map.52.own), channel_id=1, source_target_pairs={{0,160},{16,240},{32,192},{48,144},{64,224},{80,176},{96,128},{112... | collective-permute-start | bytes 245768 | tf_op jit(solution)/shard_map/ppermute | solution.py:315
  28.8 0.3 collective-permute-start.8
  29.1 4.8 %collective-permute-done.7.far = bf16[10,32,128]{2,1,0:T(8,128)(2,1)S(1)} collective-permute-done((bf16[10,32,128]{2,1,0:T(8,128)(2,1)S(1)}, bf16[10,32,128]{2,1,0:T(8,128)(2,1)S(1)}, u32[]{:S(2)}, u32[]{:S(2)}) %collective-permute-start.7) | collective-permute-done | bytes 81952 | tf_op jit(solution)/shard_map/ppermute | solution.py:315
  33.9 0.9 %collective-permute-start.11 = (bf16[10,32,128]{2,1,0:T(8,128)(2,1)S(1)}, bf16[10,32,128]{2,1,0:T(8,128)(2,1)S(1)}, u32[]{:S(2)}, u32[]{:S(2)}) collective-permute-start(bf16[10,32,128]{2,1,0:T(8,128)(2,1)S(1)} %collective-permute-done.7.far), channel_id=1, source_target_pairs={{0,16},{16,0},{32,48},{48,32},{64,80},{80,64},{96,112},{112,96},{1... | collective-permute-start | bytes 245768 | tf_op jit(solution)/shard_map/ppermute | solution.py:315
  34.8 0.7 %collective-permute-start.10 = (bf16[10,32,128]{2,1,0:T(8,128)(2,1)S(1)}, bf16[10,32,128]{2,1,0:T(8,128)(2,1)S(1)}, u32[]{:S(2)}, u32[]{:S(2)}) collective-permute-start(bf16[10,32,128]{2,1,0:T(8,128)(2,1)S(1)} %collective-permute-done.6.side_y), channel_id=1, source_target_pairs={{0,16},{16,0},{32,48},{48,32},{64,80},{80,64},{96,112},{112,96},{1... | collective-permute-start | bytes 245768 | tf_op jit(solution)/shard_map/ppermute | solution.py:315
  35.4 0.8 %collective-permute-start.9 = (bf16[10,32,128]{2,1,0:T(8,128)(2,1)S(1)}, bf16[10,32,128]{2,1,0:T(8,128)(2,1)S(1)}, u32[]{:S(2)}, u32[]{:S(2)}) collective-permute-start(bf16[10,32,128]{2,1,0:T(8,128)(2,1)S(1)} %collective-permute-done.5.side), channel_id=1, source_target_pairs={{0,16},{16,0},{32,48},{48,32},{64,80},{80,64},{96,112},{112,96},{1... | collective-permute-start | bytes 245768 | tf_op jit(solution)/shard_map/ppermute | solution.py:315
  36.2 0.1 collective-permute-done.10.side_y_o
  36.4 0.8 %collective-permute-done.9.side_o = bf16[10,32,128]{2,1,0:T(8,128)(2,1)S(1)} collective-permute-done((bf16[10,32,128]{2,1,0:T(8,128)(2,1)S(1)}, bf16[10,32,128]{2,1,0:T(8,128)(2,1)S(1)}, u32[]{:S(2)}, u32[]{:S(2)}) %collective-permute-start.9) | collective-permute-done | bytes 81952 | tf_op jit(solution)/shard_map/ppermute | solution.py:315
  37.1 1.7 %shard_map.53 = bf16[8,4,16,128]{3,2,1,0:T(8,128)(2,1)} custom-call(bf16[512,256]{1,0:T(8,128)(2,1)S(1)} %bitcast.5, bf16[10,32,128]{2,1,0:T(8,128)(2,1)S(1)} %shard_map.52.own, bf16[10,32,128]{2,1,0:T(8,128)(2,1)S(1)} %collective-permute-done.5.side, bf16[10,32,128]{2,1,0:T(8,128)(2,1)S(1)} %collective-permute-done.6.side_y, ...), custom_call_target="tpu_custom_call" | custom-call | flops 400000000 | bytes 1100000 | tf_op jit(solution)/shard_map/pallas_call | solution.py:290
  38.9 0.7 %shard_map.56 = bf16[16,2,8,64]{3,2,1,0:T(8,128)(2,1)} custom-call(f32[16,16,512]{2,1,0:T(8,128)S(1)} %all-to-all-done.parts), custom_call_target="tpu_custom_call" | custom-call | flops 200000 | bytes 600000 | tf_op jit(solution)/shard_map/pallas_call | solution.py:222
  (15 shorter events, 0.2 us)
Async XLA Ops:
  0.6 4.7 %collective-permute-start.2 = (bf16[4,4,4,8,256]{4,3,2,1,0:T(8,128)(2,1)}, bf16[4,4,4,8,256]{4,3,2,1,0:T(8,128)(2,1)S(1)}, u32[]{:S(2)}, u32[]{:S(2)}) collective-permute-start(bf16[4,4,4,8,256]{4,3,2,1,0:T(8,128)(2,1)} %bitcast.3), channel_id=1, source_target_pairs={{0,16},{16,0},{32,48},{48,32},{64,80},{80,64},{96,112},{112,96},{1... | collective-permute-start | bytes 786440 | tf_op jit(solution)/shard_map/ppermute | solution.py:315
  1.4 3.9 %collective-permute-start = (bf16[8,4,16,128]{3,2,1,0:T(8,128)(2,1)}, bf16[8,4,16,128]{3,2,1,0:T(8,128)(2,1)S(1)}, u32[]{:S(2)}, u32[]{:S(2)}) collective-permute-start(bf16[8,4,16,128]{3,2,1,0:T(8,128)(2,1)} %cot_hbm.1), channel_id=1, source_target_pairs={{0,16},{16,0},{32,48},{48,32},{64,80},{80,64},{96,112},{112,96},{1... | collective-permute-start | bytes 393224 | tf_op jit(solution)/shard_map/ppermute | solution.py:315
  1.5 3.8 %collective-permute-start.1 = (bf16[16,2,8,64]{3,2,1,0:T(8,128)(2,1)}, bf16[16,2,8,64]{3,2,1,0:T(8,128)(2,1)S(1)}, u32[]{:S(2)}, u32[]{:S(2)}) collective-permute-start(bf16[16,2,8,64]{3,2,1,0:T(8,128)(2,1)} %feat_hbm.1), channel_id=1, source_target_pairs={{0,16},{16,0},{32,48},{48,32},{64,80},{80,64},{96,112},{112,96},{1... | collective-permute-start | bytes 98312 | tf_op jit(solution)/shard_map/ppermute | solution.py:315
  1.9 0.9 %copy-start = (bf16[4,4,4,256,8]{3,4,2,1,0:T(8,128)(2,1)S(1)}, bf16[4,4,4,256,8]{3,4,2,1,0:T(8,128)(2,1)}, u32[]{:S(2)}) copy-start(bf16[4,4,4,256,8]{3,4,2,1,0:T(8,128)(2,1)} %param.4) | copy-start | bytes 786436
  2.9 0.9 %copy-start.1 = (bf16[8,4,16,128]{3,2,1,0:T(8,128)(2,1)S(1)}, bf16[8,4,16,128]{3,2,1,0:T(8,128)(2,1)}, u32[]{:S(2)}) copy-start(bf16[8,4,16,128]{3,2,1,0:T(8,128)(2,1)} %cot_hbm.1) | copy-start | bytes 393220
  3.8 0.8 %copy-start.2 = (bf16[16,2,8,64]{3,2,1,0:T(8,128)(2,1)S(1)}, bf16[16,2,8,64]{3,2,1,0:T(8,128)(2,1)}, u32[]{:S(2)}) copy-start(bf16[16,2,8,64]{3,2,1,0:T(8,128)(2,1)} %feat_hbm.1) | copy-start | bytes 98308
  5.4 9.1 %collective-permute-start.3 = (bf16[96,128]{1,0:T(8,128)(2,1)S(1)}, bf16[96,128]{1,0:T(8,128)(2,1)S(1)}, u32[]{:S(2)}, u32[]{:S(2)}) collective-permute-start(bf16[96,128]{1,0:T(8,128)(2,1)S(1)} %get-tuple-element.22), channel_id=1, source_target_pairs={{0,1},{1,2},{2,3},{3,4},{4,5},{5,6},{6,7},{7,8},{8,9},{9,10},{10,1... | collective-permute-start | bytes 73736 | tf_op jit(solution)/shard_map/ppermute | solution.py:322
  16.2 22.7 %all-to-all-start = ((f32[16,16,512]{2,1,0:T(8,128)}), f32[16,16,512]{2,1,0:T(8,128)S(1)}, u32[]{:S(2)}, u32[]{:S(2)}) async-start(f32[16,16,512]{2,1,0:T(8,128)} %bitcast.2), calls=%async_computation | async-start | bytes 1048576 | tf_op jit(solution)/shard_map/all_to_all | solution.py:329
  22.9 1.3 %collective-permute-start.4 = (bf16[96,128]{1,0:T(8,128)(2,1)S(1)}, bf16[96,128]{1,0:T(8,128)(2,1)S(1)}, u32[]{:S(2)}, u32[]{:S(2)}) collective-permute-start(bf16[96,128]{1,0:T(8,128)(2,1)S(1)} %collective-permute-done.3.halo), channel_id=1, source_target_pairs={{0,16},{16,0},{32,48},{48,32},{64,80},{80,64},{96,112},{112,96},{1... | collective-permute-start | bytes 73736 | tf_op jit(solution)/shard_map/ppermute | solution.py:315
  24.2 9.7 %collective-permute-start.7 = (bf16[10,32,128]{2,1,0:T(8,128)(2,1)S(1)}, bf16[10,32,128]{2,1,0:T(8,128)(2,1)S(1)}, u32[]{:S(2)}, u32[]{:S(2)}) collective-permute-start(bf16[10,32,128]{2,1,0:T(8,128)(2,1)S(1)} %shard_map.52.own), channel_id=1, source_target_pairs={{0,64},{16,208},{32,96},{48,240},{64,0},{80,144},{96,32},{112,176}... | collective-permute-start | bytes 245768 | tf_op jit(solution)/shard_map/ppermute | solution.py:315
  27.0 7.8 %collective-permute-start.6 = (bf16[10,32,128]{2,1,0:T(8,128)(2,1)S(1)}, bf16[10,32,128]{2,1,0:T(8,128)(2,1)S(1)}, u32[]{:S(2)}, u32[]{:S(2)}) collective-permute-start(bf16[10,32,128]{2,1,0:T(8,128)(2,1)S(1)} %shard_map.52.own), channel_id=1, source_target_pairs={{0,160},{16,240},{32,192},{48,144},{64,224},{80,176},{96,128},{112... | collective-permute-start | bytes 245768 | tf_op jit(solution)/shard_map/ppermute | solution.py:315
  28.8 6.7 %collective-permute-start.5 = (bf16[10,32,128]{2,1,0:T(8,128)(2,1)S(1)}, bf16[10,32,128]{2,1,0:T(8,128)(2,1)S(1)}, u32[]{:S(2)}, u32[]{:S(2)}) collective-permute-start(bf16[10,32,128]{2,1,0:T(8,128)(2,1)S(1)} %shard_map.52.own), channel_id=1, source_target_pairs={{0,32},{16,112},{32,64},{48,16},{64,96},{80,48},{96,0},{112,80},{1... | collective-permute-start | bytes 245768 | tf_op jit(solution)/shard_map/ppermute | solution.py:315
  28.8 7.5 %collective-permute-start.8 = (bf16[10,32,128]{2,1,0:T(8,128)(2,1)S(1)}, bf16[10,32,128]{2,1,0:T(8,128)(2,1)S(1)}, u32[]{:S(2)}, u32[]{:S(2)}) collective-permute-start(bf16[10,32,128]{2,1,0:T(8,128)(2,1)S(1)} %shard_map.52.own), channel_id=1, source_target_pairs={{0,128},{16,144},{32,160},{48,176},{64,192},{80,208},{96,224},{112... | collective-permute-start | bytes 245768 | tf_op jit(solution)/shard_map/ppermute | solution.py:315
  33.9 2.4 %collective-permute-start.11 = (bf16[10,32,128]{2,1,0:T(8,128)(2,1)S(1)}, bf16[10,32,128]{2,1,0:T(8,128)(2,1)S(1)}, u32[]{:S(2)}, u32[]{:S(2)}) collective-permute-start(bf16[10,32,128]{2,1,0:T(8,128)(2,1)S(1)} %collective-permute-done.7.far), channel_id=1, source_target_pairs={{0,16},{16,0},{32,48},{48,32},{64,80},{80,64},{96,112},{112,96},{1... | collective-permute-start | bytes 245768 | tf_op jit(solution)/shard_map/ppermute | solution.py:315
  34.8 1.6 %collective-permute-start.10 = (bf16[10,32,128]{2,1,0:T(8,128)(2,1)S(1)}, bf16[10,32,128]{2,1,0:T(8,128)(2,1)S(1)}, u32[]{:S(2)}, u32[]{:S(2)}) collective-permute-start(bf16[10,32,128]{2,1,0:T(8,128)(2,1)S(1)} %collective-permute-done.6.side_y), channel_id=1, source_target_pairs={{0,16},{16,0},{32,48},{48,32},{64,80},{80,64},{96,112},{112,96},{1... | collective-permute-start | bytes 245768 | tf_op jit(solution)/shard_map/ppermute | solution.py:315
  35.4 1.7 %collective-permute-start.9 = (bf16[10,32,128]{2,1,0:T(8,128)(2,1)S(1)}, bf16[10,32,128]{2,1,0:T(8,128)(2,1)S(1)}, u32[]{:S(2)}, u32[]{:S(2)}) collective-permute-start(bf16[10,32,128]{2,1,0:T(8,128)(2,1)S(1)} %collective-permute-done.5.side), channel_id=1, source_target_pairs={{0,16},{16,0},{32,48},{48,32},{64,80},{80,64},{96,112},{112,96},{1... | collective-permute-start | bytes 245768 | tf_op jit(solution)/shard_map/ppermute | solution.py:315

commit v3 on v2

--- a/solution.py
+++ b/solution.py
@@ -13,13 +13,13 @@
     return jax.ShapeDtypeStruct(shape, kind)
 
 
-def call(body, outs, scratch, cost, **kw):
+def call(body, outs, scratch, cost, limit=12 * 1024, **kw):
     return pl.pallas_call(
         body,
         out_shape=outs,
         scratch_shapes=scratch,
         cost_estimate=pl.CostEstimate(flops=cost[0], bytes_accessed=cost[1], transcendentals=0),
-        compiler_params=pltpu.CompilerParams(vmem_limit_bytes=12 * 1024 * 1024),
+        compiler_params=pltpu.CompilerParams(vmem_limit_bytes=limit * 1024),
         **kw,
     )
 
@@ -52,12 +52,10 @@
             cs[pl.ds((o * 4 + a) * 16, 16), :] = cot[o, a].astype(F32)
 
 
-def half_rows(cs, core, out):
+def turned_rows(cs, out):
     for a in range(4):
-        for n in range(9):
-            near = cs[pl.ds(a * 16 + n, 8, stride=64), :]
-            far = cs[pl.ds(a * 16 + n + 7, 8, stride=64), :]
-            out[a, n * 8 : (n + 1) * 8, :] = pick(core, near, far)
+        for n in range(16):
+            out[a, n * 8 : (n + 1) * 8, :] = cs[pl.ds(a * 16 + n, 8, stride=64), :]
 
 
 def edge_rows(tiles, cs, core):
@@ -74,13 +72,9 @@
     out[...] = wk[...].T
 
 
-def mine_body(feat_hbm, cot_hbm, w_hbm, flat, edge, rows, wt, w_out, feat, cot, fs, cs, wk, sems):
+def mine_body(feat_hbm, cot_hbm, flat, edge, cot, feat, fs, cs, sems):
     core = core_index()
-    loads = [
-        pltpu.make_async_copy(feat_hbm, feat, sems.at[0]),
-        pltpu.make_async_copy(cot_hbm, cot, sems.at[1]),
-        pltpu.make_async_copy(w_hbm, w_out, sems.at[2]),
-    ]
+    loads = [pltpu.make_async_copy(feat_hbm, feat, sems.at[0]), pltpu.make_async_copy(cot_hbm, cot, sems.at[1])]
     for load in loads:
         load.start()
     loads[0].wait()
@@ -90,26 +84,21 @@
     loads[1].wait()
     fine_rows(cot, cs)
     edge[...] = edge_rows(tiles, cs, core).astype(BF)
-    half_rows(cs, core, rows)
-    loads[2].wait()
-    turned_weights(w_out, wk, wt)
-
-
-def mine(feat, cot, w):
+
+
+def mine(feat, cot):
     return call(
         mine_body,
-        (s((8, 16, 128)), s((48, 128)), s((4, 72, 128), F32), s((256, 512)), s((4, 4, 4, 8, 256))),
+        (s((8, 16, 128)), s((48, 128)), s((8, 4, 16, 128))),
         [
             pltpu.VMEM((16, 2, 8, 64), BF),
-            pltpu.VMEM((8, 4, 16, 128), BF),
             pltpu.VMEM((256, 64), F32),
             pltpu.VMEM((512, 128), F32),
-            pltpu.VMEM((512, 256), BF),
-            pltpu.SemaphoreType.DMA((3,)),
+            pltpu.SemaphoreType.DMA((2,)),
         ],
-        (0, 1500000),
-        in_specs=[pl.BlockSpec(memory_space=pltpu.HBM)] * 3,
-    )(feat, cot, w)
+        (0, 1000000),
+        in_specs=[pl.BlockSpec(memory_space=pltpu.HBM)] * 2,
+    )(*(pltpu.with_memory_space_constraint(a, pltpu.HBM) for a in (feat, cot)))
 
 
 def pack_body(feat, cot, flat, edge, both, out, fs, cs):
@@ -133,57 +122,80 @@
     )(feat, cot, flat, edge)
 
 
-def turn_body(cot, w, rows, wt, cs, wk):
-    fine_rows(cot, cs)
-    half_rows(cs, core_index(), rows)
-    turned_weights(w, wk, wt)
-
-
-def turn(cot, w):
+def turn_body(cot, cot_o, w_o, w_hbm, rows, wt, w, cs, wk, sem):
+    load = pltpu.make_async_copy(w_hbm, w, sem)
+    load.start()
+    for k, x in enumerate((cot, cot_o)):
+        fine_rows(x, cs)
+        turned_rows(cs, rows.at[k])
+    turned_weights(w_o, wk, wt.at[1])
+    load.wait()
+    turned_weights(w, wk, wt.at[0])
+
+
+def turn(cot, cot_o, w_o, w):
     return call(
         turn_body,
-        (s((4, 72, 128), F32), s((256, 512))),
-        [pltpu.VMEM((512, 128), F32), pltpu.VMEM((512, 256), BF)],
+        (s((2, 4, 128, 128), F32), s((2, 256, 512)), s((4, 4, 4, 8, 256))),
+        [pltpu.VMEM((512, 128), F32), pltpu.VMEM((512, 256), BF), pltpu.SemaphoreType.DMA],
         (0, 1500000),
-    )(cot, w)
-
-
-def merge_body(both, halo, halo_o, out):
-    core = core_index()
-    own, other = halo[0:32, :].astype(F32), halo_o[0:32, :].astype(F32)
-    out[0] = pick(core, own, other).astype(BF)
-    out[9] = pick(core, other, own).astype(BF)
-    for v in range(8):
-        out[v + 1] = both[v]
-
-
-def merge(both, halo, halo_o):
-    return call(merge_body, s((10, 32, 128)), [], (0, 200000))(both, halo, halo_o)
-
-
-def grad_body(wt, wt_o, rows, rows_o, halo, out, cols):
-    core = core_index()
+        in_specs=[pl.BlockSpec(memory_space=pltpu.VMEM)] * 3 + [pl.BlockSpec(memory_space=pltpu.HBM)],
+    )(cot, cot_o, w_o, pltpu.with_memory_space_constraint(w, pltpu.HBM))
+
+
+def place():
+    me = lax.axis_index("chan")
+    core = lax.rem(me, 2)
+    return lax.rem(lax.div(me, 2), 4), lax.div(me, 8), core
+
+
+def either(core, zero, one):
+    return zero + core * (one - zero)
+
+
+def grad_body(wt, rows, halo, halo_o, both, far, side_y, side, away, kept, cols, chosen):
+    x, row, core = place()
+    chip = lambda px, py: pl.multiple_of((py * 4 + px) * 32, 32)
+    near = lax.rem(x + 1 + 2 * core, 4)
+    starts = (
+        chip(lax.rem(x + 2, 4), either(core, row, 1 - row)),
+        chip(near, 1 - row),
+        chip(near, row),
+    )
+    for k in range(2):
+        for n, start in enumerate(starts):
+            chosen[k, n * 32 : (n + 1) * 32, :] = wt[k, pl.ds(start, 32), :]
+        for n, py in ((6, 1 - row), (7, row)):
+            start = pl.multiple_of(chip(x, py) + core * 16, 16)
+            chosen[k, n * 16 : (n + 1) * 16, :] = wt[k, pl.ds(start, 16), :]
+
+    top = [pick(core, halo[...].astype(F32), halo_o[...].astype(F32))]
+    low = [pick(core, halo_o[...].astype(F32), halo[...].astype(F32))]
+    for out in (far, side_y, side, away):
+        out[0] = top[0][:32].astype(BF)
+        out[9] = low[0][:32].astype(BF)
+        for v in range(8):
+            out[v + 1] = both[v]
+
     i = lax.broadcasted_iota(jnp.int32, (256, 512), 0)
     j = lax.broadcasted_iota(jnp.int32, (256, 512), 1)
     want = 2 * (j & 63) + (j >> 7) - 1
     same = (i >> 7) == ((j >> 6) & 1)
     select = jnp.where(((i & 127) == want) & same, 1.0, 0.0).astype(BF)
-    zero = jnp.zeros((80, 128), BF)
-    for k, body in enumerate((rows, rows_o)):
+    zero = jnp.zeros((144, 128), BF)
+    for k in range(2):
         plane = []
         for a in range(4):
-            at = 32 + (k * 4 + a) * 8
-            edge = halo[at : at + 8, :].astype(F32)
-            whole = pick(
-                core, jnp.concatenate([edge, body[a]], axis=0), jnp.concatenate([body[a], edge], axis=0)
-            )
+            mine_at, theirs_at = 32 + (k * 4 + a) * 8, 32 + ((1 - k) * 4 + a) * 8
+            own, other = halo[mine_at : mine_at + 8, :].astype(F32), halo_o[theirs_at : theirs_at + 8, :].astype(F32)
+            whole = jnp.concatenate([pick(core, own, other), rows[k, a], pick(core, other, own)], axis=0)
             plane.append(whole.astype(BF))
         for p in range(4):
-            low = plane[p - 1] if p > 0 else zero
-            high = plane[p + 1] if p < 3 else zero
-            cols[k, p] = dot(jnp.concatenate([low, high], axis=1), select).astype(BF)
-    for pair in range(2):
-        sides = []
+            before = plane[p - 1] if p > 0 else zero
+            after = plane[p + 1] if p < 3 else zero
+            cols[k, p] = dot(jnp.concatenate([before, after], axis=1), select).astype(BF)
+    for pair in range(4):
+        total = None
         for k in range(2):
             halves = []
             for v in (2 * pair, 2 * pair + 1):
@@ -191,46 +203,55 @@
                     cols[k, p, 16 * v : 16 * v + 32, r * 128 : (r + 1) * 128] for p in range(4) for r in range(4)
                 ]
                 halves.append(jnp.concatenate(parts, axis=0))
-            sides.append(jnp.concatenate(halves, axis=1))
-        out[:, pair * 256 : (pair + 1) * 256] = dot(wt[...], sides[0]) + dot(wt_o[...], sides[1])
-
-
-def grad(wt, wt_o, rows, rows_o, halo):
+            part = dot(chosen[k], jnp.concatenate(halves, axis=1))
+            total = part if total is None else total + part
+        high = total.astype(BF)
+        rest = (total - high.astype(F32)).astype(BF)
+        for half in range(2):
+            v, lanes = 2 * pair + half, slice(half * 128, (half + 1) * 128)
+            for n, out in enumerate((far, side_y, side)):
+                out[10 + v] = high[n * 32 : (n + 1) * 32, lanes]
+                out[18 + v] = rest[n * 32 : (n + 1) * 32, lanes]
+            away[10 + v, 0:16, :] = high[96:112, lanes]
+            away[10 + v, 16:32, :] = rest[96:112, lanes]
+            kept[v] = total[112:128, lanes]
+
+
+def grad(wt, rows, halo, halo_o, both):
+    whole = s((26, 32, 128))
     return call(
         grad_body,
-        s((256, 512), F32),
-        [pltpu.VMEM((2, 4, 80, 512), BF)],
-        (500000000, 1400000),
-    )(wt, wt_o, rows, rows_o, halo)
-
-
-def total_body(parts, out, rows):
-    for half in range(2):
-        acc = parts[half]
-        for chip in range(1, 8):
-            acc = acc + parts[2 * chip + half]
-        for k in range(4):
-            v = 4 * half + k
-            for u in range(2):
-                rows[pl.ds(u * 8 + v, 16, stride=16), :] = acc[:, k * 128 + u * 64 : k * 128 + (u + 1) * 64]
+        (whole, whole, whole, s((18, 32, 128)), s((8, 16, 128), F32)),
+        [pltpu.VMEM((2, 4, 144, 512), BF), pltpu.VMEM((2, 128, 512), BF)],
+        (500000000, 2500000),
+    )(wt, rows, halo, halo_o, both)
+
+
+def total_body(kept, away, *refs):
+    arrived, (out, rows) = refs[:6], refs[6:]
+    mine = pl.ds(pl.multiple_of(core_index() * 16, 16), 16)
+    for v in range(8):
+        acc = kept[v] + (away[10 + v, 0:16, :].astype(F32) + away[10 + v, 16:32, :].astype(F32))
+        for ref in arrived:
+            acc = acc + (ref[10 + v, mine, :].astype(F32) + ref[18 + v, mine, :].astype(F32))
+        for u in range(2):
+            rows[pl.ds(u * 8 + v, 16, stride=16), :] = acc[:, u * 64 : (u + 1) * 64]
     for ch in range(16):
         for u in range(2):
             out[ch, u] = rows[pl.ds(ch * 16 + u * 8, 8), :].astype(BF)
 
 
-def total(parts):
-    return call(total_body, s((16, 2, 8, 64)), [pltpu.VMEM((256, 64), F32)], (200000, 600000))(parts)
+def total(kept, away, *arrived):
+    return call(total_body, s((16, 2, 8, 64)), [pltpu.VMEM((256, 64), F32)], (200000, 600000))(kept, away, *arrived)
 
 
 def up_body(weights, own, side, side_y, far, away, side_o, side_y_o, far_o, out, f, y, fine):
-    me = lax.axis_index("chan")
-    core = lax.rem(me, 2)
-    x, row = lax.rem(lax.div(me, 2), 4), lax.div(me, 8)
+    x, row, core = place()
     near = lax.rem(x + 3 + 2 * core, 4)
     near_o = lax.rem(x + 5 - 2 * core, 4)
     across = lax.rem(x + 2, 4)
     flip = 1 - row
-    far_row = row + core - 2 * row * core
+    far_row = either(core, row, flip)
     places = (
         (own, x, row),
         (away, x, flip),
@@ -316,21 +337,20 @@
 
     w_own = jnp.transpose(weights, (0, 1, 2, 4, 3))
     cot_other, feat_other, w_other = send(cotangent, swap), send(features, swap), send(w_own, swap)
-    flat, edge, rows, wt, w_near = mine(features, cotangent, w_own)
+    flat, edge, cot = mine(features, cotangent)
     cot_other, feat_other, w_other, flat = lax.optimization_barrier((cot_other, feat_other, w_other, flat))
     both, edges = pack(feat_other, cot_other, flat, edge)
     halo = lax.ppermute(edges, ("chan", "space"), cross)
-    rows_other, wt_other = turn(cot_other, w_other)
     halo_other = send(halo, swap)
-
-    partial = grad(wt, wt_other, rows, rows_other, halo)
-    chip = merge(both, halo, halo_other)
-    side, away = send(chip, beside), send(chip, over_y)
-    pieces = lax.all_to_all(partial.reshape(16, 16, 512), "chan", 0, 0, tiled=True)
-    side_y, far = send(chip, beside_y), send(chip, over)
-    side_o, side_y_o, far_o = send(side, swap), send(side_y, swap), send(far, swap)
-    decoded = upsample(w_near.reshape(512, 256), chip, side, side_y, far, away, side_o, side_y_o, far_o)
-    return decoded, total(pieces)
+    rows, wt, w_near = turn(cot, cot_other, w_other, w_own)
+    far, side_y, side, away, kept = grad(wt, rows, halo, halo_other, both)
+    own = away
+
+    far, side_y = send(far, over), send(side_y, beside_y)
+    side, away = send(side, beside), send(away, over_y)
+    far_o, side_y_o, side_o = send(far, swap), send(side_y, swap), send(side, swap)
+    decoded = upsample(w_near.reshape(512, 256), own, side, side_y, far, away, side_o, side_y_o, far_o)
+    return decoded, total(kept, away, side, side_y, far, side_o, side_y_o, far_o)
 
 
 def solution(mesh):

time: 40.1 us -> 39.3 us (0.980)
  the two profiles are of different devices: /device:TPU:25 before, /device:TPU:24 now
where the time goes in v3:
time: 39.3 us; the launch traced here: 39.1 us
  waiting for transfers between devices  23.4 us (60%)
  starting transfers between devices  9.33 us (24%)
  Pallas kernels  5.69 us (14%)
  between operations  0.69 us (2%)
    ppermute x11, waiting for transfers between devices, local(): send = lambda a, pairs: lax.ppermute(a, 'chan', pairs)  17 us
    ppermute x1, waiting for transfers between devices, local(): halo = lax.ppermute(edges, ('chan', 'space'), cross)  6.4 us
    ppermute x11, starting transfers between devices, local(): send = lambda a, pairs: lax.ppermute(a, 'chan', pairs)  5.51 us
    ppermute x1, starting transfers between devices, local(): halo = lax.ppermute(edges, ('chan', 'space'), cross)  3.83 us
    pallas_call x1, Pallas kernels, upsample(): call(up_body, s((8, 4, 16, 128)), [pltpu.VMEM((10, 256, 128), BF), pltpu....  1.74 us
    pallas_call x1, Pallas kernels, turn(): call(turn_body, (s((2, 4, 128, 128), F32), s((2, 256, 512)), s((4, 4, 4,...  1.08 us
    pallas_call x1, Pallas kernels, grad(): call(grad_body, (whole, whole, whole, s((18, 32, 128)), s((8, 16, 128), F...  1 us
    pallas_call x1, Pallas kernels, mine(): call(mine_body, (s((8, 16, 128)), s((48, 128)), s((8, 4, 16, 128))), [plt...  1 us
  transfers between devices with their start and end apart: 12, of which 6 were waited for; matrix products, arithmetic and copies ran while one was open for 0% of the time, Pallas kernels for 5%

profile of v3, /device:TPU:24, one launch (start us, length us, event | category | flops | bytes accessed | tf_op | source)
XLA Modules:
  0.0 39.1 jit_solution(14514634528323836197)
XLA Ops:
  0.6 0.1 collective-permute-start.2
  0.7 0.5 %collective-permute-start = (bf16[8,4,16,128]{3,2,1,0:T(8,128)(2,1)}, bf16[8,4,16,128]{3,2,1,0:T(8,128)(2,1)S(1)}, u32[]{:S(2)}, u32[]{:S(2)}) collective-permute-start(bf16[8,4,16,128]{3,2,1,0:T(8,128)(2,1)} %cot_hbm.1), channel_id=1, source_target_pairs={{0,16},{16,0},{32,48},{48,32},{64,80},{80,64},{96,112},{112,96},{1... | collective-permute-start | bytes 393224 | tf_op jit(solution)/shard_map/ppermute | solution.py:336
  1.2 0.1 collective-permute-start.1
  1.3 1.0 %shard_map.50 = (bf16[8,16,128]{2,1,0:T(8,128)(2,1)S(1)}, bf16[48,128]{1,0:T(8,128)(2,1)S(1)}, bf16[8,4,16,128]{3,2,1,0:T(8,128)(2,1)S(1)}) custom-call(bf16[16,2,8,64]{3,2,1,0:T(8,128)(2,1)} %feat_hbm.1, bf16[8,4,16,128]{3,2,1,0:T(8,128)(2,1)} %cot_hbm.1), custom_call_target="tpu_custom_call" | custom-call | bytes 1000000 | tf_op jit(solution)/shard_map/pallas_call | solution.py:90
  2.3 0.4 %collective-permute-done.1.feat = bf16[16,2,8,64]{3,2,1,0:T(8,128)(2,1)S(1)} collective-permute-done((bf16[16,2,8,64]{3,2,1,0:T(8,128)(2,1)}, bf16[16,2,8,64]{3,2,1,0:T(8,128)(2,1)S(1)}, u32[]{:S(2)}, u32[]{:S(2)}) %collective-permute-start.1) | collective-permute-done | bytes 32800 | tf_op jit(solution)/shard_map/ppermute | solution.py:336
  2.7 0.0 collective-permute-done.cot_o.cot
  2.7 0.0 collective-permute-done.2.w_o
  2.8 0.1 shard_map.52
  2.9 3.8 %collective-permute-start.3 = (bf16[96,128]{1,0:T(8,128)(2,1)S(1)}, bf16[96,128]{1,0:T(8,128)(2,1)S(1)}, u32[]{:S(2)}, u32[]{:S(2)}) collective-permute-start(bf16[96,128]{1,0:T(8,128)(2,1)S(1)} %get-tuple-element.29), channel_id=1, source_target_pairs={{0,1},{1,2},{2,3},{3,4},{4,5},{5,6},{6,7},{7,8},{8,9},{9,10},{10,1... | collective-permute-start | bytes 73736 | tf_op jit(solution)/shard_map/ppermute | solution.py:343
  6.7 6.4 %collective-permute-done.3.halo = bf16[96,128]{1,0:T(8,128)(2,1)S(1)} collective-permute-done((bf16[96,128]{1,0:T(8,128)(2,1)S(1)}, bf16[96,128]{1,0:T(8,128)(2,1)S(1)}, u32[]{:S(2)}, u32[]{:S(2)}) %collective-permute-start.3) | collective-permute-done | bytes 24608 | tf_op jit(solution)/shard_map/ppermute | solution.py:343
  13.1 0.0 collective-permute-start.4
  13.1 1.1 %shard_map.51 = (f32[2,4,128,128]{3,2,1,0:T(8,128)S(1)}, bf16[2,256,512]{2,1,0:T(8,128)(2,1)S(1)}, bf16[4,4,4,8,256]{4,3,2,1,0:T(8,128)(2,1)S(1)}) custom-call(bf16[8,4,16,128]{3,2,1,0:T(8,128)(2,1)S(1)} %get-tuple-element.19.cot, bf16[8,4,16,128]{3,2,1,0:T(8,128)(2,1)S(1)} %collective-permute-done.cot_o.cot, ...), custom_call_target="tpu_custom_call" | custom-call | bytes 1500000 | tf_op jit(solution)/shard_map/pallas_call | solution.py:137
  14.2 0.1 collective-permute-done.4.halo_o
  14.3 1.0 %shard_map.53 = (bf16[26,32,128]{2,1,0:T(8,128)(2,1)S(1)}, bf16[26,32,128]{2,1,0:T(8,128)(2,1)S(1)}, bf16[26,32,128]{2,1,0:T(8,128)(2,1)S(1)}, bf16[18,32,128]{2,1,0:T(8,128)(2,1)S(1)}, f32[8,16,128]{2,1,0:T(8,128)S(1)}) custom-call(bf16[2,256,512]{2,1,0:T(8,128)(2,1)S(1)} %get-tuple-element.24.wt, f32[2,4,128,128]{3,2,1,0:T(8,128)S(1)} %get-tuple-element.25.rows, ...), custom_call_target="tpu_custom_call" | custom-call | flops 500000000 | bytes 2500000 | tf_op jit(solution)/shard_map/pallas_call | solution.py:222
  15.3 1.6 %collective-permute-start.5 = (bf16[26,32,128]{2,1,0:T(8,128)(2,1)S(1)}, bf16[26,32,128]{2,1,0:T(8,128)(2,1)S(1)}, u32[]{:S(2)}, u32[]{:S(2)}) collective-permute-start(bf16[26,32,128]{2,1,0:T(8,128)(2,1)S(1)} %get-tuple-element.32), channel_id=1, source_target_pairs={{0,32},{16,112},{32,64},{48,16},{64,96},{80,48},{96,0},{112,80},{1... | collective-permute-start | bytes 638984 | tf_op jit(solution)/shard_map/ppermute | solution.py:336
  16.9 0.8 %collective-permute-start.6 = (bf16[26,32,128]{2,1,0:T(8,128)(2,1)S(1)}, bf16[26,32,128]{2,1,0:T(8,128)(2,1)S(1)}, u32[]{:S(2)}, u32[]{:S(2)}) collective-permute-start(bf16[26,32,128]{2,1,0:T(8,128)(2,1)S(1)} %get-tuple-element.33), channel_id=1, source_target_pairs={{0,160},{16,240},{32,192},{48,144},{64,224},{80,176},{96,128},{112... | collective-permute-start | bytes 638984 | tf_op jit(solution)/shard_map/ppermute | solution.py:336
  17.6 2.0 %collective-permute-start.7 = (bf16[26,32,128]{2,1,0:T(8,128)(2,1)S(1)}, bf16[26,32,128]{2,1,0:T(8,128)(2,1)S(1)}, u32[]{:S(2)}, u32[]{:S(2)}) collective-permute-start(bf16[26,32,128]{2,1,0:T(8,128)(2,1)S(1)} %get-tuple-element.34), channel_id=1, source_target_pairs={{0,64},{16,208},{32,96},{48,240},{64,0},{80,144},{96,32},{112,176}... | collective-permute-start | bytes 638984 | tf_op jit(solution)/shard_map/ppermute | solution.py:336
  19.6 2.8 %collective-permute-done.5.side.refs_0_ = bf16[26,32,128]{2,1,0:T(8,128)(2,1)S(1)} collective-permute-done((bf16[26,32,128]{2,1,0:T(8,128)(2,1)S(1)}, bf16[26,32,128]{2,1,0:T(8,128)(2,1)S(1)}, u32[]{:S(2)}, u32[]{:S(2)}) %collective-permute-start.5) | collective-permute-done | bytes 213024 | tf_op jit(solution)/shard_map/ppermute | solution.py:336
  22.4 0.0 collective-permute-start.9
  22.4 7.9 %collective-permute-done.6.side_y.refs_1_ = bf16[26,32,128]{2,1,0:T(8,128)(2,1)S(1)} collective-permute-done((bf16[26,32,128]{2,1,0:T(8,128)(2,1)S(1)}, bf16[26,32,128]{2,1,0:T(8,128)(2,1)S(1)}, u32[]{:S(2)}, u32[]{:S(2)}) %collective-permute-start.6) | collective-permute-done | bytes 213024 | tf_op jit(solution)/shard_map/ppermute | solution.py:336
  30.3 0.5 %collective-permute-start.11 = (bf16[26,32,128]{2,1,0:T(8,128)(2,1)S(1)}, bf16[26,32,128]{2,1,0:T(8,128)(2,1)S(1)}, u32[]{:S(2)}, u32[]{:S(2)}) collective-permute-start(bf16[26,32,128]{2,1,0:T(8,128)(2,1)S(1)} %collective-permute-done.7.far.refs_2_), channel_id=1, source_target_pairs={{0,16},{16,0},{32,48},{48,32},{64,80},{80,64},{96,112},{112,96},{1... | collective-permute-start | bytes 638984 | tf_op jit(solution)/shard_map/ppermute | solution.py:336
  30.8 5.8 %collective-permute-done.8.away = bf16[18,32,128]{2,1,0:T(8,128)(2,1)S(1)} collective-permute-done((bf16[18,32,128]{2,1,0:T(8,128)(2,1)S(1)}, bf16[18,32,128]{2,1,0:T(8,128)(2,1)S(1)}, u32[]{:S(2)}, u32[]{:S(2)}) %collective-permute-start.8) | collective-permute-done | bytes 147488 | tf_op jit(solution)/shard_map/ppermute | solution.py:336
  36.6 1.7 %shard_map.54 = bf16[8,4,16,128]{3,2,1,0:T(8,128)(2,1)} custom-call(bf16[512,256]{1,0:T(8,128)(2,1)S(1)} %bitcast.2, bf16[18,32,128]{2,1,0:T(8,128)(2,1)S(1)} %get-tuple-element.31.own, bf16[26,32,128]{2,1,0:T(8,128)(2,1)S(1)} %collective-permute-done.5.side.refs_0_, bf16[26,32,128]{2,1,0:T(8,128)(2,1)S(1)} %collective-permute-done.6.side_y.refs_1_, ...), custom_call_target="tpu_custom_call" | custom-call | flops 400000000 | bytes 1100000 | tf_op jit(solution)/shard_map/pallas_call | solution.py:311
  38.3 0.8 %shard_map.55 = bf16[16,2,8,64]{3,2,1,0:T(8,128)(2,1)} custom-call(f32[8,16,128]{2,1,0:T(8,128)S(1)} %get-tuple-element.35.kept, bf16[18,32,128]{2,1,0:T(8,128)(2,1)S(1)} %collective-permute-done.8.away, bf16[26,32,128]{2,1,0:T(8,128)(2,1)S(1)} %collective-permute-done.5.side.refs_0_, bf16[26,32,128]{2,1,0:T(8,128)(2,1)S(1)} %collective-permute-done.6.side_y.refs_1_, ...), custom_call_target="tpu_custom_call" | custom-call | flops 200000 | bytes 600000 | tf_op jit(solution)/shard_map/pallas_call | solution.py:245
  (6 shorter events, 0.0 us)
Async XLA Ops:
  0.6 2.1 %collective-permute-start.2 = (bf16[4,4,4,8,256]{4,3,2,1,0:T(8,128)(2,1)}, bf16[4,4,4,8,256]{4,3,2,1,0:T(8,128)(2,1)S(1)}, u32[]{:S(2)}, u32[]{:S(2)}) collective-permute-start(bf16[4,4,4,8,256]{4,3,2,1,0:T(8,128)(2,1)} %bitcast.3), channel_id=1, source_target_pairs={{0,16},{16,0},{32,48},{48,32},{64,80},{80,64},{96,112},{112,96},{1... | collective-permute-start | bytes 786440 | tf_op jit(solution)/shard_map/ppermute | solution.py:336
  0.7 2.0 %collective-permute-start = (bf16[8,4,16,128]{3,2,1,0:T(8,128)(2,1)}, bf16[8,4,16,128]{3,2,1,0:T(8,128)(2,1)S(1)}, u32[]{:S(2)}, u32[]{:S(2)}) collective-permute-start(bf16[8,4,16,128]{3,2,1,0:T(8,128)(2,1)} %cot_hbm.1), channel_id=1, source_target_pairs={{0,16},{16,0},{32,48},{48,32},{64,80},{80,64},{96,112},{112,96},{1... | collective-permute-start | bytes 393224 | tf_op jit(solution)/shard_map/ppermute | solution.py:336
  1.2 1.5 %collective-permute-start.1 = (bf16[16,2,8,64]{3,2,1,0:T(8,128)(2,1)}, bf16[16,2,8,64]{3,2,1,0:T(8,128)(2,1)S(1)}, u32[]{:S(2)}, u32[]{:S(2)}) collective-permute-start(bf16[16,2,8,64]{3,2,1,0:T(8,128)(2,1)} %feat_hbm.1), channel_id=1, source_target_pairs={{0,16},{16,0},{32,48},{48,32},{64,80},{80,64},{96,112},{112,96},{1... | collective-permute-start | bytes 98312 | tf_op jit(solution)/shard_map/ppermute | solution.py:336
  2.9 10.2 %collective-permute-start.3 = (bf16[96,128]{1,0:T(8,128)(2,1)S(1)}, bf16[96,128]{1,0:T(8,128)(2,1)S(1)}, u32[]{:S(2)}, u32[]{:S(2)}) collective-permute-start(bf16[96,128]{1,0:T(8,128)(2,1)S(1)} %get-tuple-element.29), channel_id=1, source_target_pairs={{0,1},{1,2},{2,3},{3,4},{4,5},{5,6},{6,7},{7,8},{8,9},{9,10},{10,1... | collective-permute-start | bytes 73736 | tf_op jit(solution)/shard_map/ppermute | solution.py:343
  13.1 1.2 %collective-permute-start.4 = (bf16[96,128]{1,0:T(8,128)(2,1)S(1)}, bf16[96,128]{1,0:T(8,128)(2,1)S(1)}, u32[]{:S(2)}, u32[]{:S(2)}) collective-permute-start(bf16[96,128]{1,0:T(8,128)(2,1)S(1)} %collective-permute-done.3.halo), channel_id=1, source_target_pairs={{0,16},{16,0},{32,48},{48,32},{64,80},{80,64},{96,112},{112,96},{1... | collective-permute-start | bytes 73736 | tf_op jit(solution)/shard_map/ppermute | solution.py:336
  15.3 7.1 %collective-permute-start.5 = (bf16[26,32,128]{2,1,0:T(8,128)(2,1)S(1)}, bf16[26,32,128]{2,1,0:T(8,128)(2,1)S(1)}, u32[]{:S(2)}, u32[]{:S(2)}) collective-permute-start(bf16[26,32,128]{2,1,0:T(8,128)(2,1)S(1)} %get-tuple-element.32), channel_id=1, source_target_pairs={{0,32},{16,112},{32,64},{48,16},{64,96},{80,48},{96,0},{112,80},{1... | collective-permute-start | bytes 638984 | tf_op jit(solution)/shard_map/ppermute | solution.py:336
  16.9 13.5 %collective-permute-start.6 = (bf16[26,32,128]{2,1,0:T(8,128)(2,1)S(1)}, bf16[26,32,128]{2,1,0:T(8,128)(2,1)S(1)}, u32[]{:S(2)}, u32[]{:S(2)}) collective-permute-start(bf16[26,32,128]{2,1,0:T(8,128)(2,1)S(1)} %get-tuple-element.33), channel_id=1, source_target_pairs={{0,160},{16,240},{32,192},{48,144},{64,224},{80,176},{96,128},{112... | collective-permute-start | bytes 638984 | tf_op jit(solution)/shard_map/ppermute | solution.py:336
  17.6 12.7 %collective-permute-start.7 = (bf16[26,32,128]{2,1,0:T(8,128)(2,1)S(1)}, bf16[26,32,128]{2,1,0:T(8,128)(2,1)S(1)}, u32[]{:S(2)}, u32[]{:S(2)}) collective-permute-start(bf16[26,32,128]{2,1,0:T(8,128)(2,1)S(1)} %get-tuple-element.34), channel_id=1, source_target_pairs={{0,64},{16,208},{32,96},{48,240},{64,0},{80,144},{96,32},{112,176}... | collective-permute-start | bytes 638984 | tf_op jit(solution)/shard_map/ppermute | solution.py:336
  22.4 14.2 %collective-permute-start.9 = (bf16[26,32,128]{2,1,0:T(8,128)(2,1)S(1)}, bf16[26,32,128]{2,1,0:T(8,128)(2,1)S(1)}, u32[]{:S(2)}, u32[]{:S(2)}) collective-permute-start(bf16[26,32,128]{2,1,0:T(8,128)(2,1)S(1)} %collective-permute-done.5.side.refs_0_), channel_id=1, source_target_pairs={{0,16},{16,0},{32,48},{48,32},{64,80},{80,64},{96,112},{112,96},{1... | collective-permute-start | bytes 638984 | tf_op jit(solution)/shard_map/ppermute | solution.py:336
  30.3 6.3 %collective-permute-start.10 = (bf16[26,32,128]{2,1,0:T(8,128)(2,1)S(1)}, bf16[26,32,128]{2,1,0:T(8,128)(2,1)S(1)}, u32[]{:S(2)}, u32[]{:S(2)}) collective-permute-start(bf16[26,32,128]{2,1,0:T(8,128)(2,1)S(1)} %collective-permute-done.6.side_y.refs_1_), channel_id=1, source_target_pairs={{0,16},{16,0},{32,48},{48,32},{64,80},{80,64},{96,112},{112,96},{1... | collective-permute-start | bytes 638984 | tf_op jit(solution)/shard_map/ppermute | solution.py:336
  30.3 6.3 %collective-permute-start.11 = (bf16[26,32,128]{2,1,0:T(8,128)(2,1)S(1)}, bf16[26,32,128]{2,1,0:T(8,128)(2,1)S(1)}, u32[]{:S(2)}, u32[]{:S(2)}) collective-permute-start(bf16[26,32,128]{2,1,0:T(8,128)(2,1)S(1)} %collective-permute-done.7.far.refs_2_), channel_id=1, source_target_pairs={{0,16},{16,0},{32,48},{48,32},{64,80},{80,64},{96,112},{112,96},{1... | collective-permute-start | bytes 638984 | tf_op jit(solution)/shard_map/ppermute | solution.py:336
  30.8 5.8 %collective-permute-start.8 = (bf16[18,32,128]{2,1,0:T(8,128)(2,1)S(1)}, bf16[18,32,128]{2,1,0:T(8,128)(2,1)S(1)}, u32[]{:S(2)}, u32[]{:S(2)}) collective-permute-start(bf16[18,32,128]{2,1,0:T(8,128)(2,1)S(1)} %get-tuple-element.31.own), channel_id=1, source_target_pairs={{0,128},{16,144},{32,160},{48,176},{64,192},{80,208},{96,224},{112... | collective-permute-start | bytes 442376 | tf_op jit(solution)/shard_map/ppermute | solution.py:336

commit v4 on v3

v4 whole, which is shorter than its diff:
```python
import jax
import jax.numpy as jnp
from jax import lax
from jax.experimental import pallas as pl
from jax.experimental.pallas import tpu as pltpu
from jax.sharding import PartitionSpec as P

BF = jnp.bfloat16
F32 = jnp.float32


def s(shape, kind=BF):
    return jax.ShapeDtypeStruct(shape, kind)


def call(body, outs, scratch, cost, limit=12 * 1024, **kw):
    return pl.pallas_call(
        body,
        out_shape=outs,
        scratch_shapes=scratch,
        cost_estimate=pl.CostEstimate(flops=cost[0], bytes_accessed=cost[1], transcendentals=0),
        compiler_params=pltpu.CompilerParams(vmem_limit_bytes=limit * 1024),
        **kw,
    )


def dot(a, b, dims=((1,), (0,))):
    return lax.dot_general(a, b, (dims, ((), ())), preferred_element_type=F32)


def core_index():
    return lax.rem(lax.axis_index("chan"), 2)


def pick(core, zero, one):
    return jnp.where(jnp.full(zero.shape, core, jnp.int32) == 0, zero, one)


def cell_rows(feat, fs, rows):
    for ch in range(16):
        for u in range(2):
            fs[pl.ds(ch * 16 + u * 8, 8), :] = feat[ch, u].astype(F32)
    return [
        jnp.concatenate([fs[pl.ds(v, 16, stride=16), :], fs[pl.ds(8 + v, 16, stride=16), :]], axis=1)
        for v in rows
    ]


def fine_rows(cot, cs):
    for o in range(8):
        for a in range(4):
            cs[pl.ds((o * 4 + a) * 16, 16), :] = cot[o, a].astype(F32)


def edge_rows(feat, cot, fs, cs):
    core = core_index()
    first, last = cell_rows(feat, fs, (0, 7))
    fine_rows(cot, cs)
    turned = [
        pick(core, cs[pl.ds(a * 16 + 15, 8, stride=64), :], cs[pl.ds(a * 16, 8, stride=64), :]) for a in range(4)
    ]
    return pick(core, last, first), turned


def turned_weights(w, wk, out):
    for p in range(4):
        for r in range(4):
            taps = [w[p, q, r].astype(F32) for q in range(4)]
            wk[pl.ds((p * 4 + r) * 32, 32), :] = jnp.concatenate(taps, axis=0).astype(BF)
    out[...] = wk[...].T


def selection():
    i = lax.broadcasted_iota(jnp.int32, (256, 512), 0)
    j = lax.broadcasted_iota(jnp.int32, (256, 512), 1)
    want = 2 * (j & 63) + (j >> 7) - 1
    same = (i >> 7) == ((j >> 6) & 1)
    return jnp.where(((i & 127) == want) & same, 1.0, 0.0).astype(BF)


def spreading():
    i = lax.broadcasted_iota(jnp.int32, (256, 256), 0)
    j = lax.broadcasted_iota(jnp.int32, (256, 256), 1)
    return jnp.where(((j >> 7) == ((i >> 6) & 1)) & ((j & 127) == 2 * (i & 63) + (i >> 7)), 1.0, 0.0).astype(BF)


def mine_body(feat_hbm, cot_hbm, edge, feat, cot, select, spread, fs, cs, sems):
    loads = [pltpu.make_async_copy(feat_hbm, feat, sems.at[0]), pltpu.make_async_copy(cot_hbm, cot, sems.at[1])]
    for load in loads:
        load.start()
    select[...] = selection()
    spread[...] = spreading()
    for load in loads:
        load.wait()
    row, turned = edge_rows(feat, cot, fs, cs)
    edge[...] = jnp.concatenate([row] + turned, axis=0)


def mine(feat, cot):
    return call(
        mine_body,
        (s((48, 128), F32), s((16, 2, 8, 64)), s((8, 4, 16, 128)), s((256, 512)), s((256, 256))),
        [pltpu.VMEM((256, 64), F32), pltpu.VMEM((512, 128), F32), pltpu.SemaphoreType.DMA((2,))],
        (0, 1000000),
        in_specs=[pl.BlockSpec(memory_space=pltpu.HBM)] * 2,
    )(*(pltpu.with_memory_space_constraint(a, pltpu.HBM) for a in (feat, cot)))


def pack_body(feat, cot, edge, out, fs, cs):
    core = core_index()
    row, turned = edge_rows(feat, cot, fs, cs)
    own = edge[0:16, :]
    out[...] = jnp.concatenate([pick(core, own, row), pick(core, row, own), edge[16:48, :]] + turned, axis=0).astype(BF)


def pack(feat, cot, edge):
    return call(
        pack_body,
        s((96, 128)),
        [pltpu.VMEM((256, 64), F32), pltpu.VMEM((512, 128), F32)],
        (0, 600000),
    )(feat, cot, edge)


def place():
    me = lax.axis_index("chan")
    core = lax.rem(me, 2)
    return lax.rem(lax.div(me, 2), 4), lax.div(me, 8), core


def either(core, zero, one):
    return zero + core * (one - zero)


def columns(planes, p, select):
    zero = jnp.zeros_like(planes[0])
    before = planes[p - 1] if p > 0 else zero
    after = planes[p + 1] if p < 3 else zero
    return dot(jnp.concatenate([before, after], axis=1), select).astype(BF)


def ready_body(feat, feat_o, cot, cot_o, w_o, select_ref, w_hbm, both, chosen, cols, ends, w, fs, cs, wk, wt, sem):
    load = pltpu.make_async_copy(w_hbm, w, sem)
    load.start()
    x, row, core = place()
    own, other = cell_rows(feat, fs, range(8)), cell_rows(feat_o, fs, range(8))
    for v in range(8):
        both[v] = jnp.concatenate([pick(core, own[v], other[v]), pick(core, other[v], own[v])], axis=0).astype(BF)
    select = select_ref[...]
    empty = jnp.zeros((8, 128), F32)
    for k, ref in enumerate((cot, cot_o)):
        fine_rows(ref, cs)
        planes = []
        for a in range(4):
            rows = [cs[pl.ds(a * 16 + n, 8, stride=64), :] for n in range(16)]
            ends[k, a, 0:8, :], ends[k, a, 8:16, :] = rows[0], rows[15]
            planes.append(jnp.concatenate([empty] + rows + [empty], axis=0).astype(BF))
        for p in range(4):
            cols[k, p] = columns(planes, p, select)
    chip = lambda px, py: pl.multiple_of((py * 4 + px) * 32, 32)
    near = lax.rem(x + 1 + 2 * core, 4)
    starts = (
        chip(lax.rem(x + 2, 4), either(core, row, 1 - row)),
        chip(near, 1 - row),
        chip(near, row),
    )
    for k, ref in ((1, w_o), (0, w)):
        if k == 0:
            load.wait()
        turned_weights(ref, wk, wt)
        for n, start in enumerate(starts):
            chosen[k, n * 32 : (n + 1) * 32, :] = wt[pl.ds(start, 32), :]
        for n, py in ((6, 1 - row), (7, row)):
            start = pl.multiple_of(chip(x, py) + core * 16, 16)
            chosen[k, n * 16 : (n + 1) * 16, :] = wt[pl.ds(start, 16), :]


def ready(feat, feat_o, cot, cot_o, w_o, select, w):
    return call(
        ready_body,
        (
            s((8, 32, 128)),
            s((2, 128, 512)),
            s((2, 4, 144, 512)),
            s((2, 4, 16, 128), F32),
            s((4, 4, 4, 8, 256)),
        ),
        [
            pltpu.VMEM((256, 64), F32),
            pltpu.VMEM((512, 128), F32),
            pltpu.VMEM((512, 256), BF),
            pltpu.VMEM((256, 512), BF),
            pltpu.SemaphoreType.DMA,
        ],
        (200000000, 2500000),
        in_specs=[pl.BlockSpec(memory_space=pltpu.VMEM)] * 6 + [pl.BlockSpec(memory_space=pltpu.HBM)],
    )(feat, feat_o, cot, cot_o, w_o, select, pltpu.with_memory_space_constraint(w, pltpu.HBM))


def grad_body(chosen, cols, ends, select_ref, halo, halo_o, both, far, side_y, side, away, kept):
    core = core_index()
    up = pick(core, halo[0:32, :].astype(F32), halo_o[0:32, :].astype(F32)).astype(BF)
    down = pick(core, halo_o[0:32, :].astype(F32), halo[0:32, :].astype(F32)).astype(BF)
    for out in (far, side_y, side, away):
        out[0], out[9] = up, down
        for v in range(8):
            out[v + 1] = both[v]
    select = select_ref[...]
    tips = {}
    for k in range(2):
        planes = []
        for a in range(4):
            mine_at, theirs_at = 32 + (k * 4 + a) * 8, 32 + ((1 - k) * 4 + a) * 8
            own, other = halo[mine_at : mine_at + 8, :].astype(F32), halo_o[theirs_at : theirs_at + 8, :].astype(F32)
            pieces = [pick(core, own, other), ends[k, a], pick(core, other, own)]
            planes.append(jnp.concatenate(pieces, axis=0).astype(BF))
        for p in range(4):
            tips[k, p] = columns(planes, p, select)
    for pair in range(4):
        total = None
        for k in range(2):
            halves = []
            for v in (2 * pair, 2 * pair + 1):
                parts = []
                for p in range(4):
                    for r in range(4):
                        lanes = slice(r * 128, (r + 1) * 128)
                        if v == 0:
                            parts += [tips[k, p][0:16, lanes], cols[k, p, 16:32, lanes]]
                        elif v == 7:
                            parts += [cols[k, p, 112:128, lanes], tips[k, p][16:32, lanes]]
                        else:
                            parts.append(cols[k, p, 16 * v : 16 * v + 32, lanes])
                halves.append(jnp.concatenate(parts, axis=0))
            part = dot(chosen[k], jnp.concatenate(halves, axis=1))
            total = part if total is None else total + part
        high = total.astype(BF)
        rest = (total - high.astype(F32)).astype(BF)
        for half in range(2):
            v, lanes = 2 * pair + half, slice(half * 128, (half + 1) * 128)
            for n, out in enumerate((far, side_y, side)):
                out[10 + v] = high[n * 32 : (n + 1) * 32, lanes]
                out[18 + v] = rest[n * 32 : (n + 1) * 32, lanes]
            away[10 + v, 0:16, :] = high[96:112, lanes]
            away[10 + v, 16:32, :] = rest[96:112, lanes]
            kept[v] = total[112:128, lanes]


def grad(*args):
    whole = s((26, 32, 128))
    return call(
        grad_body,
        (whole, whole, whole, s((18, 32, 128)), s((8, 16, 128), F32)),
        [],
        (400000000, 2500000),
    )(*args)


def total_body(kept, away, *refs):
    arrived, (out, rows) = refs[:6], refs[6:]
    mine = pl.ds(pl.multiple_of(core_index() * 16, 16), 16)
    for v in range(8):
        acc = kept[v] + (away[10 + v, 0:16, :].astype(F32) + away[10 + v, 16:32, :].astype(F32))
        for ref in arrived:
            acc = acc + (ref[10 + v, mine, :].astype(F32) + ref[18 + v, mine, :].astype(F32))
        for u in range(2):
            rows[pl.ds(u * 8 + v, 16, stride=16), :] = acc[:, u * 64 : (u + 1) * 64]
    for ch in range(16):
        for u in range(2):
            out[ch, u] = rows[pl.ds(ch * 16 + u * 8, 8), :].astype(BF)


def up_body(weights, spread_ref, own, side, side_y, far, away, side_o, side_y_o, far_o, out, f, y, fine):
    x, row, core = place()
    near = lax.rem(x + 3 + 2 * core, 4)
    near_o = lax.rem(x + 5 - 2 * core, 4)
    across = lax.rem(x + 2, 4)
    flip = 1 - row
    far_row = either(core, row, flip)
    places = (
        (own, x, row),
        (away, x, flip),
        (side, near, row),
        (side_o, near_o, row),
        (side_y, near, flip),
        (side_y_o, near_o, flip),
        (far, across, far_row),
        (far_o, across, 1 - far_row),
    )
    for ref, px, py in places:
        rows = pl.ds(pl.multiple_of((py * 4 + px) * 32, 32), 32)
        for t in range(10):
            f[t, rows, :] = ref[t]
    w = weights[...]
    for t in range(5):
        y[t] = dot(w, jnp.concatenate([f[2 * t], f[2 * t + 1]], axis=1))

    def tap(p, q, r, v):
        t = v + 1
        return y[t // 2, pl.ds(((p * 4 + q) * 4 + r) * 8, 8), (t % 2) * 128 : (t % 2 + 1) * 128]

    lane = lax.broadcasted_iota(jnp.int32, (8, 128), 1)
    first_half = lane < 64
    cell = lane & 63
    spread = spread_ref[...]
    for pb in range(2):
        blocks = {0: [], 1: []}
        for n in range(8):
            pairs = ((1, n), (3, n - 1)) if pb == 0 else ((2, n), (0, n + 1))
            got = {0: [], 1: []}
            for r in range(4):
                t = [sum(tap(p, q, r, v) for q, v in pairs) for p in range(4)]
                moved = pltpu.roll(jnp.where(first_half, t[3], t[0]), 64, 1)
                got[0].append(t[1] + jnp.where(first_half, 0.0, moved))
                got[1].append(t[2] + jnp.where(first_half, moved, 0.0))
            for pa in range(2):
                t0, t1, t2, t3 = got[pa]
                even = t1 + jnp.where(cell == 0, 0.0, pltpu.roll(t3, 1, 1))
                odd = t2 + jnp.where(cell == 63, 0.0, pltpu.roll(t0, 127, 1))
                blocks[pa].append(jnp.concatenate([even, odd], axis=1))
        for pa in range(2):
            rows = dot(jnp.concatenate(blocks[pa], axis=0).astype(BF), spread)
            for n in range(8):
                for m in range(2):
                    fine[pl.ds((2 * m + pa) * 16 + 2 * n + pb, 8, stride=64), :] = rows[
                        n * 8 : (n + 1) * 8, m * 128 : (m + 1) * 128
                    ]
    for o in range(8):
        for a in range(4):
            out[o, a] = fine[pl.ds((o * 4 + a) * 16, 16), :].astype(BF)


def last_body(weights, spread, own, kept, side, side_y, far, away, side_o, side_y_o, far_o, up, grad_out, f, y, fine, rows):
    total_body(kept, away, side, side_y, far, side_o, side_y_o, far_o, grad_out, rows)
    up_body(weights, spread, own, side, side_y, far, away, side_o, side_y_o, far_o, up, f, y, fine)


def last(*args):
    return call(
        last_body,
        (s((8, 4, 16, 128)), s((16, 2, 8, 64))),
        [
            pltpu.VMEM((10, 256, 128), BF),
            pltpu.VMEM((5, 512, 256), F32),
            pltpu.VMEM((512, 128), F32),
            pltpu.VMEM((256, 64), F32),
        ],
        (400000000, 2500000),
    )(*args)


def local(features, weights, cotangent):
    tiles = lax.axis_size("space")
    chans = lax.axis_size("chan")
    at = lambda ch, sp: ch * tiles + sp
    index = lambda x, row, core: (row * 4 + x % 4) * 2 + core
    swap = [(ch, ch ^ 1) for ch in range(chans)]
    cross = []
    for ch in range(chans):
        for sp in range(tiles):
            to = sp + 1 - 2 * (ch % 2)
            if 0 <= to < tiles:
                cross.append((at(ch, sp), at(ch, to)))
    chips = [(x, row, core) for row in range(2) for x in range(4) for core in range(2)]
    beside = [(index(x, row, c), index(x + 1 - 2 * c, row, c)) for x, row, c in chips]
    beside_y = [(index(x, row, c), index(x + 1 - 2 * c, 1 - row, c)) for x, row, c in chips]
    over = [(index(x, row, c), index(x + 2, (row + c) % 2, c)) for x, row, c in chips]
    over_y = [(index(x, row, c), index(x, 1 - row, c)) for x, row, c in chips]
    send = lambda a, pairs: lax.ppermute(a, "chan", pairs)

    w_own = jnp.transpose(weights, (0, 1, 2, 4, 3))
    cot_other = send(cotangent, swap)
    feat_other = send(features, swap)
    w_other = send(w_own, swap)
    edge, feat, cot, select, spread = mine(features, cotangent)
    cot_other, feat_other, edge = lax.optimization_barrier((cot_other, feat_other, edge))
    edges = pack(feat_other, cot_other, edge)
    halo = lax.ppermute(edges, ("chan", "space"), cross)
    both, chosen, cols, ends, w_near = ready(feat, feat_other, cot, cot_other, w_other, select, w_own)
    halo_other = send(halo, swap)
    far, side_y, side, away, kept = grad(chosen, cols, ends, select, halo, halo_other, both)
    own = away

    far, side_y = send(far, over), send(side_y, beside_y)
    side, away = send(side, beside), send(away, over_y)
    far_o, side_y_o, side_o = send(far, swap), send(side_y, swap), send(side, swap)
    return last(w_near.reshape(512, 256), spread, own, kept, side, side_y, far, away, side_o, side_y_o, far_o)


def solution(mesh):
    return jax.shard_map(
        local,
        mesh=mesh,
        in_specs=(
            P("chan", None, "space", None),
            P(None, None, None, None, "chan"),
            P("chan", None, "space", None),
        ),
        out_specs=(P("chan", None, "space", None), P("chan", None, "space", None)),
        check_vma=False,
    )
```

time: 39.3 us -> 38.8 us (0.987)
    pallas_call x5 -> x4, Pallas kernels: 4.69 us -> 4.57 us  [the longest x1 1.8 us: last(): call(last_body, (s((8, 4, 16, 128)), s((16, 2, 8, 64))), [pltpu.VMEM((10,...]
  transfers between devices with their start and end apart: 12 -> 12, of which waited for: 6 -> 5; matrix products, arithmetic and copies ran while one was open for 0% -> 0% of each run, Pallas kernels for 5% -> 7%
where the time goes in v4:
time: 38.8 us; the launch traced here: 38.7 us
  waiting for transfers between devices  23.2 us (60%)
  starting transfers between devices  9.33 us (24%)
  Pallas kernels  5.45 us (14%)
  between operations  0.69 us (2%)
    ppermute x11, waiting for transfers between devices, local(): send = lambda a, pairs: lax.ppermute(a, 'chan', pairs)  16.8 us
    ppermute x1, waiting for transfers between devices, local(): halo = lax.ppermute(edges, ('chan', 'space'), cross)  6.4 us
    ppermute x11, starting transfers between devices, local(): send = lambda a, pairs: lax.ppermute(a, 'chan', pairs)  5.51 us
    ppermute x1, starting transfers between devices, local(): halo = lax.ppermute(edges, ('chan', 'space'), cross)  3.82 us
    pallas_call x1, Pallas kernels, last(): call(last_body, (s((8, 4, 16, 128)), s((16, 2, 8, 64))), [pltpu.VMEM((10,...  1.8 us
    pallas_call x1, Pallas kernels, ready(): call(ready_body, (s((8, 32, 128)), s((2, 128, 512)), s((2, 4, 144, 512)),...  1.63 us
    pallas_call x1, Pallas kernels, mine(): call(mine_body, (s((48, 128), F32), s((16, 2, 8, 64)), s((8, 4, 16, 128))...  1.05 us
    pallas_call x1, Pallas kernels, grad(): call(grad_body, (whole, whole, whole, s((18, 32, 128)), s((8, 16, 128), F...  0.88 us
  transfers between devices with their start and end apart: 12, of which 5 were waited for; matrix products, arithmetic and copies ran while one was open for 0% of the time, Pallas kernels for 7%

profile of v4, /device:TPU:24, one launch (start us, length us, event | category | flops | bytes accessed | tf_op | source)
XLA Modules:
  0.0 38.7 jit_solution(1754635273958982180)
XLA Ops:
  0.6 0.1 collective-permute-start.2
  0.7 0.5 %collective-permute-start = (bf16[8,4,16,128]{3,2,1,0:T(8,128)(2,1)}, bf16[8,4,16,128]{3,2,1,0:T(8,128)(2,1)S(1)}, u32[]{:S(2)}, u32[]{:S(2)}) collective-permute-start(bf16[8,4,16,128]{3,2,1,0:T(8,128)(2,1)} %cot_hbm.1), channel_id=1, source_target_pairs={{0,16},{16,0},{32,48},{48,32},{64,80},{80,64},{96,112},{112,96},{1... | collective-permute-start | bytes 393224 | tf_op jit(solution)/shard_map/ppermute | solution.py:369
  1.2 0.1 collective-permute-start.1
  1.3 1.0 %shard_map.50 = (f32[48,128]{1,0:T(8,128)S(1)}, bf16[16,2,8,64]{3,2,1,0:T(8,128)(2,1)S(1)}, bf16[8,4,16,128]{3,2,1,0:T(8,128)(2,1)S(1)}, bf16[256,512]{1,0:T(8,128)(2,1)S(1)}, bf16[256,256]{1,0:T(8,128)(2,1)S(1)}) custom-call(bf16[16,2,8,64]{3,2,1,0:T(8,128)(2,1)} %feat_hbm.1, bf16[8,4,16,128]{3,2,1,0:T(8,128)(2,1)} %cot_hbm.1), custom_call_target="tpu_custom_call" | custom-call | bytes 1000000 | tf_op jit(solution)/shard_map/pallas_call | solution.py:100
  2.4 0.4 collective-permute-done.1.feat_o.feat
  2.7 0.0 collective-permute-done.cot_o.cot
  2.7 0.1 shard_map.52
  2.8 3.8 %collective-permute-start.3 = (bf16[96,128]{1,0:T(8,128)(2,1)S(1)}, bf16[96,128]{1,0:T(8,128)(2,1)S(1)}, u32[]{:S(2)}, u32[]{:S(2)}) collective-permute-start(bf16[96,128]{1,0:T(8,128)(2,1)S(1)} %shard_map.52), channel_id=1, source_target_pairs={{0,1},{1,2},{2,3},{3,4},{4,5},{5,6},{6,7},{7,8},{8,9},{9,10},{10,1... | collective-permute-start | bytes 73736 | tf_op jit(solution)/shard_map/ppermute | solution.py:378
  6.7 6.4 %collective-permute-done.3.halo = bf16[96,128]{1,0:T(8,128)(2,1)S(1)} collective-permute-done((bf16[96,128]{1,0:T(8,128)(2,1)S(1)}, bf16[96,128]{1,0:T(8,128)(2,1)S(1)}, u32[]{:S(2)}, u32[]{:S(2)}) %collective-permute-start.3) | collective-permute-done | bytes 24608 | tf_op jit(solution)/shard_map/ppermute | solution.py:378
  13.1 0.0 collective-permute-start.4
  13.1 0.0 collective-permute-done.2.w_o
  13.1 1.6 %shard_map.51 = (bf16[8,32,128]{2,1,0:T(8,128)(2,1)S(1)}, bf16[2,128,512]{2,1,0:T(8,128)(2,1)S(1)}, bf16[2,4,144,512]{3,2,1,0:T(8,128)(2,1)S(1)}, f32[2,4,16,128...) custom-call(bf16[16,2,8,64]{3,2,1,0:T(8,128)(2,1)S(1)} %get-tuple-element.20.feat, ...), custom_call_target="tpu_custom_call" | custom-call | flops 200000000 | bytes 2500000 | tf_op jit(solution)/shard_map/pallas_call | solution.py:179
  14.7 0.0 collective-permute-done.4.halo_o
  14.7 0.9 %shard_map.53 = (bf16[26,32,128]{2,1,0:T(8,128)(2,1)S(1)}, bf16[26,32,128]{2,1,0:T(8,128)(2,1)S(1)}, bf16[26,32,128]{2,1,0:T(8,128)(2,1)S(1)}, bf16[18,32,128]{2,1,0:T(8,128)(2,1)S(1)}, f32[8,16,128]{2,1,0:T(8,128)S(1)}) custom-call(bf16[2,128,512]{2,1,0:T(8,128)(2,1)S(1)} %get-tuple-element.28.chosen, bf16[2,4,144,512]{3,2,1,0:T(8,128)(2,1)S(1)} %get-tuple-element.29.cols, ...), custom_call_target="tpu_custom_call" | custom-call | flops 400000000 | bytes 2500000 | tf_op jit(solution)/shard_map/pallas_call | solution.py:251
  15.6 1.6 %collective-permute-start.5 = (bf16[26,32,128]{2,1,0:T(8,128)(2,1)S(1)}, bf16[26,32,128]{2,1,0:T(8,128)(2,1)S(1)}, u32[]{:S(2)}, u32[]{:S(2)}) collective-permute-start(bf16[26,32,128]{2,1,0:T(8,128)(2,1)S(1)} %get-tuple-element.35), channel_id=1, source_target_pairs={{0,32},{16,112},{32,64},{48,16},{64,96},{80,48},{96,0},{112,80},{1... | collective-permute-start | bytes 638984 | tf_op jit(solution)/shard_map/ppermute | solution.py:369
  17.2 0.8 %collective-permute-start.6 = (bf16[26,32,128]{2,1,0:T(8,128)(2,1)S(1)}, bf16[26,32,128]{2,1,0:T(8,128)(2,1)S(1)}, u32[]{:S(2)}, u32[]{:S(2)}) collective-permute-start(bf16[26,32,128]{2,1,0:T(8,128)(2,1)S(1)} %get-tuple-element.36), channel_id=1, source_target_pairs={{0,160},{16,240},{32,192},{48,144},{64,224},{80,176},{96,128},{112... | collective-permute-start | bytes 638984 | tf_op jit(solution)/shard_map/ppermute | solution.py:369
  17.9 2.0 %collective-permute-start.7 = (bf16[26,32,128]{2,1,0:T(8,128)(2,1)S(1)}, bf16[26,32,128]{2,1,0:T(8,128)(2,1)S(1)}, u32[]{:S(2)}, u32[]{:S(2)}) collective-permute-start(bf16[26,32,128]{2,1,0:T(8,128)(2,1)S(1)} %get-tuple-element.37), channel_id=1, source_target_pairs={{0,64},{16,208},{32,96},{48,240},{64,0},{80,144},{96,32},{112,176}... | collective-permute-start | bytes 638984 | tf_op jit(solution)/shard_map/ppermute | solution.py:369
  19.9 2.8 %collective-permute-done.5.side = bf16[26,32,128]{2,1,0:T(8,128)(2,1)S(1)} collective-permute-done((bf16[26,32,128]{2,1,0:T(8,128)(2,1)S(1)}, bf16[26,32,128]{2,1,0:T(8,128)(2,1)S(1)}, u32[]{:S(2)}, u32[]{:S(2)}) %collective-permute-start.5) | collective-permute-done | bytes 213024 | tf_op jit(solution)/shard_map/ppermute | solution.py:369
  22.7 0.0 collective-permute-start.9
  22.7 7.9 %collective-permute-done.6.side_y = bf16[26,32,128]{2,1,0:T(8,128)(2,1)S(1)} collective-permute-done((bf16[26,32,128]{2,1,0:T(8,128)(2,1)S(1)}, bf16[26,32,128]{2,1,0:T(8,128)(2,1)S(1)}, u32[]{:S(2)}, u32[]{:S(2)}) %collective-permute-start.6) | collective-permute-done | bytes 213024 | tf_op jit(solution)/shard_map/ppermute | solution.py:369
  30.6 0.0 collective-permute-done.7.far
  30.6 0.5 %collective-permute-start.11 = (bf16[26,32,128]{2,1,0:T(8,128)(2,1)S(1)}, bf16[26,32,128]{2,1,0:T(8,128)(2,1)S(1)}, u32[]{:S(2)}, u32[]{:S(2)}) collective-permute-start(bf16[26,32,128]{2,1,0:T(8,128)(2,1)S(1)} %collective-permute-done.7.far), channel_id=1, source_target_pairs={{0,16},{16,0},{32,48},{48,32},{64,80},{80,64},{96,112},{112,96},{1... | collective-permute-start | bytes 638984 | tf_op jit(solution)/shard_map/ppermute | solution.py:369
  31.1 5.8 %collective-permute-done.8.away = bf16[18,32,128]{2,1,0:T(8,128)(2,1)S(1)} collective-permute-done((bf16[18,32,128]{2,1,0:T(8,128)(2,1)S(1)}, bf16[18,32,128]{2,1,0:T(8,128)(2,1)S(1)}, u32[]{:S(2)}, u32[]{:S(2)}) %collective-permute-start.8) | collective-permute-done | bytes 147488 | tf_op jit(solution)/shard_map/ppermute | solution.py:369
  36.9 1.8 %shard_map.54 = (bf16[8,4,16,128]{3,2,1,0:T(8,128)(2,1)}, bf16[16,2,8,64]{3,2,1,0:T(8,128)(2,1)}) custom-call(bf16[512,256]{1,0:T(8,128)(2,1)S(1)} %bitcast.2, bf16[256,256]{1,0:T(8,128)(2,1)S(1)} %get-tuple-element.27.spread, bf16[18,32,128]{2,1,0:T(8,128)(2,1)S(1)} %get-tuple-element.33.own, f32[8,16,128]{2,1,0:T(8,128)S(1)} %get-tuple-element.34.kept, ...), custom_call_target="tpu_custom_call" | custom-call | flops 400000000 | bytes 2500000 | tf_op jit(solution)/shard_map/pallas_call | solution.py:339
  (5 shorter events, 0.0 us)
Async XLA Ops:
  0.6 12.4 %collective-permute-start.2 = (bf16[4,4,4,8,256]{4,3,2,1,0:T(8,128)(2,1)}, bf16[4,4,4,8,256]{4,3,2,1,0:T(8,128)(2,1)S(1)}, u32[]{:S(2)}, u32[]{:S(2)}) collective-permute-start(bf16[4,4,4,8,256]{4,3,2,1,0:T(8,128)(2,1)} %bitcast.3), channel_id=1, source_target_pairs={{0,16},{16,0},{32,48},{48,32},{64,80},{80,64},{96,112},{112,96},{1... | collective-permute-start | bytes 786440 | tf_op jit(solution)/shard_map/ppermute | solution.py:369
  0.7 2.0 %collective-permute-start = (bf16[8,4,16,128]{3,2,1,0:T(8,128)(2,1)}, bf16[8,4,16,128]{3,2,1,0:T(8,128)(2,1)S(1)}, u32[]{:S(2)}, u32[]{:S(2)}) collective-permute-start(bf16[8,4,16,128]{3,2,1,0:T(8,128)(2,1)} %cot_hbm.1), channel_id=1, source_target_pairs={{0,16},{16,0},{32,48},{48,32},{64,80},{80,64},{96,112},{112,96},{1... | collective-permute-start | bytes 393224 | tf_op jit(solution)/shard_map/ppermute | solution.py:369
  1.2 1.5 %collective-permute-start.1 = (bf16[16,2,8,64]{3,2,1,0:T(8,128)(2,1)}, bf16[16,2,8,64]{3,2,1,0:T(8,128)(2,1)S(1)}, u32[]{:S(2)}, u32[]{:S(2)}) collective-permute-start(bf16[16,2,8,64]{3,2,1,0:T(8,128)(2,1)} %feat_hbm.1), channel_id=1, source_target_pairs={{0,16},{16,0},{32,48},{48,32},{64,80},{80,64},{96,112},{112,96},{1... | collective-permute-start | bytes 98312 | tf_op jit(solution)/shard_map/ppermute | solution.py:369
  2.8 10.2 %collective-permute-start.3 = (bf16[96,128]{1,0:T(8,128)(2,1)S(1)}, bf16[96,128]{1,0:T(8,128)(2,1)S(1)}, u32[]{:S(2)}, u32[]{:S(2)}) collective-permute-start(bf16[96,128]{1,0:T(8,128)(2,1)S(1)} %shard_map.52), channel_id=1, source_target_pairs={{0,1},{1,2},{2,3},{3,4},{4,5},{5,6},{6,7},{7,8},{8,9},{9,10},{10,1... | collective-permute-start | bytes 73736 | tf_op jit(solution)/shard_map/ppermute | solution.py:378
  13.1 1.6 %collective-permute-start.4 = (bf16[96,128]{1,0:T(8,128)(2,1)S(1)}, bf16[96,128]{1,0:T(8,128)(2,1)S(1)}, u32[]{:S(2)}, u32[]{:S(2)}) collective-permute-start(bf16[96,128]{1,0:T(8,128)(2,1)S(1)} %collective-permute-done.3.halo), channel_id=1, source_target_pairs={{0,16},{16,0},{32,48},{48,32},{64,80},{80,64},{96,112},{112,96},{1... | collective-permute-start | bytes 73736 | tf_op jit(solution)/shard_map/ppermute | solution.py:369
  15.6 7.1 %collective-permute-start.5 = (bf16[26,32,128]{2,1,0:T(8,128)(2,1)S(1)}, bf16[26,32,128]{2,1,0:T(8,128)(2,1)S(1)}, u32[]{:S(2)}, u32[]{:S(2)}) collective-permute-start(bf16[26,32,128]{2,1,0:T(8,128)(2,1)S(1)} %get-tuple-element.35), channel_id=1, source_target_pairs={{0,32},{16,112},{32,64},{48,16},{64,96},{80,48},{96,0},{112,80},{1... | collective-permute-start | bytes 638984 | tf_op jit(solution)/shard_map/ppermute | solution.py:369
  17.2 13.4 %collective-permute-start.6 = (bf16[26,32,128]{2,1,0:T(8,128)(2,1)S(1)}, bf16[26,32,128]{2,1,0:T(8,128)(2,1)S(1)}, u32[]{:S(2)}, u32[]{:S(2)}) collective-permute-start(bf16[26,32,128]{2,1,0:T(8,128)(2,1)S(1)} %get-tuple-element.36), channel_id=1, source_target_pairs={{0,160},{16,240},{32,192},{48,144},{64,224},{80,176},{96,128},{112... | collective-permute-start | bytes 638984 | tf_op jit(solution)/shard_map/ppermute | solution.py:369
  17.9 12.7 %collective-permute-start.7 = (bf16[26,32,128]{2,1,0:T(8,128)(2,1)S(1)}, bf16[26,32,128]{2,1,0:T(8,128)(2,1)S(1)}, u32[]{:S(2)}, u32[]{:S(2)}) collective-permute-start(bf16[26,32,128]{2,1,0:T(8,128)(2,1)S(1)} %get-tuple-element.37), channel_id=1, source_target_pairs={{0,64},{16,208},{32,96},{48,240},{64,0},{80,144},{96,32},{112,176}... | collective-permute-start | bytes 638984 | tf_op jit(solution)/shard_map/ppermute | solution.py:369
  22.7 14.1 %collective-permute-start.9 = (bf16[26,32,128]{2,1,0:T(8,128)(2,1)S(1)}, bf16[26,32,128]{2,1,0:T(8,128)(2,1)S(1)}, u32[]{:S(2)}, u32[]{:S(2)}) collective-permute-start(bf16[26,32,128]{2,1,0:T(8,128)(2,1)S(1)} %collective-permute-done.5.side), channel_id=1, source_target_pairs={{0,16},{16,0},{32,48},{48,32},{64,80},{80,64},{96,112},{112,96},{1... | collective-permute-start | bytes 638984 | tf_op jit(solution)/shard_map/ppermute | solution.py:369
  30.6 6.3 %collective-permute-start.10 = (bf16[26,32,128]{2,1,0:T(8,128)(2,1)S(1)}, bf16[26,32,128]{2,1,0:T(8,128)(2,1)S(1)}, u32[]{:S(2)}, u32[]{:S(2)}) collective-permute-start(bf16[26,32,128]{2,1,0:T(8,128)(2,1)S(1)} %collective-permute-done.6.side_y), channel_id=1, source_target_pairs={{0,16},{16,0},{32,48},{48,32},{64,80},{80,64},{96,112},{112,96},{1... | collective-permute-start | bytes 638984 | tf_op jit(solution)/shard_map/ppermute | solution.py:369
  30.6 6.3 %collective-permute-start.11 = (bf16[26,32,128]{2,1,0:T(8,128)(2,1)S(1)}, bf16[26,32,128]{2,1,0:T(8,128)(2,1)S(1)}, u32[]{:S(2)}, u32[]{:S(2)}) collective-permute-start(bf16[26,32,128]{2,1,0:T(8,128)(2,1)S(1)} %collective-permute-done.7.far), channel_id=1, source_target_pairs={{0,16},{16,0},{32,48},{48,32},{64,80},{80,64},{96,112},{112,96},{1... | collective-permute-start | bytes 638984 | tf_op jit(solution)/shard_map/ppermute | solution.py:369
  31.1 5.8 %collective-permute-start.8 = (bf16[18,32,128]{2,1,0:T(8,128)(2,1)S(1)}, bf16[18,32,128]{2,1,0:T(8,128)(2,1)S(1)}, u32[]{:S(2)}, u32[]{:S(2)}) collective-permute-start(bf16[18,32,128]{2,1,0:T(8,128)(2,1)S(1)} %get-tuple-element.33.own), channel_id=1, source_target_pairs={{0,128},{16,144},{32,160},{48,176},{64,192},{80,208},{96,224},{112... | collective-permute-start | bytes 442376 | tf_op jit(solution)/shard_map/ppermute | solution.py:369

commit v5 on v4

--- a/solution.py
+++ b/solution.py
@@ -197,7 +197,46 @@
     )(feat, feat_o, cot, cot_o, w_o, select, pltpu.with_memory_space_constraint(w, pltpu.HBM))
 
 
-def grad_body(chosen, cols, ends, select_ref, halo, halo_o, both, far, side_y, side, away, kept):
+def partial_rows(chosen, tile, pair):
+    total = None
+    for k in range(2):
+        halves = []
+        for v in (2 * pair, 2 * pair + 1):
+            parts = []
+            for p in range(4):
+                for r in range(4):
+                    parts += tile(k, p, v, slice(r * 128, (r + 1) * 128))
+            halves.append(jnp.concatenate(parts, axis=0))
+        part = dot(chosen[k], jnp.concatenate(halves, axis=1))
+        total = part if total is None else total + part
+    high = total.astype(BF)
+    return high, (total - high.astype(F32)).astype(BF), total
+
+
+def middle_body(chosen, cols, mid, mid_away, mid_kept):
+    tile = lambda k, p, v, lanes: [cols[k, p, 16 * v : 16 * v + 32, lanes]]
+    for pair in (1, 2):
+        high, rest, total = partial_rows(chosen, tile, pair)
+        for half in range(2):
+            i, lanes = 2 * pair + half - 2, slice(half * 128, (half + 1) * 128)
+            mid[i], mid[4 + i] = high[0:96, lanes], rest[0:96, lanes]
+            mid_away[i, 0:16, :] = high[96:112, lanes]
+            mid_away[i, 16:32, :] = rest[96:112, lanes]
+            mid_kept[i] = total[112:128, lanes]
+
+
+def middle(chosen, cols):
+    return call(
+        middle_body,
+        (s((8, 96, 128)), s((4, 32, 128)), s((4, 16, 128), F32)),
+        [],
+        (200000000, 1500000),
+    )(chosen, cols)
+
+
+def grad_body(
+    chosen, cols, ends, select_ref, halo, halo_o, both, mid, mid_away, mid_kept, far, side_y, side, away, kept
+):
     core = core_index()
     up = pick(core, halo[0:32, :].astype(F32), halo_o[0:32, :].astype(F32)).astype(BF)
     down = pick(core, halo_o[0:32, :].astype(F32), halo[0:32, :].astype(F32)).astype(BF)
@@ -216,26 +255,16 @@
             planes.append(jnp.concatenate(pieces, axis=0).astype(BF))
         for p in range(4):
             tips[k, p] = columns(planes, p, select)
-    for pair in range(4):
-        total = None
-        for k in range(2):
-            halves = []
-            for v in (2 * pair, 2 * pair + 1):
-                parts = []
-                for p in range(4):
-                    for r in range(4):
-                        lanes = slice(r * 128, (r + 1) * 128)
-                        if v == 0:
-                            parts += [tips[k, p][0:16, lanes], cols[k, p, 16:32, lanes]]
-                        elif v == 7:
-                            parts += [cols[k, p, 112:128, lanes], tips[k, p][16:32, lanes]]
-                        else:
-                            parts.append(cols[k, p, 16 * v : 16 * v + 32, lanes])
-                halves.append(jnp.concatenate(parts, axis=0))
-            part = dot(chosen[k], jnp.concatenate(halves, axis=1))
-            total = part if total is None else total + part
-        high = total.astype(BF)
-        rest = (total - high.astype(F32)).astype(BF)
+
+    def tile(k, p, v, lanes):
+        if v == 0:
+            return [tips[k, p][0:16, lanes], cols[k, p, 16:32, lanes]]
+        if v == 7:
+            return [cols[k, p, 112:128, lanes], tips[k, p][16:32, lanes]]
+        return [cols[k, p, 16 * v : 16 * v + 32, lanes]]
+
+    for pair in (0, 3):
+        high, rest, total = partial_rows(chosen, tile, pair)
         for half in range(2):
             v, lanes = 2 * pair + half, slice(half * 128, (half + 1) * 128)
             for n, out in enumerate((far, side_y, side)):
@@ -244,6 +273,12 @@
             away[10 + v, 0:16, :] = high[96:112, lanes]
             away[10 + v, 16:32, :] = rest[96:112, lanes]
             kept[v] = total[112:128, lanes]
+    for i in range(4):
+        for n, out in enumerate((far, side_y, side)):
+            out[12 + i] = mid[i, n * 32 : (n + 1) * 32, :]
+            out[20 + i] = mid[4 + i, n * 32 : (n + 1) * 32, :]
+        away[12 + i] = mid_away[i]
+        kept[2 + i] = mid_kept[i]
 
 
 def grad(*args):
@@ -378,7 +413,8 @@
     halo = lax.ppermute(edges, ("chan", "space"), cross)
     both, chosen, cols, ends, w_near = ready(feat, feat_other, cot, cot_other, w_other, select, w_own)
     halo_other = send(halo, swap)
-    far, side_y, side, away, kept = grad(chosen, cols, ends, select, halo, halo_other, both)
+    rows = middle(chosen, cols)
+    far, side_y, side, away, kept = grad(chosen, cols, ends, select, halo, halo_other, both, *rows)
     own = away
 
     far, side_y = send(far, over), send(side_y, beside_y)

time: 38.8 us -> 39 us (level)
  transfers between devices with their start and end apart: 12 -> 12, of which waited for: 5 -> 5; matrix products, arithmetic and copies ran while one was open for 0% -> 0% of each run, Pallas kernels for 7% -> 8%
where the time goes in v5:
time: 39 us; the launch traced here: 38.8 us
  waiting for transfers between devices  23.2 us (59%)
  starting transfers between devices  9.32 us (24%)
  Pallas kernels  5.57 us (14%)
  between operations  0.7 us (2%)
    ppermute x11, waiting for transfers between devices, local(): send = lambda a, pairs: lax.ppermute(a, 'chan', pairs)  16.8 us
    ppermute x1, waiting for transfers between devices, local(): halo = lax.ppermute(edges, ('chan', 'space'), cross)  6.4 us
    ppermute x11, starting transfers between devices, local(): send = lambda a, pairs: lax.ppermute(a, 'chan', pairs)  5.51 us
    ppermute x1, starting transfers between devices, local(): halo = lax.ppermute(edges, ('chan', 'space'), cross)  3.82 us
    pallas_call x1, Pallas kernels, last(): call(last_body, (s((8, 4, 16, 128)), s((16, 2, 8, 64))), [pltpu.VMEM((10,...  1.8 us
    pallas_call x1, Pallas kernels, ready(): call(ready_body, (s((8, 32, 128)), s((2, 128, 512)), s((2, 4, 144, 512)),...  1.63 us
    pallas_call x1, Pallas kernels, mine(): call(mine_body, (s((48, 128), F32), s((16, 2, 8, 64)), s((8, 4, 16, 128))...  1.05 us
  transfers between devices with their start and end apart: 12, of which 5 were waited for; matrix products, arithmetic and copies ran while one was open for 0% of the time, Pallas kernels for 8%

profile of v5, /device:TPU:24, one launch (start us, length us, event | category | flops | bytes accessed | tf_op | source)
XLA Modules:
  0.0 38.8 jit_solution(4932536698091380202)
XLA Ops:
  0.6 0.1 collective-permute-start.2
  0.7 0.5 %collective-permute-start = (bf16[8,4,16,128]{3,2,1,0:T(8,128)(2,1)}, bf16[8,4,16,128]{3,2,1,0:T(8,128)(2,1)S(1)}, u32[]{:S(2)}, u32[]{:S(2)}) collective-permute-start(bf16[8,4,16,128]{3,2,1,0:T(8,128)(2,1)} %cot_hbm.1), channel_id=1, source_target_pairs={{0,16},{16,0},{32,48},{48,32},{64,80},{80,64},{96,112},{112,96},{1... | collective-permute-start | bytes 393224 | tf_op jit(solution)/shard_map/ppermute | solution.py:404
  1.2 0.1 collective-permute-start.1
  1.3 1.0 %shard_map.50 = (f32[48,128]{1,0:T(8,128)S(1)}, bf16[16,2,8,64]{3,2,1,0:T(8,128)(2,1)S(1)}, bf16[8,4,16,128]{3,2,1,0:T(8,128)(2,1)S(1)}, bf16[256,512]{1,0:T(8,128)(2,1)S(1)}, bf16[256,256]{1,0:T(8,128)(2,1)S(1)}) custom-call(bf16[16,2,8,64]{3,2,1,0:T(8,128)(2,1)} %feat_hbm.1, bf16[8,4,16,128]{3,2,1,0:T(8,128)(2,1)} %cot_hbm.1), custom_call_target="tpu_custom_call" | custom-call | bytes 1000000 | tf_op jit(solution)/shard_map/pallas_call | solution.py:100
  2.4 0.4 collective-permute-done.1.feat_o.feat
  2.7 0.0 collective-permute-done.cot_o.cot
  2.7 0.1 shard_map.52
  2.8 3.8 %collective-permute-start.3 = (bf16[96,128]{1,0:T(8,128)(2,1)S(1)}, bf16[96,128]{1,0:T(8,128)(2,1)S(1)}, u32[]{:S(2)}, u32[]{:S(2)}) collective-permute-start(bf16[96,128]{1,0:T(8,128)(2,1)S(1)} %shard_map.52), channel_id=1, source_target_pairs={{0,1},{1,2},{2,3},{3,4},{4,5},{5,6},{6,7},{7,8},{8,9},{9,10},{10,1... | collective-permute-start | bytes 73736 | tf_op jit(solution)/shard_map/ppermute | solution.py:413
  6.7 6.4 %collective-permute-done.3.halo = bf16[96,128]{1,0:T(8,128)(2,1)S(1)} collective-permute-done((bf16[96,128]{1,0:T(8,128)(2,1)S(1)}, bf16[96,128]{1,0:T(8,128)(2,1)S(1)}, u32[]{:S(2)}, u32[]{:S(2)}) %collective-permute-start.3) | collective-permute-done | bytes 24608 | tf_op jit(solution)/shard_map/ppermute | solution.py:413
  13.1 0.0 collective-permute-start.4
  13.1 0.0 collective-permute-done.2.w_o
  13.1 1.6 %shard_map.51 = (bf16[8,32,128]{2,1,0:T(8,128)(2,1)S(1)}, bf16[2,128,512]{2,1,0:T(8,128)(2,1)S(1)}, bf16[2,4,144,512]{3,2,1,0:T(8,128)(2,1)S(1)}, f32[2,4,16,128...) custom-call(bf16[16,2,8,64]{3,2,1,0:T(8,128)(2,1)S(1)} %get-tuple-element.23.feat, ...), custom_call_target="tpu_custom_call" | custom-call | flops 200000000 | bytes 2500000 | tf_op jit(solution)/shard_map/pallas_call | solution.py:179
  14.7 0.3 shard_map.53
  15.0 0.0 collective-permute-done.4.halo_o
  15.0 0.7 %shard_map.54 = (bf16[26,32,128]{2,1,0:T(8,128)(2,1)S(1)}, bf16[26,32,128]{2,1,0:T(8,128)(2,1)S(1)}, bf16[26,32,128]{2,1,0:T(8,128)(2,1)S(1)}, bf16[18,32,128]{2,1,0:T(8,128)(2,1)S(1)}, f32[8,16,128]{2,1,0:T(8,128)S(1)}) custom-call(bf16[2,128,512]{2,1,0:T(8,128)(2,1)S(1)} %get-tuple-element.31.chosen, bf16[2,4,144,512]{3,2,1,0:T(8,128)(2,1)S(1)} %get-tuple-element.32.cols, ...), custom_call_target="tpu_custom_call" | custom-call | flops 400000000 | bytes 2500000 | tf_op jit(solution)/shard_map/pallas_call | solution.py:286
  15.7 1.6 %collective-permute-start.5 = (bf16[26,32,128]{2,1,0:T(8,128)(2,1)S(1)}, bf16[26,32,128]{2,1,0:T(8,128)(2,1)S(1)}, u32[]{:S(2)}, u32[]{:S(2)}) collective-permute-start(bf16[26,32,128]{2,1,0:T(8,128)(2,1)S(1)} %get-tuple-element.41), channel_id=1, source_target_pairs={{0,32},{16,112},{32,64},{48,16},{64,96},{80,48},{96,0},{112,80},{1... | collective-permute-start | bytes 638984 | tf_op jit(solution)/shard_map/ppermute | solution.py:404
  17.3 0.8 %collective-permute-start.6 = (bf16[26,32,128]{2,1,0:T(8,128)(2,1)S(1)}, bf16[26,32,128]{2,1,0:T(8,128)(2,1)S(1)}, u32[]{:S(2)}, u32[]{:S(2)}) collective-permute-start(bf16[26,32,128]{2,1,0:T(8,128)(2,1)S(1)} %get-tuple-element.42), channel_id=1, source_target_pairs={{0,160},{16,240},{32,192},{48,144},{64,224},{80,176},{96,128},{112... | collective-permute-start | bytes 638984 | tf_op jit(solution)/shard_map/ppermute | solution.py:404
  18.1 2.0 %collective-permute-start.7 = (bf16[26,32,128]{2,1,0:T(8,128)(2,1)S(1)}, bf16[26,32,128]{2,1,0:T(8,128)(2,1)S(1)}, u32[]{:S(2)}, u32[]{:S(2)}) collective-permute-start(bf16[26,32,128]{2,1,0:T(8,128)(2,1)S(1)} %get-tuple-element.43), channel_id=1, source_target_pairs={{0,64},{16,208},{32,96},{48,240},{64,0},{80,144},{96,32},{112,176}... | collective-permute-start | bytes 638984 | tf_op jit(solution)/shard_map/ppermute | solution.py:404
  20.0 2.8 %collective-permute-done.5.side = bf16[26,32,128]{2,1,0:T(8,128)(2,1)S(1)} collective-permute-done((bf16[26,32,128]{2,1,0:T(8,128)(2,1)S(1)}, bf16[26,32,128]{2,1,0:T(8,128)(2,1)S(1)}, u32[]{:S(2)}, u32[]{:S(2)}) %collective-permute-start.5) | collective-permute-done | bytes 213024 | tf_op jit(solution)/shard_map/ppermute | solution.py:404
  22.9 7.9 %collective-permute-done.6.side_y = bf16[26,32,128]{2,1,0:T(8,128)(2,1)S(1)} collective-permute-done((bf16[26,32,128]{2,1,0:T(8,128)(2,1)S(1)}, bf16[26,32,128]{2,1,0:T(8,128)(2,1)S(1)}, u32[]{:S(2)}, u32[]{:S(2)}) %collective-permute-start.6) | collective-permute-done | bytes 213024 | tf_op jit(solution)/shard_map/ppermute | solution.py:404
  30.7 0.0 collective-permute-done.7.far
  30.7 0.5 %collective-permute-start.11 = (bf16[26,32,128]{2,1,0:T(8,128)(2,1)S(1)}, bf16[26,32,128]{2,1,0:T(8,128)(2,1)S(1)}, u32[]{:S(2)}, u32[]{:S(2)}) collective-permute-start(bf16[26,32,128]{2,1,0:T(8,128)(2,1)S(1)} %collective-permute-done.7.far), channel_id=1, source_target_pairs={{0,16},{16,0},{32,48},{48,32},{64,80},{80,64},{96,112},{112,96},{1... | collective-permute-start | bytes 638984 | tf_op jit(solution)/shard_map/ppermute | solution.py:404
  31.3 5.8 %collective-permute-done.8.away = bf16[18,32,128]{2,1,0:T(8,128)(2,1)S(1)} collective-permute-done((bf16[18,32,128]{2,1,0:T(8,128)(2,1)S(1)}, bf16[18,32,128]{2,1,0:T(8,128)(2,1)S(1)}, u32[]{:S(2)}, u32[]{:S(2)}) %collective-permute-start.8) | collective-permute-done | bytes 147488 | tf_op jit(solution)/shard_map/ppermute | solution.py:404
  37.0 1.8 %shard_map.55 = (bf16[8,4,16,128]{3,2,1,0:T(8,128)(2,1)}, bf16[16,2,8,64]{3,2,1,0:T(8,128)(2,1)}) custom-call(bf16[512,256]{1,0:T(8,128)(2,1)S(1)} %bitcast.2, bf16[256,256]{1,0:T(8,128)(2,1)S(1)} %get-tuple-element.30.spread, bf16[18,32,128]{2,1,0:T(8,128)(2,1)S(1)} %get-tuple-element.39.own, f32[8,16,128]{2,1,0:T(8,128)S(1)} %get-tuple-element.40.kept, ...), custom_call_target="tpu_custom_call" | custom-call | flops 400000000 | bytes 2500000 | tf_op jit(solution)/shard_map/pallas_call | solution.py:374
  (6 shorter events, 0.0 us)
Async XLA Ops:
  0.6 12.4 %collective-permute-start.2 = (bf16[4,4,4,8,256]{4,3,2,1,0:T(8,128)(2,1)}, bf16[4,4,4,8,256]{4,3,2,1,0:T(8,128)(2,1)S(1)}, u32[]{:S(2)}, u32[]{:S(2)}) collective-permute-start(bf16[4,4,4,8,256]{4,3,2,1,0:T(8,128)(2,1)} %bitcast.3), channel_id=1, source_target_pairs={{0,16},{16,0},{32,48},{48,32},{64,80},{80,64},{96,112},{112,96},{1... | collective-permute-start | bytes 786440 | tf_op jit(solution)/shard_map/ppermute | solution.py:404
  0.7 2.0 %collective-permute-start = (bf16[8,4,16,128]{3,2,1,0:T(8,128)(2,1)}, bf16[8,4,16,128]{3,2,1,0:T(8,128)(2,1)S(1)}, u32[]{:S(2)}, u32[]{:S(2)}) collective-permute-start(bf16[8,4,16,128]{3,2,1,0:T(8,128)(2,1)} %cot_hbm.1), channel_id=1, source_target_pairs={{0,16},{16,0},{32,48},{48,32},{64,80},{80,64},{96,112},{112,96},{1... | collective-permute-start | bytes 393224 | tf_op jit(solution)/shard_map/ppermute | solution.py:404
  1.2 1.5 %collective-permute-start.1 = (bf16[16,2,8,64]{3,2,1,0:T(8,128)(2,1)}, bf16[16,2,8,64]{3,2,1,0:T(8,128)(2,1)S(1)}, u32[]{:S(2)}, u32[]{:S(2)}) collective-permute-start(bf16[16,2,8,64]{3,2,1,0:T(8,128)(2,1)} %feat_hbm.1), channel_id=1, source_target_pairs={{0,16},{16,0},{32,48},{48,32},{64,80},{80,64},{96,112},{112,96},{1... | collective-permute-start | bytes 98312 | tf_op jit(solution)/shard_map/ppermute | solution.py:404
  2.8 10.2 %collective-permute-start.3 = (bf16[96,128]{1,0:T(8,128)(2,1)S(1)}, bf16[96,128]{1,0:T(8,128)(2,1)S(1)}, u32[]{:S(2)}, u32[]{:S(2)}) collective-permute-start(bf16[96,128]{1,0:T(8,128)(2,1)S(1)} %shard_map.52), channel_id=1, source_target_pairs={{0,1},{1,2},{2,3},{3,4},{4,5},{5,6},{6,7},{7,8},{8,9},{9,10},{10,1... | collective-permute-start | bytes 73736 | tf_op jit(solution)/shard_map/ppermute | solution.py:413
  13.1 2.0 %collective-permute-start.4 = (bf16[96,128]{1,0:T(8,128)(2,1)S(1)}, bf16[96,128]{1,0:T(8,128)(2,1)S(1)}, u32[]{:S(2)}, u32[]{:S(2)}) collective-permute-start(bf16[96,128]{1,0:T(8,128)(2,1)S(1)} %collective-permute-done.3.halo), channel_id=1, source_target_pairs={{0,16},{16,0},{32,48},{48,32},{64,80},{80,64},{96,112},{112,96},{1... | collective-permute-start | bytes 73736 | tf_op jit(solution)/shard_map/ppermute | solution.py:404
  15.7 7.1 %collective-permute-start.5 = (bf16[26,32,128]{2,1,0:T(8,128)(2,1)S(1)}, bf16[26,32,128]{2,1,0:T(8,128)(2,1)S(1)}, u32[]{:S(2)}, u32[]{:S(2)}) collective-permute-start(bf16[26,32,128]{2,1,0:T(8,128)(2,1)S(1)} %get-tuple-element.41), channel_id=1, source_target_pairs={{0,32},{16,112},{32,64},{48,16},{64,96},{80,48},{96,0},{112,80},{1... | collective-permute-start | bytes 638984 | tf_op jit(solution)/shard_map/ppermute | solution.py:404
  17.3 13.4 %collective-permute-start.6 = (bf16[26,32,128]{2,1,0:T(8,128)(2,1)S(1)}, bf16[26,32,128]{2,1,0:T(8,128)(2,1)S(1)}, u32[]{:S(2)}, u32[]{:S(2)}) collective-permute-start(bf16[26,32,128]{2,1,0:T(8,128)(2,1)S(1)} %get-tuple-element.42), channel_id=1, source_target_pairs={{0,160},{16,240},{32,192},{48,144},{64,224},{80,176},{96,128},{112... | collective-permute-start | bytes 638984 | tf_op jit(solution)/shard_map/ppermute | solution.py:404
  18.1 12.7 %collective-permute-start.7 = (bf16[26,32,128]{2,1,0:T(8,128)(2,1)S(1)}, bf16[26,32,128]{2,1,0:T(8,128)(2,1)S(1)}, u32[]{:S(2)}, u32[]{:S(2)}) collective-permute-start(bf16[26,32,128]{2,1,0:T(8,128)(2,1)S(1)} %get-tuple-element.43), channel_id=1, source_target_pairs={{0,64},{16,208},{32,96},{48,240},{64,0},{80,144},{96,32},{112,176}... | collective-permute-start | bytes 638984 | tf_op jit(solution)/shard_map/ppermute | solution.py:404
  22.9 14.1 %collective-permute-start.9 = (bf16[26,32,128]{2,1,0:T(8,128)(2,1)S(1)}, bf16[26,32,128]{2,1,0:T(8,128)(2,1)S(1)}, u32[]{:S(2)}, u32[]{:S(2)}) collective-permute-start(bf16[26,32,128]{2,1,0:T(8,128)(2,1)S(1)} %collective-permute-done.5.side), channel_id=1, source_target_pairs={{0,16},{16,0},{32,48},{48,32},{64,80},{80,64},{96,112},{112,96},{1... | collective-permute-start | bytes 638984 | tf_op jit(solution)/shard_map/ppermute | solution.py:404
  30.7 6.3 %collective-permute-start.10 = (bf16[26,32,128]{2,1,0:T(8,128)(2,1)S(1)}, bf16[26,32,128]{2,1,0:T(8,128)(2,1)S(1)}, u32[]{:S(2)}, u32[]{:S(2)}) collective-permute-start(bf16[26,32,128]{2,1,0:T(8,128)(2,1)S(1)} %collective-permute-done.6.side_y), channel_id=1, source_target_pairs={{0,16},{16,0},{32,48},{48,32},{64,80},{80,64},{96,112},{112,96},{1... | collective-permute-start | bytes 638984 | tf_op jit(solution)/shard_map/ppermute | solution.py:404
  30.7 6.3 %collective-permute-start.11 = (bf16[26,32,128]{2,1,0:T(8,128)(2,1)S(1)}, bf16[26,32,128]{2,1,0:T(8,128)(2,1)S(1)}, u32[]{:S(2)}, u32[]{:S(2)}) collective-permute-start(bf16[26,32,128]{2,1,0:T(8,128)(2,1)S(1)} %collective-permute-done.7.far), channel_id=1, source_target_pairs={{0,16},{16,0},{32,48},{48,32},{64,80},{80,64},{96,112},{112,96},{1... | collective-permute-start | bytes 638984 | tf_op jit(solution)/shard_map/ppermute | solution.py:404
  31.3 5.8 %collective-permute-start.8 = (bf16[18,32,128]{2,1,0:T(8,128)(2,1)S(1)}, bf16[18,32,128]{2,1,0:T(8,128)(2,1)S(1)}, u32[]{:S(2)}, u32[]{:S(2)}) collective-permute-start(bf16[18,32,128]{2,1,0:T(8,128)(2,1)S(1)} %get-tuple-element.39.own), channel_id=1, source_target_pairs={{0,128},{16,144},{32,160},{48,176},{64,192},{80,208},{96,224},{112... | collective-permute-start | bytes 442376 | tf_op jit(solution)/shard_map/ppermute | solution.py:404

commit v6 on v5

--- a/solution.py
+++ b/solution.py
@@ -132,11 +132,15 @@
     return zero + core * (one - zero)
 
 
-def columns(planes, p, select):
+def neighbours(planes, p):
     zero = jnp.zeros_like(planes[0])
     before = planes[p - 1] if p > 0 else zero
     after = planes[p + 1] if p < 3 else zero
-    return dot(jnp.concatenate([before, after], axis=1), select).astype(BF)
+    return jnp.concatenate([before, after], axis=1)
+
+
+def columns(planes, p, select):
+    return dot(neighbours(planes, p), select).astype(BF)
 
 
 def ready_body(feat, feat_o, cot, cot_o, w_o, select_ref, w_hbm, both, chosen, cols, ends, w, fs, cs, wk, wt, sem):
@@ -245,7 +249,7 @@
         for v in range(8):
             out[v + 1] = both[v]
     select = select_ref[...]
-    tips = {}
+    pairs = []
     for k in range(2):
         planes = []
         for a in range(4):
@@ -253,8 +257,9 @@
             own, other = halo[mine_at : mine_at + 8, :].astype(F32), halo_o[theirs_at : theirs_at + 8, :].astype(F32)
             pieces = [pick(core, own, other), ends[k, a], pick(core, other, own)]
             planes.append(jnp.concatenate(pieces, axis=0).astype(BF))
-        for p in range(4):
-            tips[k, p] = columns(planes, p, select)
+        pairs += [neighbours(planes, p) for p in range(4)]
+    ends_of = dot(jnp.concatenate(pairs, axis=0), select).astype(BF)
+    tips = {(k, p): ends_of[(k * 4 + p) * 32 : (k * 4 + p + 1) * 32] for k in range(2) for p in range(4)}
 
     def tile(k, p, v, lanes):
         if v == 0:

time: 39 us -> 38.8 us (level)
  no operation moved by 1% of the time
where the time goes in v6:
time: 38.8 us; the launch traced here: 38.6 us
  waiting for transfers between devices  23.2 us (60%)
  starting transfers between devices  9.33 us (24%)
  Pallas kernels  5.4 us (14%)
  between operations  0.7 us (2%)
    ppermute x11, waiting for transfers between devices, local(): send = lambda a, pairs: lax.ppermute(a, 'chan', pairs)  16.8 us
    ppermute x1, waiting for transfers between devices, local(): halo = lax.ppermute(edges, ('chan', 'space'), cross)  6.4 us
    ppermute x11, starting transfers between devices, local(): send = lambda a, pairs: lax.ppermute(a, 'chan', pairs)  5.51 us
    ppermute x1, starting transfers between devices, local(): halo = lax.ppermute(edges, ('chan', 'space'), cross)  3.82 us
    pallas_call x1, Pallas kernels, last(): call(last_body, (s((8, 4, 16, 128)), s((16, 2, 8, 64))), [pltpu.VMEM((10,...  1.8 us
    pallas_call x1, Pallas kernels, ready(): call(ready_body, (s((8, 32, 128)), s((2, 128, 512)), s((2, 4, 144, 512)),...  1.63 us
    pallas_call x1, Pallas kernels, mine(): call(mine_body, (s((48, 128), F32), s((16, 2, 8, 64)), s((8, 4, 16, 128))...  1.05 us
  transfers between devices with their start and end apart: 12, of which 5 were waited for; matrix products, arithmetic and copies ran while one was open for 0% of the time, Pallas kernels for 8%

profile of v6, /device:TPU:24, one launch (start us, length us, event | category | flops | bytes accessed | tf_op | source)
XLA Modules:
  0.0 38.6 jit_solution(237559679226154561)
XLA Ops:
  0.6 0.1 collective-permute-start.2
  0.7 0.5 %collective-permute-start = (bf16[8,4,16,128]{3,2,1,0:T(8,128)(2,1)}, bf16[8,4,16,128]{3,2,1,0:T(8,128)(2,1)S(1)}, u32[]{:S(2)}, u32[]{:S(2)}) collective-permute-start(bf16[8,4,16,128]{3,2,1,0:T(8,128)(2,1)} %cot_hbm.1), channel_id=1, source_target_pairs={{0,16},{16,0},{32,48},{48,32},{64,80},{80,64},{96,112},{112,96},{1... | collective-permute-start | bytes 393224 | tf_op jit(solution)/shard_map/ppermute | solution.py:409
  1.2 0.1 collective-permute-start.1
  1.3 1.0 %shard_map.50 = (f32[48,128]{1,0:T(8,128)S(1)}, bf16[16,2,8,64]{3,2,1,0:T(8,128)(2,1)S(1)}, bf16[8,4,16,128]{3,2,1,0:T(8,128)(2,1)S(1)}, bf16[256,512]{1,0:T(8,128)(2,1)S(1)}, bf16[256,256]{1,0:T(8,128)(2,1)S(1)}) custom-call(bf16[16,2,8,64]{3,2,1,0:T(8,128)(2,1)} %feat_hbm.1, bf16[8,4,16,128]{3,2,1,0:T(8,128)(2,1)} %cot_hbm.1), custom_call_target="tpu_custom_call" | custom-call | bytes 1000000 | tf_op jit(solution)/shard_map/pallas_call | solution.py:100
  2.4 0.4 collective-permute-done.1.feat_o.feat
  2.7 0.0 collective-permute-done.cot_o.cot
  2.7 0.1 shard_map.52
  2.8 3.8 %collective-permute-start.3 = (bf16[96,128]{1,0:T(8,128)(2,1)S(1)}, bf16[96,128]{1,0:T(8,128)(2,1)S(1)}, u32[]{:S(2)}, u32[]{:S(2)}) collective-permute-start(bf16[96,128]{1,0:T(8,128)(2,1)S(1)} %shard_map.52), channel_id=1, source_target_pairs={{0,1},{1,2},{2,3},{3,4},{4,5},{5,6},{6,7},{7,8},{8,9},{9,10},{10,1... | collective-permute-start | bytes 73736 | tf_op jit(solution)/shard_map/ppermute | solution.py:418
  6.7 6.4 %collective-permute-done.3.halo = bf16[96,128]{1,0:T(8,128)(2,1)S(1)} collective-permute-done((bf16[96,128]{1,0:T(8,128)(2,1)S(1)}, bf16[96,128]{1,0:T(8,128)(2,1)S(1)}, u32[]{:S(2)}, u32[]{:S(2)}) %collective-permute-start.3) | collective-permute-done | bytes 24608 | tf_op jit(solution)/shard_map/ppermute | solution.py:418
  13.1 0.0 collective-permute-start.4
  13.1 0.0 collective-permute-done.2.w_o
  13.1 1.6 %shard_map.51 = (bf16[8,32,128]{2,1,0:T(8,128)(2,1)S(1)}, bf16[2,128,512]{2,1,0:T(8,128)(2,1)S(1)}, bf16[2,4,144,512]{3,2,1,0:T(8,128)(2,1)S(1)}, f32[2,4,16,128...) custom-call(bf16[16,2,8,64]{3,2,1,0:T(8,128)(2,1)S(1)} %get-tuple-element.23.feat, ...), custom_call_target="tpu_custom_call" | custom-call | flops 200000000 | bytes 2500000 | tf_op jit(solution)/shard_map/pallas_call | solution.py:183
  14.7 0.3 shard_map.53
  15.0 0.0 collective-permute-done.4.halo_o
  15.0 0.5 %shard_map.54 = (bf16[26,32,128]{2,1,0:T(8,128)(2,1)S(1)}, bf16[26,32,128]{2,1,0:T(8,128)(2,1)S(1)}, bf16[26,32,128]{2,1,0:T(8,128)(2,1)S(1)}, bf16[18,32,128]{2,1,0:T(8,128)(2,1)S(1)}, f32[8,16,128]{2,1,0:T(8,128)S(1)}) custom-call(bf16[2,128,512]{2,1,0:T(8,128)(2,1)S(1)} %get-tuple-element.31.chosen, bf16[2,4,144,512]{3,2,1,0:T(8,128)(2,1)S(1)} %get-tuple-element.32.cols, ...), custom_call_target="tpu_custom_call" | custom-call | flops 400000000 | bytes 2500000 | tf_op jit(solution)/shard_map/pallas_call | solution.py:291
  15.6 1.6 %collective-permute-start.5 = (bf16[26,32,128]{2,1,0:T(8,128)(2,1)S(1)}, bf16[26,32,128]{2,1,0:T(8,128)(2,1)S(1)}, u32[]{:S(2)}, u32[]{:S(2)}) collective-permute-start(bf16[26,32,128]{2,1,0:T(8,128)(2,1)S(1)} %get-tuple-element.41), channel_id=1, source_target_pairs={{0,32},{16,112},{32,64},{48,16},{64,96},{80,48},{96,0},{112,80},{1... | collective-permute-start | bytes 638984 | tf_op jit(solution)/shard_map/ppermute | solution.py:409
  17.1 0.8 %collective-permute-start.6 = (bf16[26,32,128]{2,1,0:T(8,128)(2,1)S(1)}, bf16[26,32,128]{2,1,0:T(8,128)(2,1)S(1)}, u32[]{:S(2)}, u32[]{:S(2)}) collective-permute-start(bf16[26,32,128]{2,1,0:T(8,128)(2,1)S(1)} %get-tuple-element.42), channel_id=1, source_target_pairs={{0,160},{16,240},{32,192},{48,144},{64,224},{80,176},{96,128},{112... | collective-permute-start | bytes 638984 | tf_op jit(solution)/shard_map/ppermute | solution.py:409
  17.9 2.0 %collective-permute-start.7 = (bf16[26,32,128]{2,1,0:T(8,128)(2,1)S(1)}, bf16[26,32,128]{2,1,0:T(8,128)(2,1)S(1)}, u32[]{:S(2)}, u32[]{:S(2)}) collective-permute-start(bf16[26,32,128]{2,1,0:T(8,128)(2,1)S(1)} %get-tuple-element.43), channel_id=1, source_target_pairs={{0,64},{16,208},{32,96},{48,240},{64,0},{80,144},{96,32},{112,176}... | collective-permute-start | bytes 638984 | tf_op jit(solution)/shard_map/ppermute | solution.py:409
  19.9 2.8 %collective-permute-done.5.side = bf16[26,32,128]{2,1,0:T(8,128)(2,1)S(1)} collective-permute-done((bf16[26,32,128]{2,1,0:T(8,128)(2,1)S(1)}, bf16[26,32,128]{2,1,0:T(8,128)(2,1)S(1)}, u32[]{:S(2)}, u32[]{:S(2)}) %collective-permute-start.5) | collective-permute-done | bytes 213024 | tf_op jit(solution)/shard_map/ppermute | solution.py:409
  22.7 7.9 %collective-permute-done.6.side_y = bf16[26,32,128]{2,1,0:T(8,128)(2,1)S(1)} collective-permute-done((bf16[26,32,128]{2,1,0:T(8,128)(2,1)S(1)}, bf16[26,32,128]{2,1,0:T(8,128)(2,1)S(1)}, u32[]{:S(2)}, u32[]{:S(2)}) %collective-permute-start.6) | collective-permute-done | bytes 213024 | tf_op jit(solution)/shard_map/ppermute | solution.py:409
  30.6 0.5 %collective-permute-start.11 = (bf16[26,32,128]{2,1,0:T(8,128)(2,1)S(1)}, bf16[26,32,128]{2,1,0:T(8,128)(2,1)S(1)}, u32[]{:S(2)}, u32[]{:S(2)}) collective-permute-start(bf16[26,32,128]{2,1,0:T(8,128)(2,1)S(1)} %collective-permute-done.7.far), channel_id=1, source_target_pairs={{0,16},{16,0},{32,48},{48,32},{64,80},{80,64},{96,112},{112,96},{1... | collective-permute-start | bytes 638984 | tf_op jit(solution)/shard_map/ppermute | solution.py:409
  31.1 5.8 %collective-permute-done.8.away = bf16[18,32,128]{2,1,0:T(8,128)(2,1)S(1)} collective-permute-done((bf16[18,32,128]{2,1,0:T(8,128)(2,1)S(1)}, bf16[18,32,128]{2,1,0:T(8,128)(2,1)S(1)}, u32[]{:S(2)}, u32[]{:S(2)}) %collective-permute-start.8) | collective-permute-done | bytes 147488 | tf_op jit(solution)/shard_map/ppermute | solution.py:409
  36.8 0.0 collective-permute-done.9.side_o
  36.8 1.8 %shard_map.55 = (bf16[8,4,16,128]{3,2,1,0:T(8,128)(2,1)}, bf16[16,2,8,64]{3,2,1,0:T(8,128)(2,1)}) custom-call(bf16[512,256]{1,0:T(8,128)(2,1)S(1)} %bitcast.2, bf16[256,256]{1,0:T(8,128)(2,1)S(1)} %get-tuple-element.30.spread, bf16[18,32,128]{2,1,0:T(8,128)(2,1)S(1)} %get-tuple-element.39.own, f32[8,16,128]{2,1,0:T(8,128)S(1)} %get-tuple-element.40.kept, ...), custom_call_target="tpu_custom_call" | custom-call | flops 400000000 | bytes 2500000 | tf_op jit(solution)/shard_map/pallas_call | solution.py:379
  (6 shorter events, 0.0 us)
Async XLA Ops:
  0.6 12.4 %collective-permute-start.2 = (bf16[4,4,4,8,256]{4,3,2,1,0:T(8,128)(2,1)}, bf16[4,4,4,8,256]{4,3,2,1,0:T(8,128)(2,1)S(1)}, u32[]{:S(2)}, u32[]{:S(2)}) collective-permute-start(bf16[4,4,4,8,256]{4,3,2,1,0:T(8,128)(2,1)} %bitcast.3), channel_id=1, source_target_pairs={{0,16},{16,0},{32,48},{48,32},{64,80},{80,64},{96,112},{112,96},{1... | collective-permute-start | bytes 786440 | tf_op jit(solution)/shard_map/ppermute | solution.py:409
  0.7 2.0 %collective-permute-start = (bf16[8,4,16,128]{3,2,1,0:T(8,128)(2,1)}, bf16[8,4,16,128]{3,2,1,0:T(8,128)(2,1)S(1)}, u32[]{:S(2)}, u32[]{:S(2)}) collective-permute-start(bf16[8,4,16,128]{3,2,1,0:T(8,128)(2,1)} %cot_hbm.1), channel_id=1, source_target_pairs={{0,16},{16,0},{32,48},{48,32},{64,80},{80,64},{96,112},{112,96},{1... | collective-permute-start | bytes 393224 | tf_op jit(solution)/shard_map/ppermute | solution.py:409
  1.2 1.5 %collective-permute-start.1 = (bf16[16,2,8,64]{3,2,1,0:T(8,128)(2,1)}, bf16[16,2,8,64]{3,2,1,0:T(8,128)(2,1)S(1)}, u32[]{:S(2)}, u32[]{:S(2)}) collective-permute-start(bf16[16,2,8,64]{3,2,1,0:T(8,128)(2,1)} %feat_hbm.1), channel_id=1, source_target_pairs={{0,16},{16,0},{32,48},{48,32},{64,80},{80,64},{96,112},{112,96},{1... | collective-permute-start | bytes 98312 | tf_op jit(solution)/shard_map/ppermute | solution.py:409
  2.8 10.2 %collective-permute-start.3 = (bf16[96,128]{1,0:T(8,128)(2,1)S(1)}, bf16[96,128]{1,0:T(8,128)(2,1)S(1)}, u32[]{:S(2)}, u32[]{:S(2)}) collective-permute-start(bf16[96,128]{1,0:T(8,128)(2,1)S(1)} %shard_map.52), channel_id=1, source_target_pairs={{0,1},{1,2},{2,3},{3,4},{4,5},{5,6},{6,7},{7,8},{8,9},{9,10},{10,1... | collective-permute-start | bytes 73736 | tf_op jit(solution)/shard_map/ppermute | solution.py:418
  13.1 2.0 %collective-permute-start.4 = (bf16[96,128]{1,0:T(8,128)(2,1)S(1)}, bf16[96,128]{1,0:T(8,128)(2,1)S(1)}, u32[]{:S(2)}, u32[]{:S(2)}) collective-permute-start(bf16[96,128]{1,0:T(8,128)(2,1)S(1)} %collective-permute-done.3.halo), channel_id=1, source_target_pairs={{0,16},{16,0},{32,48},{48,32},{64,80},{80,64},{96,112},{112,96},{1... | collective-permute-start | bytes 73736 | tf_op jit(solution)/shard_map/ppermute | solution.py:409
  15.6 7.1 %collective-permute-start.5 = (bf16[26,32,128]{2,1,0:T(8,128)(2,1)S(1)}, bf16[26,32,128]{2,1,0:T(8,128)(2,1)S(1)}, u32[]{:S(2)}, u32[]{:S(2)}) collective-permute-start(bf16[26,32,128]{2,1,0:T(8,128)(2,1)S(1)} %get-tuple-element.41), channel_id=1, source_target_pairs={{0,32},{16,112},{32,64},{48,16},{64,96},{80,48},{96,0},{112,80},{1... | collective-permute-start | bytes 638984 | tf_op jit(solution)/shard_map/ppermute | solution.py:409
  17.1 13.4 %collective-permute-start.6 = (bf16[26,32,128]{2,1,0:T(8,128)(2,1)S(1)}, bf16[26,32,128]{2,1,0:T(8,128)(2,1)S(1)}, u32[]{:S(2)}, u32[]{:S(2)}) collective-permute-start(bf16[26,32,128]{2,1,0:T(8,128)(2,1)S(1)} %get-tuple-element.42), channel_id=1, source_target_pairs={{0,160},{16,240},{32,192},{48,144},{64,224},{80,176},{96,128},{112... | collective-permute-start | bytes 638984 | tf_op jit(solution)/shard_map/ppermute | solution.py:409
  17.9 12.7 %collective-permute-start.7 = (bf16[26,32,128]{2,1,0:T(8,128)(2,1)S(1)}, bf16[26,32,128]{2,1,0:T(8,128)(2,1)S(1)}, u32[]{:S(2)}, u32[]{:S(2)}) collective-permute-start(bf16[26,32,128]{2,1,0:T(8,128)(2,1)S(1)} %get-tuple-element.43), channel_id=1, source_target_pairs={{0,64},{16,208},{32,96},{48,240},{64,0},{80,144},{96,32},{112,176}... | collective-permute-start | bytes 638984 | tf_op jit(solution)/shard_map/ppermute | solution.py:409
  22.7 14.1 %collective-permute-start.9 = (bf16[26,32,128]{2,1,0:T(8,128)(2,1)S(1)}, bf16[26,32,128]{2,1,0:T(8,128)(2,1)S(1)}, u32[]{:S(2)}, u32[]{:S(2)}) collective-permute-start(bf16[26,32,128]{2,1,0:T(8,128)(2,1)S(1)} %collective-permute-done.5.side), channel_id=1, source_target_pairs={{0,16},{16,0},{32,48},{48,32},{64,80},{80,64},{96,112},{112,96},{1... | collective-permute-start | bytes 638984 | tf_op jit(solution)/shard_map/ppermute | solution.py:409
  30.6 6.3 %collective-permute-start.10 = (bf16[26,32,128]{2,1,0:T(8,128)(2,1)S(1)}, bf16[26,32,128]{2,1,0:T(8,128)(2,1)S(1)}, u32[]{:S(2)}, u32[]{:S(2)}) collective-permute-start(bf16[26,32,128]{2,1,0:T(8,128)(2,1)S(1)} %collective-permute-done.6.side_y), channel_id=1, source_target_pairs={{0,16},{16,0},{32,48},{48,32},{64,80},{80,64},{96,112},{112,96},{1... | collective-permute-start | bytes 638984 | tf_op jit(solution)/shard_map/ppermute | solution.py:409
  30.6 6.3 %collective-permute-start.11 = (bf16[26,32,128]{2,1,0:T(8,128)(2,1)S(1)}, bf16[26,32,128]{2,1,0:T(8,128)(2,1)S(1)}, u32[]{:S(2)}, u32[]{:S(2)}) collective-permute-start(bf16[26,32,128]{2,1,0:T(8,128)(2,1)S(1)} %collective-permute-done.7.far), channel_id=1, source_target_pairs={{0,16},{16,0},{32,48},{48,32},{64,80},{80,64},{96,112},{112,96},{1... | collective-permute-start | bytes 638984 | tf_op jit(solution)/shard_map/ppermute | solution.py:409
  31.1 5.8 %collective-permute-start.8 = (bf16[18,32,128]{2,1,0:T(8,128)(2,1)S(1)}, bf16[18,32,128]{2,1,0:T(8,128)(2,1)S(1)}, u32[]{:S(2)}, u32[]{:S(2)}) collective-permute-start(bf16[18,32,128]{2,1,0:T(8,128)(2,1)S(1)} %get-tuple-element.39.own), channel_id=1, source_target_pairs={{0,128},{16,144},{32,160},{48,176},{64,192},{80,208},{96,224},{112... | collective-permute-start | bytes 442376 | tf_op jit(solution)/shard_map/ppermute | solution.py:409

commit v7 on v6

--- a/solution.py
+++ b/solution.py
@@ -343,6 +343,7 @@
     first_half = lane < 64
     cell = lane & 63
     spread = spread_ref[...]
+    groups = []
     for pb in range(2):
         blocks = {0: [], 1: []}
         for n in range(8):
@@ -358,8 +359,11 @@
                 even = t1 + jnp.where(cell == 0, 0.0, pltpu.roll(t3, 1, 1))
                 odd = t2 + jnp.where(cell == 63, 0.0, pltpu.roll(t0, 127, 1))
                 blocks[pa].append(jnp.concatenate([even, odd], axis=1))
+        groups += [jnp.concatenate(blocks[pa], axis=0).astype(BF) for pa in range(2)]
+    ordered = dot(jnp.concatenate(groups, axis=0), spread)
+    for pb in range(2):
         for pa in range(2):
-            rows = dot(jnp.concatenate(blocks[pa], axis=0).astype(BF), spread)
+            rows = ordered[(pb * 2 + pa) * 64 : (pb * 2 + pa + 1) * 64]
             for n in range(8):
                 for m in range(2):
                     fine[pl.ds((2 * m + pa) * 16 + 2 * n + pb, 8, stride=64), :] = rows[

time: 38.8 us -> 38.7 us (level)
  no operation moved by 1% of the time
where the time goes in v7:
time: 38.7 us; the launch traced here: 38.6 us
  waiting for transfers between devices  23.2 us (60%)
  starting transfers between devices  9.33 us (24%)
  Pallas kernels  5.33 us (14%)
  between operations  0.7 us (2%)
    ppermute x11, waiting for transfers between devices, local(): send = lambda a, pairs: lax.ppermute(a, 'chan', pairs)  16.8 us
    ppermute x1, waiting for transfers between devices, local(): halo = lax.ppermute(edges, ('chan', 'space'), cross)  6.4 us
    ppermute x11, starting transfers between devices, local(): send = lambda a, pairs: lax.ppermute(a, 'chan', pairs)  5.51 us
    ppermute x1, starting transfers between devices, local(): halo = lax.ppermute(edges, ('chan', 'space'), cross)  3.82 us
    pallas_call x1, Pallas kernels, last(): call(last_body, (s((8, 4, 16, 128)), s((16, 2, 8, 64))), [pltpu.VMEM((10,...  1.73 us
    pallas_call x1, Pallas kernels, ready(): call(ready_body, (s((8, 32, 128)), s((2, 128, 512)), s((2, 4, 144, 512)),...  1.63 us
    pallas_call x1, Pallas kernels, mine(): call(mine_body, (s((48, 128), F32), s((16, 2, 8, 64)), s((8, 4, 16, 128))...  1.05 us
  transfers between devices with their start and end apart: 12, of which 5 were waited for; matrix products, arithmetic and copies ran while one was open for 0% of the time, Pallas kernels for 8%

profile of v7, /device:TPU:24, one launch (start us, length us, event | category | flops | bytes accessed | tf_op | source)
XLA Modules:
  0.0 38.6 jit_solution(12349159784066338061)
XLA Ops:
  0.6 0.1 collective-permute-start.2
  0.7 0.5 %collective-permute-start = (bf16[8,4,16,128]{3,2,1,0:T(8,128)(2,1)}, bf16[8,4,16,128]{3,2,1,0:T(8,128)(2,1)S(1)}, u32[]{:S(2)}, u32[]{:S(2)}) collective-permute-start(bf16[8,4,16,128]{3,2,1,0:T(8,128)(2,1)} %cot_hbm.1), channel_id=1, source_target_pairs={{0,16},{16,0},{32,48},{48,32},{64,80},{80,64},{96,112},{112,96},{1... | collective-permute-start | bytes 393224 | tf_op jit(solution)/shard_map/ppermute | solution.py:413
  1.2 0.1 collective-permute-start.1
  1.3 1.0 %shard_map.50 = (f32[48,128]{1,0:T(8,128)S(1)}, bf16[16,2,8,64]{3,2,1,0:T(8,128)(2,1)S(1)}, bf16[8,4,16,128]{3,2,1,0:T(8,128)(2,1)S(1)}, bf16[256,512]{1,0:T(8,128)(2,1)S(1)}, bf16[256,256]{1,0:T(8,128)(2,1)S(1)}) custom-call(bf16[16,2,8,64]{3,2,1,0:T(8,128)(2,1)} %feat_hbm.1, bf16[8,4,16,128]{3,2,1,0:T(8,128)(2,1)} %cot_hbm.1), custom_call_target="tpu_custom_call" | custom-call | bytes 1000000 | tf_op jit(solution)/shard_map/pallas_call | solution.py:100
  2.4 0.4 collective-permute-done.1.feat_o.feat
  2.7 0.0 collective-permute-done.cot_o.cot
  2.7 0.1 shard_map.52
  2.8 3.8 %collective-permute-start.3 = (bf16[96,128]{1,0:T(8,128)(2,1)S(1)}, bf16[96,128]{1,0:T(8,128)(2,1)S(1)}, u32[]{:S(2)}, u32[]{:S(2)}) collective-permute-start(bf16[96,128]{1,0:T(8,128)(2,1)S(1)} %shard_map.52), channel_id=1, source_target_pairs={{0,1},{1,2},{2,3},{3,4},{4,5},{5,6},{6,7},{7,8},{8,9},{9,10},{10,1... | collective-permute-start | bytes 73736 | tf_op jit(solution)/shard_map/ppermute | solution.py:422
  6.7 6.4 %collective-permute-done.3.halo = bf16[96,128]{1,0:T(8,128)(2,1)S(1)} collective-permute-done((bf16[96,128]{1,0:T(8,128)(2,1)S(1)}, bf16[96,128]{1,0:T(8,128)(2,1)S(1)}, u32[]{:S(2)}, u32[]{:S(2)}) %collective-permute-start.3) | collective-permute-done | bytes 24608 | tf_op jit(solution)/shard_map/ppermute | solution.py:422
  13.1 0.0 collective-permute-start.4
  13.1 0.0 collective-permute-done.2.w_o
  13.1 1.6 %shard_map.51 = (bf16[8,32,128]{2,1,0:T(8,128)(2,1)S(1)}, bf16[2,128,512]{2,1,0:T(8,128)(2,1)S(1)}, bf16[2,4,144,512]{3,2,1,0:T(8,128)(2,1)S(1)}, f32[2,4,16,128...) custom-call(bf16[16,2,8,64]{3,2,1,0:T(8,128)(2,1)S(1)} %get-tuple-element.23.feat, ...), custom_call_target="tpu_custom_call" | custom-call | flops 200000000 | bytes 2500000 | tf_op jit(solution)/shard_map/pallas_call | solution.py:183
  14.7 0.3 shard_map.53
  15.0 0.0 collective-permute-done.4.halo_o
  15.0 0.5 %shard_map.54 = (bf16[26,32,128]{2,1,0:T(8,128)(2,1)S(1)}, bf16[26,32,128]{2,1,0:T(8,128)(2,1)S(1)}, bf16[26,32,128]{2,1,0:T(8,128)(2,1)S(1)}, bf16[18,32,128]{2,1,0:T(8,128)(2,1)S(1)}, f32[8,16,128]{2,1,0:T(8,128)S(1)}) custom-call(bf16[2,128,512]{2,1,0:T(8,128)(2,1)S(1)} %get-tuple-element.31.chosen, bf16[2,4,144,512]{3,2,1,0:T(8,128)(2,1)S(1)} %get-tuple-element.32.cols, ...), custom_call_target="tpu_custom_call" | custom-call | flops 400000000 | bytes 2500000 | tf_op jit(solution)/shard_map/pallas_call | solution.py:291
  15.6 1.6 %collective-permute-start.5 = (bf16[26,32,128]{2,1,0:T(8,128)(2,1)S(1)}, bf16[26,32,128]{2,1,0:T(8,128)(2,1)S(1)}, u32[]{:S(2)}, u32[]{:S(2)}) collective-permute-start(bf16[26,32,128]{2,1,0:T(8,128)(2,1)S(1)} %get-tuple-element.41), channel_id=1, source_target_pairs={{0,32},{16,112},{32,64},{48,16},{64,96},{80,48},{96,0},{112,80},{1... | collective-permute-start | bytes 638984 | tf_op jit(solution)/shard_map/ppermute | solution.py:413
  17.1 0.8 %collective-permute-start.6 = (bf16[26,32,128]{2,1,0:T(8,128)(2,1)S(1)}, bf16[26,32,128]{2,1,0:T(8,128)(2,1)S(1)}, u32[]{:S(2)}, u32[]{:S(2)}) collective-permute-start(bf16[26,32,128]{2,1,0:T(8,128)(2,1)S(1)} %get-tuple-element.42), channel_id=1, source_target_pairs={{0,160},{16,240},{32,192},{48,144},{64,224},{80,176},{96,128},{112... | collective-permute-start | bytes 638984 | tf_op jit(solution)/shard_map/ppermute | solution.py:413
  17.9 2.0 %collective-permute-start.7 = (bf16[26,32,128]{2,1,0:T(8,128)(2,1)S(1)}, bf16[26,32,128]{2,1,0:T(8,128)(2,1)S(1)}, u32[]{:S(2)}, u32[]{:S(2)}) collective-permute-start(bf16[26,32,128]{2,1,0:T(8,128)(2,1)S(1)} %get-tuple-element.43), channel_id=1, source_target_pairs={{0,64},{16,208},{32,96},{48,240},{64,0},{80,144},{96,32},{112,176}... | collective-permute-start | bytes 638984 | tf_op jit(solution)/shard_map/ppermute | solution.py:413
  19.9 2.8 %collective-permute-done.5.side = bf16[26,32,128]{2,1,0:T(8,128)(2,1)S(1)} collective-permute-done((bf16[26,32,128]{2,1,0:T(8,128)(2,1)S(1)}, bf16[26,32,128]{2,1,0:T(8,128)(2,1)S(1)}, u32[]{:S(2)}, u32[]{:S(2)}) %collective-permute-start.5) | collective-permute-done | bytes 213024 | tf_op jit(solution)/shard_map/ppermute | solution.py:413
  22.7 7.9 %collective-permute-done.6.side_y = bf16[26,32,128]{2,1,0:T(8,128)(2,1)S(1)} collective-permute-done((bf16[26,32,128]{2,1,0:T(8,128)(2,1)S(1)}, bf16[26,32,128]{2,1,0:T(8,128)(2,1)S(1)}, u32[]{:S(2)}, u32[]{:S(2)}) %collective-permute-start.6) | collective-permute-done | bytes 213024 | tf_op jit(solution)/shard_map/ppermute | solution.py:413
  30.6 0.5 %collective-permute-start.11 = (bf16[26,32,128]{2,1,0:T(8,128)(2,1)S(1)}, bf16[26,32,128]{2,1,0:T(8,128)(2,1)S(1)}, u32[]{:S(2)}, u32[]{:S(2)}) collective-permute-start(bf16[26,32,128]{2,1,0:T(8,128)(2,1)S(1)} %collective-permute-done.7.far), channel_id=1, source_target_pairs={{0,16},{16,0},{32,48},{48,32},{64,80},{80,64},{96,112},{112,96},{1... | collective-permute-start | bytes 638984 | tf_op jit(solution)/shard_map/ppermute | solution.py:413
  31.1 5.8 %collective-permute-done.8.away = bf16[18,32,128]{2,1,0:T(8,128)(2,1)S(1)} collective-permute-done((bf16[18,32,128]{2,1,0:T(8,128)(2,1)S(1)}, bf16[18,32,128]{2,1,0:T(8,128)(2,1)S(1)}, u32[]{:S(2)}, u32[]{:S(2)}) %collective-permute-start.8) | collective-permute-done | bytes 147488 | tf_op jit(solution)/shard_map/ppermute | solution.py:413
  36.8 0.0 collective-permute-done.9.side_o
  36.8 1.7 %shard_map.55 = (bf16[8,4,16,128]{3,2,1,0:T(8,128)(2,1)}, bf16[16,2,8,64]{3,2,1,0:T(8,128)(2,1)}) custom-call(bf16[512,256]{1,0:T(8,128)(2,1)S(1)} %bitcast.2, bf16[256,256]{1,0:T(8,128)(2,1)S(1)} %get-tuple-element.30.spread, bf16[18,32,128]{2,1,0:T(8,128)(2,1)S(1)} %get-tuple-element.39.own, f32[8,16,128]{2,1,0:T(8,128)S(1)} %get-tuple-element.40.kept, ...), custom_call_target="tpu_custom_call" | custom-call | flops 400000000 | bytes 2500000 | tf_op jit(solution)/shard_map/pallas_call | solution.py:383
  (6 shorter events, 0.0 us)
Async XLA Ops:
  0.6 12.4 %collective-permute-start.2 = (bf16[4,4,4,8,256]{4,3,2,1,0:T(8,128)(2,1)}, bf16[4,4,4,8,256]{4,3,2,1,0:T(8,128)(2,1)S(1)}, u32[]{:S(2)}, u32[]{:S(2)}) collective-permute-start(bf16[4,4,4,8,256]{4,3,2,1,0:T(8,128)(2,1)} %bitcast.3), channel_id=1, source_target_pairs={{0,16},{16,0},{32,48},{48,32},{64,80},{80,64},{96,112},{112,96},{1... | collective-permute-start | bytes 786440 | tf_op jit(solution)/shard_map/ppermute | solution.py:413
  0.7 2.0 %collective-permute-start = (bf16[8,4,16,128]{3,2,1,0:T(8,128)(2,1)}, bf16[8,4,16,128]{3,2,1,0:T(8,128)(2,1)S(1)}, u32[]{:S(2)}, u32[]{:S(2)}) collective-permute-start(bf16[8,4,16,128]{3,2,1,0:T(8,128)(2,1)} %cot_hbm.1), channel_id=1, source_target_pairs={{0,16},{16,0},{32,48},{48,32},{64,80},{80,64},{96,112},{112,96},{1... | collective-permute-start | bytes 393224 | tf_op jit(solution)/shard_map/ppermute | solution.py:413
  1.2 1.5 %collective-permute-start.1 = (bf16[16,2,8,64]{3,2,1,0:T(8,128)(2,1)}, bf16[16,2,8,64]{3,2,1,0:T(8,128)(2,1)S(1)}, u32[]{:S(2)}, u32[]{:S(2)}) collective-permute-start(bf16[16,2,8,64]{3,2,1,0:T(8,128)(2,1)} %feat_hbm.1), channel_id=1, source_target_pairs={{0,16},{16,0},{32,48},{48,32},{64,80},{80,64},{96,112},{112,96},{1... | collective-permute-start | bytes 98312 | tf_op jit(solution)/shard_map/ppermute | solution.py:413
  2.8 10.2 %collective-permute-start.3 = (bf16[96,128]{1,0:T(8,128)(2,1)S(1)}, bf16[96,128]{1,0:T(8,128)(2,1)S(1)}, u32[]{:S(2)}, u32[]{:S(2)}) collective-permute-start(bf16[96,128]{1,0:T(8,128)(2,1)S(1)} %shard_map.52), channel_id=1, source_target_pairs={{0,1},{1,2},{2,3},{3,4},{4,5},{5,6},{6,7},{7,8},{8,9},{9,10},{10,1... | collective-permute-start | bytes 73736 | tf_op jit(solution)/shard_map/ppermute | solution.py:422
  13.1 2.0 %collective-permute-start.4 = (bf16[96,128]{1,0:T(8,128)(2,1)S(1)}, bf16[96,128]{1,0:T(8,128)(2,1)S(1)}, u32[]{:S(2)}, u32[]{:S(2)}) collective-permute-start(bf16[96,128]{1,0:T(8,128)(2,1)S(1)} %collective-permute-done.3.halo), channel_id=1, source_target_pairs={{0,16},{16,0},{32,48},{48,32},{64,80},{80,64},{96,112},{112,96},{1... | collective-permute-start | bytes 73736 | tf_op jit(solution)/shard_map/ppermute | solution.py:413
  15.6 7.1 %collective-permute-start.5 = (bf16[26,32,128]{2,1,0:T(8,128)(2,1)S(1)}, bf16[26,32,128]{2,1,0:T(8,128)(2,1)S(1)}, u32[]{:S(2)}, u32[]{:S(2)}) collective-permute-start(bf16[26,32,128]{2,1,0:T(8,128)(2,1)S(1)} %get-tuple-element.41), channel_id=1, source_target_pairs={{0,32},{16,112},{32,64},{48,16},{64,96},{80,48},{96,0},{112,80},{1... | collective-permute-start | bytes 638984 | tf_op jit(solution)/shard_map/ppermute | solution.py:413
  17.1 13.4 %collective-permute-start.6 = (bf16[26,32,128]{2,1,0:T(8,128)(2,1)S(1)}, bf16[26,32,128]{2,1,0:T(8,128)(2,1)S(1)}, u32[]{:S(2)}, u32[]{:S(2)}) collective-permute-start(bf16[26,32,128]{2,1,0:T(8,128)(2,1)S(1)} %get-tuple-element.42), channel_id=1, source_target_pairs={{0,160},{16,240},{32,192},{48,144},{64,224},{80,176},{96,128},{112... | collective-permute-start | bytes 638984 | tf_op jit(solution)/shard_map/ppermute | solution.py:413
  17.9 12.7 %collective-permute-start.7 = (bf16[26,32,128]{2,1,0:T(8,128)(2,1)S(1)}, bf16[26,32,128]{2,1,0:T(8,128)(2,1)S(1)}, u32[]{:S(2)}, u32[]{:S(2)}) collective-permute-start(bf16[26,32,128]{2,1,0:T(8,128)(2,1)S(1)} %get-tuple-element.43), channel_id=1, source_target_pairs={{0,64},{16,208},{32,96},{48,240},{64,0},{80,144},{96,32},{112,176}... | collective-permute-start | bytes 638984 | tf_op jit(solution)/shard_map/ppermute | solution.py:413
  22.7 14.1 %collective-permute-start.9 = (bf16[26,32,128]{2,1,0:T(8,128)(2,1)S(1)}, bf16[26,32,128]{2,1,0:T(8,128)(2,1)S(1)}, u32[]{:S(2)}, u32[]{:S(2)}) collective-permute-start(bf16[26,32,128]{2,1,0:T(8,128)(2,1)S(1)} %collective-permute-done.5.side), channel_id=1, source_target_pairs={{0,16},{16,0},{32,48},{48,32},{64,80},{80,64},{96,112},{112,96},{1... | collective-permute-start | bytes 638984 | tf_op jit(solution)/shard_map/ppermute | solution.py:413
  30.6 6.3 %collective-permute-start.10 = (bf16[26,32,128]{2,1,0:T(8,128)(2,1)S(1)}, bf16[26,32,128]{2,1,0:T(8,128)(2,1)S(1)}, u32[]{:S(2)}, u32[]{:S(2)}) collective-permute-start(bf16[26,32,128]{2,1,0:T(8,128)(2,1)S(1)} %collective-permute-done.6.side_y), channel_id=1, source_target_pairs={{0,16},{16,0},{32,48},{48,32},{64,80},{80,64},{96,112},{112,96},{1... | collective-permute-start | bytes 638984 | tf_op jit(solution)/shard_map/ppermute | solution.py:413
  30.6 6.3 %collective-permute-start.11 = (bf16[26,32,128]{2,1,0:T(8,128)(2,1)S(1)}, bf16[26,32,128]{2,1,0:T(8,128)(2,1)S(1)}, u32[]{:S(2)}, u32[]{:S(2)}) collective-permute-start(bf16[26,32,128]{2,1,0:T(8,128)(2,1)S(1)} %collective-permute-done.7.far), channel_id=1, source_target_pairs={{0,16},{16,0},{32,48},{48,32},{64,80},{80,64},{96,112},{112,96},{1... | collective-permute-start | bytes 638984 | tf_op jit(solution)/shard_map/ppermute | solution.py:413
  31.1 5.8 %collective-permute-start.8 = (bf16[18,32,128]{2,1,0:T(8,128)(2,1)S(1)}, bf16[18,32,128]{2,1,0:T(8,128)(2,1)S(1)}, u32[]{:S(2)}, u32[]{:S(2)}) collective-permute-start(bf16[18,32,128]{2,1,0:T(8,128)(2,1)S(1)} %get-tuple-element.39.own), channel_id=1, source_target_pairs={{0,128},{16,144},{32,160},{48,176},{64,192},{80,208},{96,224},{112... | collective-permute-start | bytes 442376 | tf_op jit(solution)/shard_map/ppermute | solution.py:413
